TPU v7x, 32 devices: a whole 2x2x4 slice. The times are simulated.
32 devices in a mesh: section: 2 (over core), tensor: 4 (over y, x), dp: 4 (over z).
Axes of the slice: x: 2, y: 2, z: 4, core: 2. Of those that a mesh axis runs over, the one named last changes fastest.
Arguments:
- tokens: bfloat16 [512, 4096], P('dp', 'tensor'), may hold values from -6 to 6
- section_weights: bfloat16 [2, 4096, 14336], P('section', None, 'tensor'), may hold values from -0.09375 to 0.09375
- up_weight: bfloat16 [4096, 14336], P(None, 'tensor'), may hold values from -0.09375 to 0.09375
- cotangent: bfloat16 [512, 4096], P('dp'), may hold values from -0.1796875 to 0.1796875
Outputs:
- section_grads: bfloat16 [2, 4096, 14336], P('section', 'dp', 'tensor')
- up_grads: bfloat16 [4096, 14336], P(('section', 'dp'), 'tensor')
All inputs are finite; a program needn't handle non-finite values.
Results may differ from a plain program's by a relative error of at most 0.018.
Values may be sent and summed in bfloat16 or wider, within the bound.
No kernel may reach another device: no remote copies, remote signals or barrier semaphores. Data moves between devices by JAX's collectives and lax.ppermute only.
A program may use at most 192 MiB of HBM per device.

v0:
```python
import jax
import jax.numpy as jnp
from jax import lax
from jax.sharding import PartitionSpec as P


def passed_along(value, axis, steps):
    count = lax.axis_size(axis)
    first, last = (max(0, -steps), min(count, count - steps))
    return lax.ppermute(value, axis, [(source, source + steps) for source in range(first, last)])


def matmul(left, right):
    return jnp.dot(left, right, preferred_element_type=jnp.float32)


def along_rows(left, right):
    return lax.dot_general(
        left, right, (((0,), (0,)), ((), ())), preferred_element_type=jnp.float32
    )


def local(tokens, section_weights, up_weight, cotangent):
    section = lax.axis_index("section")
    is_first = section == 0
    slot = section_weights[0]
    tokens_all = lax.all_gather(tokens, "tensor", axis=1, tiled=True)
    count = tokens_all.shape[0]
    width = tokens_all.shape[1]
    half_width = width // 2
    units = slot.shape[1]

    def first_product():
        return matmul(tokens_all, slot)

    def second_product():
        return matmul(tokens_all, up_weight)

    product = lax.cond(is_first, first_product, second_product)
    gate_pre = passed_along(product.astype(jnp.bfloat16), "section", 1).astype(product.dtype)

    def second_backward():
        sigmoid_gate = jax.nn.sigmoid(gate_pre)
        hidden = (gate_pre * sigmoid_gate * product).astype(jnp.bfloat16)
        grad_hidden = matmul(cotangent, slot)
        grad_gate = (
            grad_hidden * product * sigmoid_gate * (1.0 + gate_pre * (1.0 - sigmoid_gate))
        ).astype(jnp.bfloat16)
        grad_up = (grad_hidden * gate_pre * sigmoid_gate).astype(jnp.bfloat16)
        return (grad_gate, grad_up, hidden)

    def first_backward():
        blank = jnp.zeros((count, units), jnp.bfloat16)
        return (blank, blank, blank)

    grad_gate, grad_up, hidden = lax.cond(is_first, first_backward, second_backward)
    back_gate, back_up = passed_along((grad_gate, grad_up), "section", -1)
    up_tokens = lax.dynamic_slice_in_dim(tokens_all, section * half_width, half_width, 1)
    grad_up_used = jnp.where(is_first, back_up, grad_up)
    up_part = along_rows(up_tokens, grad_up_used)
    left_rows = jnp.where(is_first, tokens_all, cotangent)
    right_rows = jnp.where(is_first, back_gate, hidden)
    slot_part = along_rows(left_rows, right_rows)
    slot_sum, up_sum = (
        lax.psum_scatter(
            slot_part.astype(jnp.bfloat16), "dp", scatter_dimension=0, tiled=True
        ).astype(jnp.float32),
        lax.psum_scatter(
            up_part.astype(jnp.bfloat16), "dp", scatter_dimension=0, tiled=True
        ).astype(jnp.float32),
    )
    return (slot_sum.astype(jnp.bfloat16)[None], up_sum.astype(jnp.bfloat16))


def solution(mesh):
    placed = (P("dp", "tensor"), P("section", None, "tensor"), P(None, "tensor"), P("dp", None))
    return jax.shard_map(
        local,
        mesh=mesh,
        in_specs=placed,
        out_specs=(P("section", "dp", "tensor"), P(("section", "dp"), "tensor")),
        check_vma=False,
    )
```

profile of v0, /device:TPU:13, one launch (start us, length us, event | category | flops | bytes accessed | tf_op | source)
XLA Modules:
  0.0 819.9 jit_solution(477201175925530872)
XLA Ops:
  7.2 0.0 all-gather.2.cloned.1.call-start
  7.2 0.7 all-gather.2.cloned.1.call-update
  7.9 0.0 reduce-scatter.5.cloned.1.call-start
  8.0 29.3 %all-gather.2.cloned.1.call-done = bf16[128,4096]{1,0:T(8,128)(2,1)} async-done(((bf16[128,1024]{1,0:T(8,128)(2,1)}), bf16[128,4096]{1,0:T(8,128)(2,1)}) %all-gather.2.cloned.1.call-update) | async-done | bytes 1048592 | tf_op jit(solution)/shard_map/all_gather | solution.py:27
  37.3 11.8 %conditional.2 = (f32[128,3584]{1,0:T(8,128)S(1)}) conditional(s32[]{:T(128)} %convert_element_type.29, (bf16[128,4096]{1,0:T(8,128)(2,1)}, bf16[4096,3584]{1,0:T(8,128)(2,1)}) %tuple.22, (bf16[128,4096]{1,0:T(8,128)(2,1)}, bf16[4096,3584]{1,0:T(8,128)(2,1)}) %tuple.39), branch_computations={%region_0.0_spmd, %region_1.0_spmd} | conditional | flops 3758096384 | bytes 32243720 | solution.py:39
  37.3 11.8 %fusion.8 = f32[128,3584]{1,0:T(8,128)S(1)} fusion(bf16[128,4096]{1,0:T(8,128)(2,1)} %get-tuple-element.8, bf16[4096,3584]{1,0:T(8,128)(2,1)} %get-tuple-element.36), kind=kOutput, calls=%fused_computation.14 | convolution fusion | flops 3758096384 | bytes 32243712 | tf_op jit(solution)/shard_map/cond/branch_0_fun/dot_general | solution.py:14
  49.1 0.1 convert_element_type.30
  49.2 1.4 collective-permute-start
  50.6 3.1 collective-permute-done
  53.7 0.2 convert_element_type.31
  53.9 15.4 %conditional.3 = (bf16[128,3584]{1,0:T(8,128)(2,1)S(1)}, bf16[128,3584]{1,0:T(8,128)(2,1)}, bf16[128,3584]{1,0:T(8,128)(2,1)}) conditional(s32[]{:T(128)} %convert_element_type.29, (bf16[128,4096]{1,0:T(8,128)(2,1)S(1)}, bf16[4096,3584]{1,0:T(8,128)(2,1)}, f32[128,3584]{1,0:T(8,128)S(1)}, f32[128,3584]{1,0:T(8,128)S(1)}) %tuple.41, () %tuple.25), branch_computations={%region_2.0_spmd, %region_3.0_spmd} | conditional | flops 3765436416 | bytes 36831256 | solution.py:56
  53.9 15.4 %multiply_convert_fusion = (bf16[128,3584]{1,0:T(8,128)(2,1)}, bf16[128,3584]{1,0:T(8,128)(2,1)S(1)}, bf16[128,3584]{1,0:T(8,128)(2,1)}) fusion(f32[128,3584]{1,0:T(8,128)S(1)} %get-tuple-element.25, f32[128,3584]{1,0:T(8,128)S(1)} %get-tuple-element.26, bf16[128,4096]{1,0:T(8,128)(2,1)S(1)} %get-tuple-element.23, bf16[4096,3584]{1,0:T(8,128)(2,1)} %get-tuple-element.24), kind=kOutput, calls=%fused_computation | convolution fusion | flops 3765436416 | bytes 36831232 | tf_op jit(solution)/shard_map/cond/branch_0_fun/dot_general | solution.py:14
  69.3 1.0 copy-done.3
  70.2 1.3 collective-permute-start.2
  71.6 2.2 collective-permute-done.2
  73.8 8.5 %convolution_convert_fusion.1 = bf16[2048,3584]{1,0:T(8,128)(2,1)} fusion(bf16[128,3584]{1,0:T(8,128)(2,1)S(1)} %collective-permute-done.2, bf16[128,3584]{1,0:T(8,128)(2,1)} %get-tuple-element.34, pred[]{:T(512)S(6)} %eq.3, bf16[128,4096]{1,0:T(8,128)(2,1)S(1)} %copy-done, s32[]{:T(128)S(6)} %select_n.27), kind=kOutput, calls=%fused_computation.5 | convolution fusion | flops 1886846976 | bytes 17039364 | tf_op jit(solution)/shard_map/dot_general | solution.py:18
  82.3 0.0 reduce-scatter.5.cloned.1.call-update
  82.4 0.0 reduce-scatter.3.cloned.1.call-start
  82.4 1.1 copy-done.4
  83.5 1.3 collective-permute-start.1
  84.9 2.0 collective-permute-done.1
  86.9 13.6 %convolution_convert_fusion = bf16[4096,3584]{1,0:T(8,128)(2,1)} fusion(bf16[128,4096]{1,0:T(8,128)(2,1)S(1)} %copy-done, bf16[128,4096]{1,0:T(8,128)(2,1)S(1)} %copy-done.2, pred[]{:T(512)S(6)} %eq.3, bf16[128,3584]{1,0:T(8,128)(2,1)S(1)} %collective-permute-done.1, bf16[128,3584]{1,0:T(8,128)(2,1)} %get-tuple-element.33), kind=kOutput, calls=%fused_computation.4 | convolution fusion | flops 3773759488 | bytes 33292288 | tf_op jit(solution)/shard_map/dot_general | solution.py:18
  100.5 227.2 %reduce-scatter.5.cloned.1.call-done = bf16[512,3584]{1,0:T(8,128)(2,1)} async-done(((bf16[2048,3584]{1,0:T(8,128)(2,1)}), bf16[512,3584]{1,0:T(8,128)(2,1)}) %reduce-scatter.5.cloned.1.call-update) | async-done | bytes 3670032 | tf_op jit(solution)/shard_map/reduce_scatter | solution.py:68
  327.7 485.7 %reduce-scatter.3.cloned.1.call-done = bf16[1024,3584]{1,0:T(8,128)(2,1)} async-done(((bf16[4096,3584]{1,0:T(8,128)(2,1)}), bf16[1024,3584]{1,0:T(8,128)(2,1)}) %reduce-scatter.3.cloned.1.call-update) | async-done | bytes 7340048 | tf_op jit(solution)/shard_map/reduce_scatter | solution.py:65
  (9 shorter events, 0.0 us)
Async XLA Ops:
  7.2 30.1 %all-gather.2.cloned.1.call-start = ((), (), s32[]{:S(2)}) async-start(), calls=%async_computation.2 | async-start | bytes 1310720 | tf_op jit(solution)/shard_map/all_gather | solution.py:27
  7.9 319.8 %reduce-scatter.5.cloned.1.call-start = ((), (), s32[]{:S(2)}) async-start(), calls=%async_computation.4 | async-start | bytes 18350080 | tf_op jit(solution)/shard_map/reduce_scatter | solution.py:68
  49.2 4.7 copy-start.1
  49.2 4.5 collective-permute-start
  53.9 20.0 %copy-start = (bf16[128,4096]{1,0:T(8,128)(2,1)S(1)}, bf16[128,4096]{1,0:T(8,128)(2,1)}, u32[]{:S(2)}) copy-start(bf16[128,4096]{1,0:T(8,128)(2,1)} %all-gather.2.cloned.1.call-done) | copy-start | bytes 3145732
  69.3 1.0 copy-start.3
  70.2 3.6 collective-permute-start.2
  82.3 1.2 copy-start.4
  82.3 4.5 copy-start.2
  82.4 731.0 %reduce-scatter.3.cloned.1.call-start = ((), (), s32[]{:S(2)}) async-start(), calls=%async_computation.3 | async-start | bytes 36700160 | tf_op jit(solution)/shard_map/reduce_scatter | solution.py:65
  83.5 3.4 collective-permute-start.1
Sparse Core Ops, SparseCore 0:
  9.8 27.4 all-gather.1
  82.5 245.1 reduce-scatter.4
  330.6 482.7 reduce-scatter.2
where the time goes:
time: 822 us; the launch traced here: 820 us
  waiting for transfers between devices  750 us (91%)
  matrix products  49.2 us (6%)
  between operations  13.8 us (2%)
    reduce_scatter x1, waiting for transfers between devices, local(): lax.psum_scatter(slot_part.astype(jnp.bfloat16), 'dp', scatter_dimension=...  486 us
    reduce_scatter x1, waiting for transfers between devices, local(): lax.psum_scatter(up_part.astype(jnp.bfloat16), 'dp', scatter_dimension=0,...  227 us
    all_gather x1, waiting for transfers between devices, local(): tokens_all = lax.all_gather(tokens, 'tensor', axis=1, tiled=True)  29.3 us
    dot_general x2, matrix products, matmul(): return jnp.dot(left, right, preferred_element_type=jnp.float32)  27.1 us
    dot_general x2, matrix products, along_rows(): lax.dot_general(left, right, (((0,), (0,)), ((), ())), preferred_element_...  22.1 us
  transfers between devices with their start and end apart: 6, of which 6 were waited for; matrix products, arithmetic and copies ran while one was open for 2% of the time, Pallas kernels for 0%

commit v1 on v0

v1 whole, which is shorter than its diff:
```python
import jax
import jax.numpy as jnp
from jax import lax
from jax.sharding import PartitionSpec as P

AXES = ("section", "tensor", "dp")


def sent(value, mesh, target):
    shape = [mesh.shape[axis] for axis in AXES]
    pairs = []
    for s in range(shape[0]):
        for t in range(shape[1]):
            for d in range(shape[2]):
                source = (s * shape[1] + t) * shape[2] + d
                to = target(s, t, d)
                pairs.append((source, (to[0] * shape[1] + to[1]) * shape[2] + to[2]))
    return lax.ppermute(value, AXES, pairs)


def matmul(left, right):
    return jnp.dot(left, right, preferred_element_type=jnp.float32)


def along_rows(left, right):
    return lax.dot_general(
        left, right, (((0,), (0,)), ((), ())), preferred_element_type=jnp.float32
    )


def columns(value, start, width):
    return lax.dynamic_slice_in_dim(value, start, width, 1)


def placed_at(whole, piece, row, column):
    return lax.dynamic_update_slice(whole, piece, (row, column))


def gathered_everywhere(tokens, cotangent):
    tokens_all = lax.all_gather(tokens, "tensor", axis=1, tiled=True)
    tokens_all = lax.all_gather(tokens_all, "dp", axis=0, tiled=True)
    return tokens_all, lax.all_gather(cotangent, "dp", axis=0, tiled=True)


def gathered_by_chip(mesh, tokens, cotangent):
    groups = mesh.shape["dp"]
    section = lax.axis_index("section")
    tensor = lax.axis_index("tensor")
    count, block = tokens.shape
    half = block // 2
    width = cotangent.shape[1]
    quarter = width // 4

    def ring(step):
        return lambda s, t, d: (s, t, (d + step) % groups)

    def other_section(s, t, d):
        return (1 - s, t, d)

    def near(s, t, d):
        return (s, t ^ (1 + s), d)

    def far(s, t, d):
        return (s, t ^ (2 - s), d)

    steps = range(1, groups)
    parity = (tensor ^ (tensor >> 1)) & 1
    own_half = columns(tokens, section * half, half)
    mine = jnp.concatenate([own_half] + [sent(own_half, mesh, ring(k)) for k in steps], 0)
    own_quarter = columns(cotangent, (2 * parity + section) * quarter, quarter)
    first_mine = jnp.concatenate([sent(own_quarter, mesh, ring(k)) for k in steps], 0)
    theirs = sent(mine, mesh, other_section)
    both = jnp.concatenate([mine, theirs], 1)
    beside = sent(both, mesh, near)
    beside_too = sent(beside, mesh, other_section)
    across = sent(beside[:, :half], mesh, far)
    across_too = sent(across, mesh, other_section)
    first_theirs = sent(first_mine, mesh, other_section)
    second_mine = sent(first_mine, mesh, near)
    second_theirs = sent(second_mine, mesh, other_section)

    tokens_all = jnp.zeros((count * groups, width), tokens.dtype)
    near_block = tensor ^ (1 + section)
    far_block = tensor ^ (2 - section)
    for piece, at in (
        (mine, 2 * tensor + section),
        (theirs, 2 * tensor + 1 - section),
        (beside[:, :half], 2 * near_block + section),
        (beside[:, half:], 2 * near_block + 1 - section),
        (beside_too[:, :half], 2 * far_block + 1 - section),
        (beside_too[:, half:], 2 * far_block + section),
        (across, 2 * (tensor ^ 3) + section),
        (across_too, 2 * (tensor ^ 3) + 1 - section),
    ):
        tokens_all = placed_at(tokens_all, piece, 0, at * half)
    cotangent_all = jnp.zeros((count * groups, width), cotangent.dtype)
    cotangent_all = placed_at(cotangent_all, cotangent, 0, 0)
    for piece, at in (
        (first_mine, 2 * parity + section),
        (first_theirs, 2 * parity + 1 - section),
        (second_mine, 2 * (1 - parity) + section),
        (second_theirs, 2 * (1 - parity) + 1 - section),
    ):
        cotangent_all = placed_at(cotangent_all, piece, count, at * quarter)
    return tokens_all, cotangent_all


def local(mesh, tokens, section_weights, up_weight, cotangent):
    section = lax.axis_index("section")
    group = lax.axis_index("dp")
    groups = mesh.shape["dp"]
    is_first = section == 0
    slot = section_weights[0]
    units = slot.shape[1]
    width = cotangent.shape[1]

    def swapped(value):
        return sent(value, mesh, lambda s, t, d: (1 - s, t, d))

    if mesh.shape["tensor"] == 4:
        tokens_all, cotangent_all = gathered_by_chip(mesh, tokens, cotangent)
    else:
        tokens_all, cotangent_all = gathered_everywhere(tokens, cotangent)

    used = jnp.where(is_first, tokens_all, cotangent_all)
    own = matmul(used, slot).astype(jnp.bfloat16)
    other = swapped(own)
    half = units // 2
    up_own = matmul(tokens_all, columns(up_weight, section * half, half)).astype(jnp.bfloat16)
    up_other = swapped(up_own)
    up_pre = jnp.where(
        is_first,
        jnp.concatenate([up_own, up_other], 1),
        jnp.concatenate([up_other, up_own], 1),
    ).astype(jnp.float32)
    gate_pre = jnp.where(is_first, own, other).astype(jnp.float32)
    grad_hidden = jnp.where(is_first, other, own).astype(jnp.float32)
    sigmoid_gate = jax.nn.sigmoid(gate_pre)
    silu = gate_pre * sigmoid_gate
    grad_up = (grad_hidden * silu).astype(jnp.bfloat16)
    grad_gate = grad_hidden * up_pre * sigmoid_gate * (1.0 + gate_pre * (1.0 - sigmoid_gate))
    right = jnp.where(is_first, grad_gate, silu * up_pre).astype(jnp.bfloat16)
    slot_rows = width // groups
    up_rows = slot_rows // 2
    slot_sum = along_rows(columns(used, group * slot_rows, slot_rows), right)
    up_sum = along_rows(columns(tokens_all, (section * groups + group) * up_rows, up_rows), grad_up)
    return (slot_sum.astype(jnp.bfloat16)[None], up_sum.astype(jnp.bfloat16))


def solution(mesh):
    placed = (P("dp", "tensor"), P("section", None, "tensor"), P(None, "tensor"), P("dp", None))
    return jax.shard_map(
        lambda *args: local(mesh, *args),
        mesh=mesh,
        in_specs=placed,
        out_specs=(P("section", "dp", "tensor"), P(("section", "dp"), "tensor")),
        check_vma=False,
    )
```

time: 822 us -> 137 us (0.17)
  waiting for transfers between devices: 750 us -> 36.1 us
  local copies, waits for them, and re-layouts: 2.08 us -> 19 us
  starting transfers between devices: 4.21 us -> 18.5 us
  between operations: 13.8 us -> 0.73 us
  matrix products: 49.2 us -> 60.3 us
    reduce_scatter x2 -> x0, waiting for transfers between devices: 713 us -> none  [the longest x1 486 us: local(): lax.psum_scatter(slot_part.astype(jnp.bfloat16), 'dp', scatter_dimension=...]
    all_gather x1 -> x0, waiting for transfers between devices: 29.3 us -> none  [local(): tokens_all = lax.all_gather(tokens, 'tensor', axis=1, tiled=True)]
    ppermute x3 -> x16, waiting for transfers between devices: 7.32 us -> 36.1 us  [sent(): return lax.ppermute(value, AXES, pairs)]
    ppermute x3 -> x16, starting transfers between devices: 4.09 us -> 18.5 us  [sent(): return lax.ppermute(value, AXES, pairs)]
    dynamic_update_slice x0 -> x11, local copies, waits for them, and re-layouts: none -> 13.5 us  [placed_at(): return lax.dynamic_update_slice(whole, piece, (row, column))]
    dot_general x2, matrix products: 27.1 us -> 36.8 us  [matmul(): return jnp.dot(left, right, preferred_element_type=jnp.float32)]
  transfers between devices with their start and end apart: 6 -> 16, of which waited for: 6 -> 7; matrix products, arithmetic and copies ran while one was open for 2% -> 28% of each run, Pallas kernels for 0% -> 0%
where the time goes in v1:
time: 137 us
  matrix products  60.3 us (44%)
  waiting for transfers between devices  36.1 us (26%)
  local copies, waits for them, and re-layouts  19 us (14%)
  starting transfers between devices  18.5 us (14%)
  other arithmetic  2.42 us (2%)
    dot_general x2, matrix products, matmul(): return jnp.dot(left, right, preferred_element_type=jnp.float32)  36.8 us
    ppermute x16, waiting for transfers between devices, sent(): return lax.ppermute(value, AXES, pairs)  36.1 us
    dot_general x2, matrix products, along_rows(): lax.dot_general(left, right, (((0,), (0,)), ((), ())), preferred_element_...  23.5 us
    ppermute x16, starting transfers between devices, sent(): return lax.ppermute(value, AXES, pairs)  18.5 us
    dynamic_update_slice x11, local copies, waits for them, and re-layouts, placed_at(): return lax.dynamic_update_slice(whole, piece, (row, column))  13.5 us
  transfers between devices with their start and end apart: 16, of which 7 were waited for; matrix products, arithmetic and copies ran while one was open for 28% of the time, Pallas kernels for 0%

profile of v1, /device:TPU:13, one launch (start us, length us, event | category | flops | bytes accessed | tf_op | source)
XLA Modules:
  0.0 137.0 jit_solution(13917660465727189564)
XLA Ops:
  1.8 2.3 %collective-permute-start.1 = (bf16[128,512]{1,0:T(8,128)(2,1)S(1)}, bf16[128,512]{1,0:T(8,128)(2,1)S(1)}, u32[]{:S(2)}, u32[]{:S(2)}) collective-permute-start(bf16[128,512]{1,0:T(8,128)(2,1)S(1)} %constant_dynamic-slice_fusion.1), channel_id=1, source_target_pairs={{0,2},{1,3},{2,0},{3,1},{4,6},{5,7},{6,4},{7,5},{8,10},{9,11},{10,... | collective-permute-start | bytes 393224 | tf_op jit(solution)/shard_map/ppermute | solution.py:18
  4.1 2.2 %collective-permute-start = (bf16[128,512]{1,0:T(8,128)(2,1)S(1)}, bf16[128,512]{1,0:T(8,128)(2,1)S(1)}, u32[]{:S(2)}, u32[]{:S(2)}) collective-permute-start(bf16[128,512]{1,0:T(8,128)(2,1)S(1)} %constant_dynamic-slice_fusion.1), channel_id=1, source_target_pairs={{0,1},{1,2},{2,3},{3,0},{4,5},{5,6},{6,7},{7,4},{8,9},{9,10},{10,1... | collective-permute-start | bytes 393224 | tf_op jit(solution)/shard_map/ppermute | solution.py:18
  6.3 5.5 %collective-permute-done.1 = bf16[128,512]{1,0:T(8,128)(2,1)S(1)} collective-permute-done((bf16[128,512]{1,0:T(8,128)(2,1)S(1)}, bf16[128,512]{1,0:T(8,128)(2,1)S(1)}, u32[]{:S(2)}, u32[]{:S(2)}) %collective-permute-start.1) | collective-permute-done | bytes 131104 | tf_op jit(solution)/shard_map/ppermute | solution.py:18
  11.9 3.2 %collective-permute-done = bf16[128,512]{1,0:T(8,128)(2,1)S(1)} collective-permute-done((bf16[128,512]{1,0:T(8,128)(2,1)S(1)}, bf16[128,512]{1,0:T(8,128)(2,1)S(1)}, u32[]{:S(2)}, u32[]{:S(2)}) %collective-permute-start) | collective-permute-done | bytes 131104 | tf_op jit(solution)/shard_map/ppermute | solution.py:18
  15.1 2.5 %broadcast.8 = bf16[512,4096]{1,0:T(8,128)(2,1)} broadcast(bf16[]{:T(256)} %constant.8.clone.1), dimensions={} | broadcast | bytes 4194306 | tf_op jit(solution)/shard_map/broadcast.3
  18.4 1.2 collective-permute-start.3
  19.7 2.3 %collective-permute-start.8 = (bf16[128,1024]{1,0:T(8,128)(2,1)S(1)}, bf16[128,1024]{1,0:T(8,128)(2,1)S(1)}, u32[]{:S(2)}, u32[]{:S(2)}) collective-permute-start(bf16[128,1024]{1,0:T(8,128)(2,1)S(1)} %constant_dynamic-slice_fusion), channel_id=1, source_target_pairs={{0,1},{1,2},{2,3},{3,0},{4,5},{5,6},{6,7},{7,4},{8,9},{9,10},{10,1... | collective-permute-start | bytes 786440 | tf_op jit(solution)/shard_map/ppermute | solution.py:18
  22.9 1.1 pad_maximum_fusion
  24.6 14.1 %collective-permute-done.8 = bf16[128,1024]{1,0:T(8,128)(2,1)S(1)} collective-permute-done((bf16[128,1024]{1,0:T(8,128)(2,1)S(1)}, bf16[128,1024]{1,0:T(8,128)(2,1)S(1)}, u32[]{:S(2)}, u32[]{:S(2)}) %collective-permute-start.8) | collective-permute-done | bytes 262176 | tf_op jit(solution)/shard_map/ppermute | solution.py:18
  38.7 5.7 %collective-permute-done.9 = bf16[128,1024]{1,0:T(8,128)(2,1)S(1)} collective-permute-done((bf16[128,1024]{1,0:T(8,128)(2,1)S(1)}, bf16[128,1024]{1,0:T(8,128)(2,1)S(1)}, u32[]{:S(2)}, u32[]{:S(2)}) %collective-permute-start.9) | collective-permute-done | bytes 262176 | tf_op jit(solution)/shard_map/ppermute | solution.py:18
  44.5 1.1 collective-permute-done.10
  45.9 2.2 %collective-permute-start.11 = (bf16[384,1024]{1,0:T(8,128)(2,1)S(1)}, bf16[384,1024]{1,0:T(8,128)(2,1)}, u32[]{:S(2)}, u32[]{:S(2)}) collective-permute-start(bf16[384,1024]{1,0:T(8,128)(2,1)S(1)} %constant_dynamic-update-slice_fusion), channel_id=1, source_target_pairs={{0,16},{1,17},{2,18},{3,19},{4,20},{5,21},{6,22},{7,23},{8,24},{9,... | collective-permute-start | bytes 2359304 | tf_op jit(solution)/shard_map/ppermute | solution.py:18
  48.1 2.4 %dynamic_update_slice.47 = bf16[512,4096]{1,0:T(8,128)(2,1)} pad(bf16[128,4096]{1,0:T(8,128)(2,1)S(1)} %copy-done.4, bf16[]{:T(256)} %constant.8.clone.1), padding=0_384x0_0 | pad | bytes 5242882 | tf_op jit(solution)/shard_map/dynamic_update_slice | solution.py:36
  51.5 5.3 %collective-permute-done.12 = bf16[384,1024]{1,0:T(8,128)(2,1)S(1)} collective-permute-done((bf16[384,1024]{1,0:T(8,128)(2,1)S(1)}, bf16[384,1024]{1,0:T(8,128)(2,1)S(1)}, u32[]{:S(2)}, u32[]{:S(2)}) %collective-permute-start.12) | collective-permute-done | bytes 786464 | tf_op jit(solution)/shard_map/ppermute | solution.py:18
  56.8 1.8 %collective-permute-start.13 = (bf16[384,1024]{1,0:T(8,128)(2,1)S(1)}, bf16[384,1024]{1,0:T(8,128)(2,1)S(1)}, u32[]{:S(2)}, u32[]{:S(2)}) collective-permute-start(bf16[384,1024]{1,0:T(8,128)(2,1)S(1)} %collective-permute-done.12), channel_id=1, source_target_pairs={{0,16},{1,17},{2,18},{3,19},{4,20},{5,21},{6,22},{7,23},{8,24},{9,... | collective-permute-start | bytes 2359304 | tf_op jit(solution)/shard_map/ppermute | solution.py:18
  59.4 1.9 %fusion.31 = (bf16[512,512]{1,0:T(8,128)(2,1)S(1)}, bf16[512,4096]{1,0:T(8,128)(2,1)}) fusion(bf16[512,1024]{1,0:T(8,128)(2,1)} %collective-permute-done.4, bf16[512,4096]{1,0:T(8,128)(2,1)} %constant_dynamic-update-slice_fusion.6, s32[]{:T(128)S(6)} %select_n.83), kind=kLoop, calls=%fused_computation.56 | loop fusion | bytes 1572868 | tf_op jit(solution)/shard_map/slice | solution.py:88
  61.3 1.2 collective-permute-start.6
  62.6 2.1 %constant_dynamic-update-slice_fusion.10 = bf16[512,4096]{1,0:T(8,128)(2,1)} fusion(bf16[512,4096]{1,0:T(8,128)(2,1)} %constant_dynamic-update-slice_fusion.11, bf16[384,1024]{1,0:T(8,128)(2,1)} %collective-permute-done.11, s32[]{:T(128)S(6)} %select_n.90), kind=kLoop, calls=%fused_computation.51 | loop fusion | bytes 1572868 | tf_op jit(solution)/shard_map/dynamic_update_slice | solution.py:36
  65.7 1.9 %slice_dynamic-update-slice_fusion.2 = bf16[512,4096]{1,0:T(8,128)(2,1)} fusion(bf16[512,4096]{1,0:T(8,128)(2,1)} %get-tuple-element.3, s32[]{:T(128)S(6)} %select_n.84, bf16[512,1024]{1,0:T(8,128)(2,1)} %collective-permute-done.4), kind=kLoop, calls=%fused_computation.33 | loop fusion | bytes 1048580 | tf_op jit(solution)/shard_map/dynamic_update_slice | solution.py:36
  74.3 23.5 %fusion.14 = bf16[512,3584]{1,0:T(8,128)(2,1)} fusion(bf16[512,4096]{1,0:T(8,128)(2,1)S(1)} %broadcast_select_fusion, bf16[1,4096,3584]{2,1,0:T(8,128)(2,1)} %param.5), kind=kOutput, calls=%fused_computation.21 | convolution fusion | flops 15034220544 | bytes 37224448 | tf_op jit(solution)/shard_map/dot_general | solution.py:22
  97.8 2.2 %collective-permute-start.14 = (bf16[512,3584]{1,0:T(8,128)(2,1)}, bf16[512,3584]{1,0:T(8,128)(2,1)}, u32[]{:S(2)}, u32[]{:S(2)}) collective-permute-start(bf16[512,3584]{1,0:T(8,128)(2,1)} %fusion.14), channel_id=1, source_target_pairs={{0,16},{1,17},{2,18},{3,19},{4,20},{5,21},{6,22},{7,23},{8,24},{9,... | collective-permute-start | bytes 11010056 | tf_op jit(solution)/shard_map/ppermute | solution.py:18
  100.0 13.3 %fusion.20 = bf16[512,1792]{1,0:T(8,128)(2,1)S(1)} fusion(bf16[512,4096]{1,0:T(8,128)(2,1)} %constant_dynamic-update-slice_fusion.3, bf16[4096,3584]{1,0:T(8,128)(2,1)} %param.6, s32[]{:T(128)S(6)} %select_n.97), kind=kOutput, calls=%fused_computation.28 | convolution fusion | flops 7517110272 | bytes 20709380 | tf_op jit(solution)/shard_map/dot_general | solution.py:22
  113.5 9.0 %convolution_convert_fusion.1 = bf16[512,3584]{1,0:T(8,128)(2,1)} fusion(bf16[512,3584]{1,0:T(8,128)(2,1)} %collective-permute-done.14, bf16[512,3584]{1,0:T(8,128)(2,1)} %fusion.14, pred[]{:T(512)S(6)} %eq.3, bf16[512,4096]{1,0:T(8,128)(2,1)} %constant_dynamic-update-slice_fusion.3, s32[]{:T(128)S(6)} %select_n.101), kind=kOutput, calls=%fused_computation.22 | convolution fusion | flops 1899233280 | bytes 11534341 | tf_op jit(solution)/shard_map/dot_general | solution.py:26
  122.5 14.5 %fusion.13 = bf16[1,1024,3584]{2,1,0:T(8,128)(2,1)} fusion(bf16[512,1792]{1,0:T(8,128)(2,1)} %collective-permute-done.15, bf16[512,1792]{1,0:T(8,128)(2,1)} %copy-done.5, pred[]{:T(512)S(6)} %eq.3, bf16[512,3584]{1,0:T(8,128)(2,1)} %collective-permute-done.14, bf16[512,3584]{1,0:T(8,128)(2,1)} %fusion.14, bf16[512,4096]{1,0:T(8,128)(2,1)} %copy-done.3, ...), kind=kOutput, calls=%fused_computation.20 | convolution fusion | flops 3811311616 | bytes 19398660 | tf_op jit(solution)/shard_map/dot_general | solution.py:26
  (45 shorter events, 13.7 us)
Async XLA Ops:
  0.6 1.0 copy-start
  0.6 19.0 %copy-start.4 = (bf16[128,4096]{1,0:T(8,128)(2,1)S(1)}, bf16[128,4096]{1,0:T(8,128)(2,1)}, u32[]{:S(2)}) copy-start(bf16[128,4096]{1,0:T(8,128)(2,1)} %param.7) | copy-start | bytes 3145732
  1.6 4.7 %collective-permute-start.2 = (bf16[128,512]{1,0:T(8,128)(2,1)S(1)}, bf16[128,512]{1,0:T(8,128)(2,1)S(1)}, u32[]{:S(2)}, u32[]{:S(2)}) collective-permute-start(bf16[128,512]{1,0:T(8,128)(2,1)S(1)} %constant_dynamic-slice_fusion.1), channel_id=1, source_target_pairs={{0,3},{1,0},{2,1},{3,2},{4,7},{5,4},{6,5},{7,6},{8,11},{9,8},{10,9... | collective-permute-start | bytes 393224 | tf_op jit(solution)/shard_map/ppermute | solution.py:18
  1.8 10.0 %collective-permute-start.1 = (bf16[128,512]{1,0:T(8,128)(2,1)S(1)}, bf16[128,512]{1,0:T(8,128)(2,1)S(1)}, u32[]{:S(2)}, u32[]{:S(2)}) collective-permute-start(bf16[128,512]{1,0:T(8,128)(2,1)S(1)} %constant_dynamic-slice_fusion.1), channel_id=1, source_target_pairs={{0,2},{1,3},{2,0},{3,1},{4,6},{5,7},{6,4},{7,5},{8,10},{9,11},{10,... | collective-permute-start | bytes 393224 | tf_op jit(solution)/shard_map/ppermute | solution.py:18
  4.1 10.9 %collective-permute-start = (bf16[128,512]{1,0:T(8,128)(2,1)S(1)}, bf16[128,512]{1,0:T(8,128)(2,1)S(1)}, u32[]{:S(2)}, u32[]{:S(2)}) collective-permute-start(bf16[128,512]{1,0:T(8,128)(2,1)S(1)} %constant_dynamic-slice_fusion.1), channel_id=1, source_target_pairs={{0,1},{1,2},{2,3},{3,0},{4,5},{5,6},{6,7},{7,4},{8,9},{9,10},{10,1... | collective-permute-start | bytes 393224 | tf_op jit(solution)/shard_map/ppermute | solution.py:18
  18.4 4.4 %collective-permute-start.3 = (bf16[512,512]{1,0:T(8,128)(2,1)S(1)}, bf16[512,512]{1,0:T(8,128)(2,1)S(1)}, u32[]{:S(2)}, u32[]{:S(2)}) collective-permute-start(bf16[512,512]{1,0:T(8,128)(2,1)S(1)} %get-tuple-element.4), channel_id=1, source_target_pairs={{0,16},{1,17},{2,18},{3,19},{4,20},{5,21},{6,22},{7,23},{8,24},{9,... | collective-permute-start | bytes 1572872 | tf_op jit(solution)/shard_map/ppermute | solution.py:18
  19.7 19.0 %collective-permute-start.8 = (bf16[128,1024]{1,0:T(8,128)(2,1)S(1)}, bf16[128,1024]{1,0:T(8,128)(2,1)S(1)}, u32[]{:S(2)}, u32[]{:S(2)}) collective-permute-start(bf16[128,1024]{1,0:T(8,128)(2,1)S(1)} %constant_dynamic-slice_fusion), channel_id=1, source_target_pairs={{0,1},{1,2},{2,3},{3,0},{4,5},{5,6},{6,7},{7,4},{8,9},{9,10},{10,1... | collective-permute-start | bytes 786440 | tf_op jit(solution)/shard_map/ppermute | solution.py:18
  21.9 22.5 %collective-permute-start.9 = (bf16[128,1024]{1,0:T(8,128)(2,1)S(1)}, bf16[128,1024]{1,0:T(8,128)(2,1)S(1)}, u32[]{:S(2)}, u32[]{:S(2)}) collective-permute-start(bf16[128,1024]{1,0:T(8,128)(2,1)S(1)} %constant_dynamic-slice_fusion), channel_id=1, source_target_pairs={{0,2},{1,3},{2,0},{3,1},{4,6},{5,7},{6,4},{7,5},{8,10},{9,11},{10,... | collective-permute-start | bytes 786440 | tf_op jit(solution)/shard_map/ppermute | solution.py:18
  24.0 26.5 %collective-permute-start.4 = (bf16[512,1024]{1,0:T(8,128)(2,1)}, bf16[512,1024]{1,0:T(8,128)(2,1)}, u32[]{:S(2)}, u32[]{:S(2)}) collective-permute-start(bf16[512,1024]{1,0:T(8,128)(2,1)} %pad_maximum_fusion), channel_id=1, source_target_pairs={{0,4},{1,5},{2,6},{3,7},{4,0},{5,1},{6,2},{7,3},{8,12},{9,13},{10,... | collective-permute-start | bytes 3145736 | tf_op jit(solution)/shard_map/ppermute | solution.py:18
  24.2 21.3 %collective-permute-start.10 = (bf16[128,1024]{1,0:T(8,128)(2,1)S(1)}, bf16[128,1024]{1,0:T(8,128)(2,1)S(1)}, u32[]{:S(2)}, u32[]{:S(2)}) collective-permute-start(bf16[128,1024]{1,0:T(8,128)(2,1)S(1)} %constant_dynamic-slice_fusion), channel_id=1, source_target_pairs={{0,3},{1,0},{2,1},{3,2},{4,7},{5,4},{6,5},{7,6},{8,11},{9,8},{10,9... | collective-permute-start | bytes 786440 | tf_op jit(solution)/shard_map/ppermute | solution.py:18
  45.6 11.2 %collective-permute-start.12 = (bf16[384,1024]{1,0:T(8,128)(2,1)S(1)}, bf16[384,1024]{1,0:T(8,128)(2,1)S(1)}, u32[]{:S(2)}, u32[]{:S(2)}) collective-permute-start(bf16[384,1024]{1,0:T(8,128)(2,1)S(1)} %constant_dynamic-update-slice_fusion), channel_id=1, source_target_pairs={{0,4},{1,5},{2,6},{3,7},{4,0},{5,1},{6,2},{7,3},{8,12},{9,13},{10,... | collective-permute-start | bytes 2359304 | tf_op jit(solution)/shard_map/ppermute | solution.py:18
  45.9 16.7 %collective-permute-start.11 = (bf16[384,1024]{1,0:T(8,128)(2,1)S(1)}, bf16[384,1024]{1,0:T(8,128)(2,1)}, u32[]{:S(2)}, u32[]{:S(2)}) collective-permute-start(bf16[384,1024]{1,0:T(8,128)(2,1)S(1)} %constant_dynamic-update-slice_fusion), channel_id=1, source_target_pairs={{0,16},{1,17},{2,18},{3,19},{4,20},{5,21},{6,22},{7,23},{8,24},{9,... | collective-permute-start | bytes 2359304 | tf_op jit(solution)/shard_map/ppermute | solution.py:18
  50.5 20.0 %collective-permute-start.5 = (bf16[512,1024]{1,0:T(8,128)(2,1)}, bf16[512,1024]{1,0:T(8,128)(2,1)S(1)}, u32[]{:S(2)}, u32[]{:S(2)}) collective-permute-start(bf16[512,1024]{1,0:T(8,128)(2,1)} %collective-permute-done.4), channel_id=1, source_target_pairs={{0,16},{1,17},{2,18},{3,19},{4,20},{5,21},{6,22},{7,23},{8,24},{9,... | collective-permute-start | bytes 3145736 | tf_op jit(solution)/shard_map/ppermute | solution.py:18
  56.8 10.8 %collective-permute-start.13 = (bf16[384,1024]{1,0:T(8,128)(2,1)S(1)}, bf16[384,1024]{1,0:T(8,128)(2,1)S(1)}, u32[]{:S(2)}, u32[]{:S(2)}) collective-permute-start(bf16[384,1024]{1,0:T(8,128)(2,1)S(1)} %collective-permute-done.12), channel_id=1, source_target_pairs={{0,16},{1,17},{2,18},{3,19},{4,20},{5,21},{6,22},{7,23},{8,24},{9,... | collective-permute-start | bytes 2359304 | tf_op jit(solution)/shard_map/ppermute | solution.py:18
  61.3 8.3 %collective-permute-start.6 = (bf16[512,512]{1,0:T(8,128)(2,1)S(1)}, bf16[512,512]{1,0:T(8,128)(2,1)S(1)}, u32[]{:S(2)}, u32[]{:S(2)}) collective-permute-start(bf16[512,512]{1,0:T(8,128)(2,1)S(1)} %get-tuple-element.2), channel_id=1, source_target_pairs={{0,8},{1,9},{2,10},{3,11},{4,12},{5,13},{6,14},{7,15},{8,0},{9,1},... | collective-permute-start | bytes 1572872 | tf_op jit(solution)/shard_map/ppermute | solution.py:18
  68.6 5.3 %copy-start.2 = (bf16[512,4096]{1,0:T(8,128)(2,1)S(1)}, bf16[512,4096]{1,0:T(8,128)(2,1)}, u32[]{:S(2)}) copy-start(bf16[512,4096]{1,0:T(8,128)(2,1)} %constant_dynamic-update-slice_fusion.8) | copy-start | bytes 12582916
  69.7 3.3 %collective-permute-start.7 = (bf16[512,512]{1,0:T(8,128)(2,1)S(1)}, bf16[512,512]{1,0:T(8,128)(2,1)S(1)}, u32[]{:S(2)}, u32[]{:S(2)}) collective-permute-start(bf16[512,512]{1,0:T(8,128)(2,1)S(1)} %collective-permute-done.6), channel_id=1, source_target_pairs={{0,16},{1,17},{2,18},{3,19},{4,20},{5,21},{6,22},{7,23},{8,24},{9,... | collective-permute-start | bytes 1572872 | tf_op jit(solution)/shard_map/ppermute | solution.py:18
  74.3 23.5 %copy-start.3 = (bf16[512,4096]{1,0:T(8,128)(2,1)}, bf16[512,4096]{1,0:T(8,128)(2,1)S(1)}, u32[]{:S(2)}) copy-start(bf16[512,4096]{1,0:T(8,128)(2,1)S(1)} %broadcast_select_fusion) | copy-start | bytes 12582916
  97.8 15.7 %collective-permute-start.14 = (bf16[512,3584]{1,0:T(8,128)(2,1)}, bf16[512,3584]{1,0:T(8,128)(2,1)}, u32[]{:S(2)}, u32[]{:S(2)}) collective-permute-start(bf16[512,3584]{1,0:T(8,128)(2,1)} %fusion.14), channel_id=1, source_target_pairs={{0,16},{1,17},{2,18},{3,19},{4,20},{5,21},{6,22},{7,23},{8,24},{9,... | collective-permute-start | bytes 11010056 | tf_op jit(solution)/shard_map/ppermute | solution.py:18
  113.3 9.2 %copy-start.5 = (bf16[512,1792]{1,0:T(8,128)(2,1)}, bf16[512,1792]{1,0:T(8,128)(2,1)S(1)}, u32[]{:S(2)}) copy-start(bf16[512,1792]{1,0:T(8,128)(2,1)S(1)} %fusion.20) | copy-start | bytes 5505028
  113.3 9.2 %collective-permute-start.15 = (bf16[512,1792]{1,0:T(8,128)(2,1)S(1)}, bf16[512,1792]{1,0:T(8,128)(2,1)}, u32[]{:S(2)}, u32[]{:S(2)}) collective-permute-start(bf16[512,1792]{1,0:T(8,128)(2,1)S(1)} %fusion.20), channel_id=1, source_target_pairs={{0,16},{1,17},{2,18},{3,19},{4,20},{5,21},{6,22},{7,23},{8,24},{9,... | collective-permute-start | bytes 5505032 | tf_op jit(solution)/shard_map/ppermute | solution.py:18
  122.5 14.5 %copy-start.1 = (bf16[128,1024]{1,0:T(8,128)(2,1)S(1)}, bf16[128,1024]{1,0:T(8,128)(2,1)}, u32[]{:S(2)}) copy-start(bf16[128,1024]{1,0:T(8,128)(2,1)} %param.4) | copy-start | bytes 786436

commit v2 on v0

v2 whole, which is shorter than its diff:
```python
import jax
import jax.numpy as jnp
from jax import lax
from jax.experimental import pallas as pl
from jax.experimental.pallas import tpu as pltpu
from jax.sharding import PartitionSpec as P


AXES = ("section", "tensor", "dp")
TILE = 512


def sent(value, mesh, target):
    shape = [mesh.shape[axis] for axis in AXES]
    pairs = []
    for s in range(shape[0]):
        for t in range(shape[1]):
            for d in range(shape[2]):
                source = (s * shape[1] + t) * shape[2] + d
                to = target(s, t, d)
                pairs.append((source, (to[0] * shape[1] + to[1]) * shape[2] + to[2]))
    return lax.ppermute(value, AXES, pairs)


def matmul(left, right):
    return jnp.dot(left, right, preferred_element_type=jnp.float32)


def along_rows(left, right):
    return lax.dot_general(
        left, right, (((0,), (0,)), ((), ())), preferred_element_type=jnp.float32
    )


def columns(value, start, width):
    return lax.dynamic_slice_in_dim(value, start, width, 1)


def gradients(gate_pre, up_pre, grad_hidden, is_first):
    sigmoid_gate = jax.nn.sigmoid(gate_pre)
    silu = gate_pre * sigmoid_gate
    grad_gate = grad_hidden * up_pre * sigmoid_gate * (1.0 + gate_pre * (1.0 - sigmoid_gate))
    right = jnp.where(is_first, grad_gate, silu * up_pre)
    return right.astype(jnp.bfloat16), (grad_hidden * silu).astype(jnp.bfloat16)


def local_plain(mesh, tokens, section_weights, up_weight, cotangent):
    section = lax.axis_index("section")
    group = lax.axis_index("dp")
    groups = mesh.shape["dp"]
    is_first = section == 0
    slot = section_weights[0]
    units = slot.shape[1]
    width = cotangent.shape[1]

    def swapped(value):
        return sent(value, mesh, lambda s, t, d: (1 - s, t, d))

    tokens_all = lax.all_gather(tokens, "tensor", axis=1, tiled=True)
    tokens_all = lax.all_gather(tokens_all, "dp", axis=0, tiled=True)
    cotangent_all = lax.all_gather(cotangent, "dp", axis=0, tiled=True)
    used = jnp.where(is_first, tokens_all, cotangent_all)
    own = matmul(used, slot).astype(jnp.bfloat16)
    other = swapped(own)
    half = units // 2
    up_own = matmul(tokens_all, columns(up_weight, section * half, half)).astype(jnp.bfloat16)
    up_other = swapped(up_own)
    up_pre = jnp.where(
        is_first,
        jnp.concatenate([up_own, up_other], 1),
        jnp.concatenate([up_other, up_own], 1),
    ).astype(jnp.float32)
    gate_pre = jnp.where(is_first, own, other).astype(jnp.float32)
    grad_hidden = jnp.where(is_first, other, own).astype(jnp.float32)
    right, grad_up = gradients(gate_pre, up_pre, grad_hidden, is_first)
    slot_rows = width // groups
    up_rows = slot_rows // 2
    slot_sum = along_rows(columns(used, group * slot_rows, slot_rows), right)
    up_sum = along_rows(columns(tokens_all, (section * groups + group) * up_rows, up_rows), grad_up)
    return (slot_sum.astype(jnp.bfloat16)[None], up_sum.astype(jnp.bfloat16))


def cost(flops, moved):
    return pl.CostEstimate(flops=int(flops), bytes_accessed=int(moved), transcendentals=0)


def product(info, pieces, weight, first_tile, tiles, dtype, start=None, head=None, room=None):
    arrays = []
    for array, _, _, _ in pieces:
        if not any(array is a for a in arrays):
            arrays.append(array)
    which = [next(i for i, a in enumerate(arrays) if a is array) for array, _, _, _ in pieces]
    count = arrays[0].shape[0]
    above = 0 if head is None else head.shape[0]

    def kernel(info_ref, *refs):
        lefts = refs[: len(arrays)]
        rights = refs[len(arrays) : len(arrays) + len(pieces)]
        rest = list(refs[len(arrays) + len(pieces) :])
        out = rest.pop()
        total = None
        for (_, begin, depth, _), i, right in zip(pieces, which, rights):
            term = matmul(lefts[i][:, begin : begin + depth], right[...])
            total = term if total is None else total + term
        if start is not None:
            total = total + rest.pop(0)[...].astype(jnp.float32)
        if head is not None:
            out[:above, :] = rest.pop(0)[...]
        out[above:, :] = total.astype(dtype)

    specs = [pl.BlockSpec(a.shape, lambda j, info: (0, 0)) for a in arrays]
    for _, _, depth, row in pieces:
        specs.append(
            pl.BlockSpec((depth, TILE), lambda j, info, row=row: (row(info), first_tile + j))
        )
    operands = list(arrays) + [weight] * len(pieces)
    for extra in (start, head):
        if extra is not None:
            specs.append(pl.BlockSpec((extra.shape[0], TILE), lambda j, info: (0, first_tile + j)))
            operands.append(extra)
    out = jax.ShapeDtypeStruct((above + count, (room or tiles) * TILE), dtype)
    deep = sum(p[2] for p in pieces)
    return pl.pallas_call(
        kernel,
        grid_spec=pltpu.PrefetchScalarGridSpec(
            num_scalar_prefetch=1,
            grid=(tiles,),
            in_specs=specs,
            out_specs=pl.BlockSpec((above + count, TILE), lambda j, info: (0, j)),
        ),
        out_shape=out,
        compiler_params=pltpu.CompilerParams(vmem_limit_bytes=48 * 1024 * 1024),
        cost_estimate=cost(2 * count * deep * tiles * TILE, 2 * deep * tiles * TILE + out.size * 2),
    )(info, *operands)


def unset(shape, dtype):
    return pl.pallas_call(
        lambda out: None,
        out_shape=jax.ShapeDtypeStruct(shape, dtype),
        out_specs=pl.BlockSpec(memory_space=pl.ANY),
    )()


def outputs(is_gate, left_slot, left_up, gate, hidden, ups, up_of, first, units, begun):
    tiles = gate.shape[1] // TILE
    count = gate.shape[0]
    used = sorted({up_of(first + j)[0] for j in range(tiles)})

    def kernel(a_slot, a_up, gate_ref, hidden_ref, *refs):
        up_refs = refs[: len(used)]
        slot_ref, up_ref = refs[-2:]
        gate_pre = gate_ref[...].astype(jnp.float32)
        grad_hidden = hidden_ref[...].astype(jnp.float32)
        up_pre = up_refs[0][...]
        if len(used) == 2:
            j = pl.program_id(0) + first
            early = sum(up_of(first + k)[0] == used[0] for k in range(tiles)) + first
            up_pre = jnp.where(j < early, up_pre, up_refs[1][...])
        up_pre = up_pre.astype(jnp.float32)
        sigmoid_gate = jax.nn.sigmoid(gate_pre)
        silu = gate_pre * sigmoid_gate
        grad_up = (grad_hidden * silu).astype(jnp.bfloat16)
        if is_gate:
            right = grad_hidden * up_pre * sigmoid_gate * (1.0 + gate_pre * (1.0 - sigmoid_gate))
        else:
            right = silu * up_pre
        slot_ref[...] = along_rows(a_slot[...], right.astype(jnp.bfloat16)).astype(jnp.bfloat16)
        up_ref[...] = along_rows(a_up[...], grad_up).astype(jnp.bfloat16)

    def up_tile(which):
        own = [k for k in range(tiles) if up_of(first + k)[0] == which]
        base = up_of(first + own[0])[1] - own[0]
        return lambda j: (0, jnp.clip(j, own[0], own[-1]) + base)

    whole = lambda j: (0, 0)
    here = lambda j: (0, j)
    there = lambda j: (0, j + first)
    block = (count, TILE)
    specs = [
        pl.BlockSpec(left_slot.shape, whole),
        pl.BlockSpec(left_up.shape, whole),
        pl.BlockSpec(block, here),
        pl.BlockSpec(block, here),
    ] + [pl.BlockSpec(block, up_tile(k)) for k in used]
    operands = [left_slot, left_up, gate, hidden] + [ups[k] for k in used]
    rows = (left_slot.shape[1], left_up.shape[1])
    aliases = {}
    if begun is not None:
        specs += [pl.BlockSpec(memory_space=pl.ANY)] * 2
        aliases = {len(operands): 0, 1 + len(operands): 1}
        operands += list(begun)
    return pl.pallas_call(
        kernel,
        grid=(tiles,),
        in_specs=specs,
        out_specs=[pl.BlockSpec((r, TILE), there) for r in rows],
        out_shape=[jax.ShapeDtypeStruct((r, units), jnp.bfloat16) for r in rows],
        input_output_aliases=aliases,
        compiler_params=pltpu.CompilerParams(vmem_limit_bytes=48 * 1024 * 1024),
        cost_estimate=cost(
            2 * count * sum(rows) * tiles * TILE, 2 * tiles * TILE * (4 * count + sum(rows))
        ),
    )(*operands)


def local_by_chip(mesh, tokens, section_weights, up_weight, cotangent):
    groups = mesh.shape["dp"]
    section = lax.axis_index("section")
    tensor = lax.axis_index("tensor")
    group = lax.axis_index("dp")
    is_first = section == 0
    place = lax.broadcasted_iota(jnp.int32, (3,), 0)
    info = jnp.where(place == 0, section, jnp.where(place == 1, tensor, group)).astype(jnp.int32)
    slot = section_weights[0]
    count, block = tokens.shape
    half = block // 2
    width, units = slot.shape
    quarter = width // 4
    everyone = groups * count
    tiles = units // TILE
    most = (tiles + 1) // 2
    few = tiles - most
    low = jnp.bfloat16

    def moved(value, target):
        return sent(value, mesh, target)

    def ring(step):
        return lambda s, t, d: (s, t, (d + step) % groups)

    def other_section(s, t, d):
        return (1 - s, t, d)

    def near(s, t, d):
        return (s, t ^ (1 + s), d)

    def far(s, t, d):
        return (s, t ^ (2 - s), d)

    steps = range(1, groups)
    parity = (tensor ^ (tensor >> 1)) & 1
    own_half = columns(tokens, section * half, half)
    own_quarter = columns(cotangent, (2 * parity + section) * quarter, quarter)

    mine = jnp.concatenate([own_half] + [moved(own_half, ring(k)) for k in steps], 0)
    theirs = moved(mine, other_section)
    first_mine = jnp.concatenate([moved(own_quarter, ring(k)) for k in steps], 0)
    both = jnp.concatenate([mine, theirs], 1)
    beside = moved(both, near)
    beside_too = moved(beside, other_section)
    across = moved(beside[:, :half], far)
    across_too = moved(across, other_section)
    first_theirs = moved(first_mine, other_section)
    second_mine = moved(first_mine, near)
    second_theirs = moved(second_mine, other_section)

    def odd(i):
        return (i[1] ^ (i[1] >> 1)) & 1

    here = [
        (both, 0, half, lambda i: 2 * i[1] + i[0]),
        (both, half, half, lambda i: 2 * i[1] + 1 - i[0]),
    ]
    rest = [
        (beside, 0, half, lambda i: 2 * (i[1] ^ (1 + i[0])) + i[0]),
        (beside, half, half, lambda i: 2 * (i[1] ^ (1 + i[0])) + 1 - i[0]),
        (beside_too, 0, half, lambda i: 2 * (i[1] ^ (2 - i[0])) + 1 - i[0]),
        (beside_too, half, half, lambda i: 2 * (i[1] ^ (2 - i[0])) + i[0]),
        (across, 0, half, lambda i: 2 * (i[1] ^ 3) + i[0]),
        (across_too, 0, half, lambda i: 2 * (i[1] ^ 3) + 1 - i[0]),
    ]
    cots = [
        (first_mine, 0, quarter, lambda i: 2 * odd(i) + i[0]),
        (first_theirs, 0, quarter, lambda i: 2 * odd(i) + 1 - i[0]),
        (second_mine, 0, quarter, lambda i: 2 * (1 - odd(i)) + i[0]),
        (second_theirs, 0, quarter, lambda i: 2 * (1 - odd(i)) + 1 - i[0]),
    ]
    whole = [(cotangent, 0, width, lambda i: 0)]

    begun, own_rows = lax.cond(
        is_first,
        lambda: (
            product(info, here, slot, 0, tiles, jnp.float32),
            unset((count, units), low),
        ),
        lambda: (unset((everyone, units), jnp.float32), product(info, whole, slot, 0, tiles, low)),
    )
    one = lax.cond(
        is_first,
        lambda: product(info, rest, slot, 0, most, low, start=begun),
        lambda: product(info, here + rest, up_weight, few, most, low),
    )
    one_passed = moved(one, other_section)
    two = lax.cond(
        is_first,
        lambda: product(info, here + rest, up_weight, 0, few, low, room=most),
        lambda: product(info, cots, slot, 0, most, low, head=own_rows),
    )
    two_passed = moved(two, other_section)
    three = lax.cond(
        is_first,
        lambda: product(info, rest, slot, most, few, low, start=begun),
        lambda: product(info, cots, slot, most, few, low, head=own_rows),
    )
    three_passed = moved(three, other_section)

    def token_columns(at):
        chosen = None
        for array, begin, depth, row in here + rest:
            piece = array[:, begin : begin + depth]
            hit = row((section, tensor, group)) == at
            chosen = piece if chosen is None else jnp.where(hit, piece, chosen)
        return chosen

    def cotangent_columns(at):
        chosen = None
        for array, _, _, row in cots:
            hit = row((section, tensor, group)) == at
            chosen = array if chosen is None else jnp.where(hit, array, chosen)
        return jnp.concatenate([columns(cotangent, at * quarter, quarter), chosen], 0)

    left_slot, left_up = lax.cond(
        is_first,
        lambda: (
            jnp.concatenate([token_columns(2 * group), token_columns(2 * group + 1)], 1),
            token_columns(group),
        ),
        lambda: (cotangent_columns(group), token_columns(groups + group)),
    )

    def up_of(j):
        return (0, j) if j < few else (1, j - few)

    grads = lax.cond(
        is_first,
        lambda: outputs(
            True, left_slot, left_up, one, two_passed, (two, one_passed), up_of, 0, units, None
        ),
        lambda: outputs(
            False, left_slot, left_up, one_passed, two, (two_passed, one), up_of, 0, units, None
        ),
    )
    slot_sum, up_sum = lax.cond(
        is_first,
        lambda: outputs(
            True, left_slot, left_up, three, three_passed, (two, one_passed), up_of, most,
            units, grads,
        ),
        lambda: outputs(
            False, left_slot, left_up, three_passed, three, (two_passed, one), up_of, most,
            units, grads,
        ),
    )
    return (slot_sum[None], up_sum)


def solution(mesh):
    placed = (P("dp", "tensor"), P("section", None, "tensor"), P(None, "tensor"), P("dp", None))
    by_chip = mesh.shape["tensor"] == 4 and mesh.shape["dp"] == 4 and mesh.shape["section"] == 2

    def body(*arrays):
        return (local_by_chip if by_chip else local_plain)(mesh, *arrays)

    return jax.shard_map(
        body,
        mesh=mesh,
        in_specs=placed,
        out_specs=(P("section", "dp", "tensor"), P(("section", "dp"), "tensor")),
        check_vma=False,
    )
```

time: 822 us -> 138 us (0.17)
  waiting for transfers between devices: 750 us -> 43.4 us
  Pallas kernels: 0 us -> 66.8 us
  matrix products: 49.2 us -> 0 us
  between operations: 13.8 us -> 0.77 us
  starting transfers between devices: 4.21 us -> 13.8 us
    reduce_scatter x2 -> x0, waiting for transfers between devices: 713 us -> none  [the longest x1 486 us: local(): lax.psum_scatter(slot_part.astype(jnp.bfloat16), 'dp', scatter_dimension=...]
    pallas_call x0 -> x7, Pallas kernels: none -> 66.8 us  [the longest x4 52.2 us: product(): pl.pallas_call(kernel, grid_spec=pltpu.PrefetchScalarGridSpec(num_scalar_...]
    dot_general x4 -> x0, matrix products: 49.2 us -> none  [the longest x2 27.1 us: matmul(): return jnp.dot(left, right, preferred_element_type=jnp.float32)]
    ppermute x3 -> x17, waiting for transfers between devices: 7.32 us -> 43.4 us  [sent(): return lax.ppermute(value, AXES, pairs)]
    all_gather x1 -> x0, waiting for transfers between devices: 29.3 us -> none  [local(): tokens_all = lax.all_gather(tokens, 'tensor', axis=1, tiled=True)]
    ppermute x3 -> x17, starting transfers between devices: 4.09 us -> 13.8 us  [sent(): return lax.ppermute(value, AXES, pairs)]
  transfers between devices with their start and end apart: 6 -> 17, of which waited for: 6 -> 6; matrix products, arithmetic and copies ran while one was open for 2% -> 6% of each run, Pallas kernels for 0% -> 25%
where the time goes in v2:
time: 138 us; the launch traced here: 137 us
  Pallas kernels  66.8 us (48%)
  waiting for transfers between devices  43.4 us (31%)
  starting transfers between devices  13.8 us (10%)
  local copies, waits for them, and re-layouts  7.93 us (6%)
  other arithmetic  3.83 us (3%)
    pallas_call x4, Pallas kernels, product(): pl.pallas_call(kernel, grid_spec=pltpu.PrefetchScalarGridSpec(num_scalar_...  52.2 us
    ppermute x17, waiting for transfers between devices, sent(): return lax.ppermute(value, AXES, pairs)  43.4 us
    pallas_call x2, Pallas kernels, outputs(): pl.pallas_call(kernel, grid=(tiles,), in_specs=specs, out_specs=[pl.Block...  14.6 us
    ppermute x17, starting transfers between devices, sent(): return lax.ppermute(value, AXES, pairs)  13.8 us
    unnamed x16, local copies, waits for them, and re-layouts  5.21 us
  transfers between devices with their start and end apart: 17, of which 6 were waited for; matrix products, arithmetic and copies ran while one was open for 6% of the time, Pallas kernels for 25%

profile of v2, /device:TPU:13, one launch (start us, length us, event | category | flops | bytes accessed | tf_op | source)
XLA Modules:
  0.0 136.6 jit_solution(12902174191201862415)
XLA Ops:
  1.8 2.3 %collective-permute-start.7 = (bf16[128,512]{1,0:T(8,128)(2,1)S(1)}, bf16[128,512]{1,0:T(8,128)(2,1)S(1)}, u32[]{:S(2)}, u32[]{:S(2)}) collective-permute-start(bf16[128,512]{1,0:T(8,128)(2,1)S(1)} %constant_dynamic-slice_fusion.1), channel_id=1, source_target_pairs={{0,2},{1,3},{2,0},{3,1},{4,6},{5,7},{6,4},{7,5},{8,10},{9,11},{10,... | collective-permute-start | bytes 393224 | tf_op jit(solution)/shard_map/ppermute | solution.py:22
  4.1 2.2 %collective-permute-start.6 = (bf16[128,512]{1,0:T(8,128)(2,1)S(1)}, bf16[128,512]{1,0:T(8,128)(2,1)S(1)}, u32[]{:S(2)}, u32[]{:S(2)}) collective-permute-start(bf16[128,512]{1,0:T(8,128)(2,1)S(1)} %constant_dynamic-slice_fusion.1), channel_id=1, source_target_pairs={{0,1},{1,2},{2,3},{3,0},{4,5},{5,6},{6,7},{7,4},{8,9},{9,10},{10,1... | collective-permute-start | bytes 393224 | tf_op jit(solution)/shard_map/ppermute | solution.py:22
  6.3 5.5 %collective-permute-done.7 = bf16[128,512]{1,0:T(8,128)(2,1)S(1)} collective-permute-done((bf16[128,512]{1,0:T(8,128)(2,1)S(1)}, bf16[128,512]{1,0:T(8,128)(2,1)S(1)}, u32[]{:S(2)}, u32[]{:S(2)}) %collective-permute-start.7) | collective-permute-done | bytes 131104 | tf_op jit(solution)/shard_map/ppermute | solution.py:22
  11.9 3.2 %collective-permute-done.6 = bf16[128,512]{1,0:T(8,128)(2,1)S(1)} collective-permute-done((bf16[128,512]{1,0:T(8,128)(2,1)S(1)}, bf16[128,512]{1,0:T(8,128)(2,1)S(1)}, u32[]{:S(2)}, u32[]{:S(2)}) %collective-permute-start.6) | collective-permute-done | bytes 131104 | tf_op jit(solution)/shard_map/ppermute | solution.py:22
  17.4 2.3 %collective-permute-start = (bf16[128,1024]{1,0:T(8,128)(2,1)S(1)}, bf16[128,1024]{1,0:T(8,128)(2,1)S(1)}, u32[]{:S(2)}, u32[]{:S(2)}) collective-permute-start(bf16[128,1024]{1,0:T(8,128)(2,1)S(1)} %constant_dynamic-slice_fusion.2), channel_id=1, source_target_pairs={{0,1},{1,2},{2,3},{3,0},{4,5},{5,6},{6,7},{7,4},{8,9},{9,10},{10,1... | collective-permute-start | bytes 786440 | tf_op jit(solution)/shard_map/ppermute | solution.py:22
  22.6 3.0 %collective-permute-done = bf16[128,1024]{1,0:T(8,128)(2,1)S(1)} collective-permute-done((bf16[128,1024]{1,0:T(8,128)(2,1)S(1)}, bf16[128,1024]{1,0:T(8,128)(2,1)S(1)}, u32[]{:S(2)}, u32[]{:S(2)}) %collective-permute-start) | collective-permute-done | bytes 262176 | tf_op jit(solution)/shard_map/ppermute | solution.py:22
  26.3 15.7 %collective-permute-done.1 = bf16[128,1024]{1,0:T(8,128)(2,1)S(1)} collective-permute-done((bf16[128,1024]{1,0:T(8,128)(2,1)S(1)}, bf16[128,1024]{1,0:T(8,128)(2,1)S(1)}, u32[]{:S(2)}, u32[]{:S(2)}) %collective-permute-start.1) | collective-permute-done | bytes 262176 | tf_op jit(solution)/shard_map/ppermute | solution.py:22
  42.7 1.5 %collective-permute-done.2 = bf16[128,1024]{1,0:T(8,128)(2,1)S(1)} collective-permute-done((bf16[128,1024]{1,0:T(8,128)(2,1)S(1)}, bf16[128,1024]{1,0:T(8,128)(2,1)S(1)}, u32[]{:S(2)}, u32[]{:S(2)}) %collective-permute-start.2) | collective-permute-done | bytes 262176 | tf_op jit(solution)/shard_map/ppermute | solution.py:22
  47.5 14.5 %collective-permute-done.4 = bf16[384,1024]{1,0:T(8,128)(2,1)} collective-permute-done((bf16[384,1024]{1,0:T(8,128)(2,1)}, bf16[384,1024]{1,0:T(8,128)(2,1)}, u32[]{:S(2)}, u32[]{:S(2)}) %collective-permute-start.4) | collective-permute-done | bytes 786464 | tf_op jit(solution)/shard_map/ppermute | solution.py:22
  62.5 13.8 %conditional.8 = (f32[512,3584]{1,0:T(8,128)}, bf16[128,3584]{1,0:T(8,128)(2,1)}) conditional(s32[]{:T(128)} %convert_element_type.2, (s32[3]{0:T(128)S(1)}, bf16[128,4096]{1,0:T(8,128)(2,1)}, bf16[4096,3584]{1,0:T(8,128)(2,1)}) %tuple.88, (s32[3]{0:T(128)S(1)}, bf16[512,1024]{1,0:T(8,128)(2,1)}, bf16[4096,3584]{1,0:T(8,128)(2,1)}) %tuple.94), branch_computations={%region_2.3_spmd, %region_3.4_spmd} | conditional | flops 3758096384 | bytes 30277648 | solution.py:281
  62.5 13.8 %branch_0_fun.8 = bf16[128,3584]{1,0:T(8,128)(2,1)} custom-call(s32[3]{0:T(128)S(1)} %get-tuple-element.231.info_ref, bf16[128,4096]{1,0:T(8,128)(2,1)} %get-tuple-element.232.refs_0_, bf16[4096,3584]{1,0:T(8,128)(2,1)} %get-tuple-element.233.refs_1_), custom_call_target="tpu_custom_call" | custom-call | flops 3758096384 | bytes 30277632 | tf_op jit(solution)/shard_map/cond/branch_0_fun/pallas_call | solution.py:123
  76.4 13.8 %conditional.10 = (bf16[512,2048]{1,0:T(8,128)(2,1)}) conditional(s32[]{:T(128)} %convert_element_type.2, (s32[3]{0:T(128)S(1)}, bf16[512,1024]{1,0:T(8,128)(2,1)}, bf16[512,1024]{1,0:T(8,128)(2,1)S(1)}, bf16[512,1024]{1,0:T(8,128)(2,1)S(1)}, bf16[512,512]{1,0:T(8,128)(2,1)S(1)}, /*index=5*/bf16[512,512]{1,0:T(8,128)(2,1)S(1)}, ...), branch_computations={%region_6.7_spmd, %region_7.8_spmd} | conditional | flops 8589934592 | bytes 18874376 | solution.py:289
  76.4 13.8 %branch_0_fun.10 = bf16[512,2048]{1,0:T(8,128)(2,1)} custom-call(s32[3]{0:T(128)S(1)} %get-tuple-element.251.info_ref, bf16[512,1024]{1,0:T(8,128)(2,1)} %get-tuple-element.252.refs_0_, bf16[512,1024]{1,0:T(8,128)(2,1)S(1)} %get-tuple-element.253.refs_1_, bf16[512,1024]{1,0:T(8,128)(2,1)S(1)} %get-tuple-element.254.refs_2_, ...), custom_call_target="tpu_custom_call" | custom-call | flops 8589934592 | bytes 18874368 | tf_op jit(solution)/shard_map/cond/branch_0_fun/pallas_call | solution.py:123
  90.2 13.2 %conditional.11 = (bf16[512,2048]{1,0:T(8,128)(2,1)}) conditional(s32[]{:T(128)} %convert_element_type.2, (s32[3]{0:T(128)S(1)}, bf16[384,1024]{1,0:T(8,128)(2,1)}, bf16[384,1024]{1,0:T(8,128)(2,1)}, bf16[384,1024]{1,0:T(8,128)(2,1)}, bf16[384,1024]{1,0:T(8,128)(2,1)}, /*index=5*/bf16[4096,3584]{1,0:T(8,128)(2,1)}, ...), branch_computations={%region_8.9_spmd, %region_9.10_spmd} | conditional | flops 6442450944 | bytes 18874376 | solution.py:295
  90.2 13.2 %branch_0_fun.11 = bf16[512,2048]{1,0:T(8,128)(2,1)} custom-call(s32[3]{0:T(128)S(1)} %get-tuple-element.265.info_ref, bf16[384,1024]{1,0:T(8,128)(2,1)} %get-tuple-element.266.refs_0_, bf16[384,1024]{1,0:T(8,128)(2,1)} %get-tuple-element.267.refs_1_, bf16[384,1024]{1,0:T(8,128)(2,1)} %get-tuple-element.268.refs_2_, ...), custom_call_target="tpu_custom_call" | custom-call | flops 6442450944 | bytes 18874368 | tf_op jit(solution)/shard_map/cond/branch_0_fun/pallas_call | solution.py:123
  103.9 11.4 %conditional.9 = (bf16[512,1536]{1,0:T(8,128)(2,1)}) conditional(s32[]{:T(128)} %convert_element_type.2, (s32[3]{0:T(128)S(1)}, bf16[384,1024]{1,0:T(8,128)(2,1)}, bf16[384,1024]{1,0:T(8,128)(2,1)}, bf16[384,1024]{1,0:T(8,128)(2,1)}, bf16[384,1024]{1,0:T(8,128)(2,1)}, /*index=5*/bf16[4096,3584]{1,0:T(8,128)(2,1)}, ...), branch_computations={%region_4.5_spmd, %region_5.6_spmd} | conditional | flops 4831838208 | bytes 14155784 | solution.py:301
  103.9 11.4 %branch_0_fun.9 = bf16[512,1536]{1,0:T(8,128)(2,1)} custom-call(s32[3]{0:T(128)S(1)} %get-tuple-element.237.info_ref, bf16[384,1024]{1,0:T(8,128)(2,1)} %get-tuple-element.238.refs_0_, bf16[384,1024]{1,0:T(8,128)(2,1)} %get-tuple-element.239.refs_1_, bf16[384,1024]{1,0:T(8,128)(2,1)} %get-tuple-element.240.refs_2_, ...), custom_call_target="tpu_custom_call" | custom-call | flops 4831838208 | bytes 14155776 | tf_op jit(solution)/shard_map/cond/branch_0_fun/pallas_call | solution.py:123
  115.3 4.7 %conditional.7 = (bf16[512,1024]{1,0:T(8,128)(2,1)S(1)}, bf16[512,512]{1,0:T(8,128)(2,1)}) conditional(s32[]{:T(128)} %convert_element_type.2, (s32[]{:T(128)}, bf16[128,4096]{1,0:T(8,128)(2,1)}, s32[]{:T(128)}, s32[]{:T(128)}, bf16[384,1024]{1,0:T(8,128)(2,1)}, /*index=5*/bf16[384,1024]{1,0:T(8,128)(2,1)}, bf16[384,1024]{1,0:T(8,128)(2,1)}, ...), branch_computations={%region_0.1_spmd, %region_1.2_spmd} | conditional | flops 7602219 | bytes 20447778 | solution.py:323
  116.3 2.1 %select_select_fusion.1 = bf16[512,512]{1,0:T(8,128)(2,1)} fusion(bf16[512,512]{1,0:T(8,128)(2,1)S(1)} %get-tuple-element.216, bf16[512,512]{1,0:T(8,128)(2,1)S(1)} %get-tuple-element.217, bf16[512,512]{1,0:T(8,128)(2,1)} %get-tuple-element.220, bf16[512,512]{1,0:T(8,128)(2,1)} %get-tuple-element.221, bf16[512,1024]{1,0:T(8,128)(2,1)S(1)} %get-tuple-element.219, ...), kind=kLoop, calls=%fused_computation.2 | loop fusion | flops 1835008 | bytes 4718599 | tf_op jit(solution)/shard_map/cond/branch_0_fun/jit(_where)/select_n | solution.py:313
  118.4 1.5 %select_select_fusion = bf16[384,1024]{1,0:T(8,128)(2,1)S(1)} fusion(bf16[384,1024]{1,0:T(8,128)(2,1)} %get-tuple-element.212, bf16[384,1024]{1,0:T(8,128)(2,1)} %get-tuple-element.213, bf16[384,1024]{1,0:T(8,128)(2,1)} %get-tuple-element.214, bf16[384,1024]{1,0:T(8,128)(2,1)} %get-tuple-element.215, pred[]{:T(512)S(6)} %eq.70, pred[]{:T(512)S(6)} %eq.69, ...), kind=kLoop, calls=%fused_computation.1 | loop fusion | flops 1179648 | bytes 3932163 | tf_op jit(solution)/shard_map/cond/branch_0_fun/jit(_where)/select_n | solution.py:320
  121.0 8.2 %conditional.12 = ((bf16[1024,3584]{1,0:T(8,128)(2,1)}, bf16[512,3584]{1,0:T(8,128)(2,1)})) conditional(s32[]{:T(128)} %convert_element_type.2, (bf16[512,1024]{1,0:T(8,128)(2,1)}, bf16[512,512]{1,0:T(8,128)(2,1)}, bf16[512,2048]{1,0:T(8,128)(2,1)}, bf16[512,2048]{1,0:T(8,128)(2,1)}, bf16[512,2048]{1,0:T(8,128)(2,1)}, ...), branch_computations={%region_10.11_spmd, %region_11.12_spmd} | conditional | flops 3221225472 | bytes 14680072 | solution.py:335
  121.0 8.2 %branch_0_fun.12 = (bf16[1024,3584]{1,0:T(8,128)(2,1)}, bf16[512,3584]{1,0:T(8,128)(2,1)}) custom-call(bf16[512,1024]{1,0:T(8,128)(2,1)} %get-tuple-element.279.a_slot, bf16[512,512]{1,0:T(8,128)(2,1)} %get-tuple-element.280.a_up, bf16[512,2048]{1,0:T(8,128)(2,1)} %get-tuple-element.281.gate_ref, bf16[512,2048]{1,0:T(8,128)(2,1)} %get-tuple-element.282.hidden_ref, ...), custom_call_target="tpu_custom_call" | custom-call | flops 3221225472 | bytes 14680064 | tf_op jit(solution)/shard_map/cond/branch_0_fun/pallas_call | solution.py:193
  129.3 6.4 %conditional.13 = (bf16[512,3584]{1,0:T(8,128)(2,1)}, bf16[1,1024,3584]{2,1,0:T(8,128)(2,1)}) conditional(s32[]{:T(128)} %convert_element_type.2, (bf16[512,1024]{1,0:T(8,128)(2,1)}, bf16[512,512]{1,0:T(8,128)(2,1)}, bf16[512,1536]{1,0:T(8,128)(2,1)}, bf16[512,1536]{1,0:T(8,128)(2,1)S(1)}, bf16[512,2048]{1,0:T(8,128)(2,1)}, ...), branch_computations={%region_12.13_spmd, %region_13.14_spmd} | conditional | flops 2415919104 | bytes 11010064 | solution.py:344
  129.3 6.3 %branch_0_fun.13 = (bf16[1024,3584]{1,0:T(8,128)(2,1)}, bf16[512,3584]{1,0:T(8,128)(2,1)}) custom-call(bf16[512,1024]{1,0:T(8,128)(2,1)} %get-tuple-element.291.a_slot, bf16[512,512]{1,0:T(8,128)(2,1)} %get-tuple-element.292.a_up, bf16[512,1536]{1,0:T(8,128)(2,1)} %get-tuple-element.293.gate_ref, ...), custom_call_target="tpu_custom_call", output_to_operand_aliasing={{0}: (5, {}), {1}: (6, {})} | custom-call | flops 2415919104 | bytes 11010048 | tf_op jit(solution)/shard_map/cond/branch_0_fun/pallas_call | solution.py:193
  (51 shorter events, 15.3 us)
Async XLA Ops:
  0.6 1.0 copy-start
  1.6 4.7 %collective-permute-start.8 = (bf16[128,512]{1,0:T(8,128)(2,1)S(1)}, bf16[128,512]{1,0:T(8,128)(2,1)S(1)}, u32[]{:S(2)}, u32[]{:S(2)}) collective-permute-start(bf16[128,512]{1,0:T(8,128)(2,1)S(1)} %constant_dynamic-slice_fusion.1), channel_id=1, source_target_pairs={{0,3},{1,0},{2,1},{3,2},{4,7},{5,4},{6,5},{7,6},{8,11},{9,8},{10,9... | collective-permute-start | bytes 393224 | tf_op jit(solution)/shard_map/ppermute | solution.py:22
  1.8 10.0 %collective-permute-start.7 = (bf16[128,512]{1,0:T(8,128)(2,1)S(1)}, bf16[128,512]{1,0:T(8,128)(2,1)S(1)}, u32[]{:S(2)}, u32[]{:S(2)}) collective-permute-start(bf16[128,512]{1,0:T(8,128)(2,1)S(1)} %constant_dynamic-slice_fusion.1), channel_id=1, source_target_pairs={{0,2},{1,3},{2,0},{3,1},{4,6},{5,7},{6,4},{7,5},{8,10},{9,11},{10,... | collective-permute-start | bytes 393224 | tf_op jit(solution)/shard_map/ppermute | solution.py:22
  4.1 10.9 %collective-permute-start.6 = (bf16[128,512]{1,0:T(8,128)(2,1)S(1)}, bf16[128,512]{1,0:T(8,128)(2,1)S(1)}, u32[]{:S(2)}, u32[]{:S(2)}) collective-permute-start(bf16[128,512]{1,0:T(8,128)(2,1)S(1)} %constant_dynamic-slice_fusion.1), channel_id=1, source_target_pairs={{0,1},{1,2},{2,3},{3,0},{4,5},{5,6},{6,7},{7,4},{8,9},{9,10},{10,1... | collective-permute-start | bytes 393224 | tf_op jit(solution)/shard_map/ppermute | solution.py:22
  15.1 4.5 %copy-start.4 = (bf16[512,512]{1,0:T(8,128)(2,1)}, bf16[512,512]{1,0:T(8,128)(2,1)S(1)}, u32[]{:S(2)}) copy-start(bf16[512,512]{1,0:T(8,128)(2,1)S(1)} %pad_maximum_fusion.3) | copy-start | bytes 1572868
  15.1 4.5 %collective-permute-start.9 = (bf16[512,512]{1,0:T(8,128)(2,1)S(1)}, bf16[512,512]{1,0:T(8,128)(2,1)S(1)}, u32[]{:S(2)}, u32[]{:S(2)}) collective-permute-start(bf16[512,512]{1,0:T(8,128)(2,1)S(1)} %pad_maximum_fusion.3), channel_id=1, source_target_pairs={{0,16},{1,17},{2,18},{3,19},{4,20},{5,21},{6,22},{7,23},{8,24},{9,... | collective-permute-start | bytes 1572872 | tf_op jit(solution)/shard_map/ppermute | solution.py:22
  17.4 8.2 %collective-permute-start = (bf16[128,1024]{1,0:T(8,128)(2,1)S(1)}, bf16[128,1024]{1,0:T(8,128)(2,1)S(1)}, u32[]{:S(2)}, u32[]{:S(2)}) collective-permute-start(bf16[128,1024]{1,0:T(8,128)(2,1)S(1)} %constant_dynamic-slice_fusion.2), channel_id=1, source_target_pairs={{0,1},{1,2},{2,3},{3,0},{4,5},{5,6},{6,7},{7,4},{8,9},{9,10},{10,1... | collective-permute-start | bytes 786440 | tf_op jit(solution)/shard_map/ppermute | solution.py:22
  19.6 0.8 copy-start.6
  20.6 24.6 %copy-start.2 = (bf16[512,1024]{1,0:T(8,128)(2,1)}, bf16[512,1024]{1,0:T(8,128)(2,1)S(1)}, u32[]{:S(2)}) copy-start(bf16[512,1024]{1,0:T(8,128)(2,1)S(1)} %pad_maximum_fusion.2) | copy-start | bytes 3145732
  20.6 24.5 %collective-permute-start.10 = (bf16[512,1024]{1,0:T(8,128)(2,1)S(1)}, bf16[512,1024]{1,0:T(8,128)(2,1)S(1)}, u32[]{:S(2)}, u32[]{:S(2)}) collective-permute-start(bf16[512,1024]{1,0:T(8,128)(2,1)S(1)} %pad_maximum_fusion.2), channel_id=1, source_target_pairs={{0,4},{1,5},{2,6},{3,7},{4,0},{5,1},{6,2},{7,3},{8,12},{9,13},{10,... | collective-permute-start | bytes 3145736 | tf_op jit(solution)/shard_map/ppermute | solution.py:22
  20.9 21.1 %collective-permute-start.1 = (bf16[128,1024]{1,0:T(8,128)(2,1)S(1)}, bf16[128,1024]{1,0:T(8,128)(2,1)S(1)}, u32[]{:S(2)}, u32[]{:S(2)}) collective-permute-start(bf16[128,1024]{1,0:T(8,128)(2,1)S(1)} %constant_dynamic-slice_fusion.2), channel_id=1, source_target_pairs={{0,2},{1,3},{2,0},{3,1},{4,6},{5,7},{6,4},{7,5},{8,10},{9,11},{10,... | collective-permute-start | bytes 786440 | tf_op jit(solution)/shard_map/ppermute | solution.py:22
  21.8 22.4 %collective-permute-start.2 = (bf16[128,1024]{1,0:T(8,128)(2,1)S(1)}, bf16[128,1024]{1,0:T(8,128)(2,1)S(1)}, u32[]{:S(2)}, u32[]{:S(2)}) collective-permute-start(bf16[128,1024]{1,0:T(8,128)(2,1)S(1)} %constant_dynamic-slice_fusion.2), channel_id=1, source_target_pairs={{0,3},{1,0},{2,1},{3,2},{4,7},{5,4},{6,5},{7,6},{8,11},{9,8},{10,9... | collective-permute-start | bytes 786440 | tf_op jit(solution)/shard_map/ppermute | solution.py:22
  44.9 17.1 %collective-permute-start.4 = (bf16[384,1024]{1,0:T(8,128)(2,1)}, bf16[384,1024]{1,0:T(8,128)(2,1)}, u32[]{:S(2)}, u32[]{:S(2)}) collective-permute-start(bf16[384,1024]{1,0:T(8,128)(2,1)} %constant_dynamic-update-slice_fusion), channel_id=1, source_target_pairs={{0,4},{1,5},{2,6},{3,7},{4,0},{5,1},{6,2},{7,3},{8,12},{9,13},{10,... | collective-permute-start | bytes 2359304 | tf_op jit(solution)/shard_map/ppermute | solution.py:22
  45.2 17.3 %collective-permute-start.12 = (bf16[512,512]{1,0:T(8,128)(2,1)S(1)}, bf16[512,512]{1,0:T(8,128)(2,1)S(1)}, u32[]{:S(2)}, u32[]{:S(2)}) collective-permute-start(bf16[512,512]{1,0:T(8,128)(2,1)S(1)} %slice.36), channel_id=1, source_target_pairs={{0,8},{1,9},{2,10},{3,11},{4,12},{5,13},{6,14},{7,15},{8,0},{9,1},... | collective-permute-start | bytes 1572872 | tf_op jit(solution)/shard_map/ppermute | solution.py:22
  46.6 29.8 %collective-permute-start.11 = (bf16[512,1024]{1,0:T(8,128)(2,1)S(1)}, bf16[512,1024]{1,0:T(8,128)(2,1)S(1)}, u32[]{:S(2)}, u32[]{:S(2)}) collective-permute-start(bf16[512,1024]{1,0:T(8,128)(2,1)S(1)} %collective-permute-done.10), channel_id=1, source_target_pairs={{0,16},{1,17},{2,18},{3,19},{4,20},{5,21},{6,22},{7,23},{8,24},{9,... | collective-permute-start | bytes 3145736 | tf_op jit(solution)/shard_map/ppermute | solution.py:22
  47.5 28.8 %collective-permute-start.3 = (bf16[384,1024]{1,0:T(8,128)(2,1)}, bf16[384,1024]{1,0:T(8,128)(2,1)}, u32[]{:S(2)}, u32[]{:S(2)}) collective-permute-start(bf16[384,1024]{1,0:T(8,128)(2,1)} %constant_dynamic-update-slice_fusion), channel_id=1, source_target_pairs={{0,16},{1,17},{2,18},{3,19},{4,20},{5,21},{6,22},{7,23},{8,24},{9,... | collective-permute-start | bytes 2359304 | tf_op jit(solution)/shard_map/ppermute | solution.py:22
  62.0 14.4 %collective-permute-start.5 = (bf16[384,1024]{1,0:T(8,128)(2,1)}, bf16[384,1024]{1,0:T(8,128)(2,1)}, u32[]{:S(2)}, u32[]{:S(2)}) collective-permute-start(bf16[384,1024]{1,0:T(8,128)(2,1)} %collective-permute-done.4), channel_id=1, source_target_pairs={{0,16},{1,17},{2,18},{3,19},{4,20},{5,21},{6,22},{7,23},{8,24},{9,... | collective-permute-start | bytes 2359304 | tf_op jit(solution)/shard_map/ppermute | solution.py:22
  62.5 13.9 %collective-permute-start.13 = (bf16[512,512]{1,0:T(8,128)(2,1)S(1)}, bf16[512,512]{1,0:T(8,128)(2,1)S(1)}, u32[]{:S(2)}, u32[]{:S(2)}) collective-permute-start(bf16[512,512]{1,0:T(8,128)(2,1)S(1)} %collective-permute-done.12), channel_id=1, source_target_pairs={{0,16},{1,17},{2,18},{3,19},{4,20},{5,21},{6,22},{7,23},{8,24},{9,... | collective-permute-start | bytes 1572872 | tf_op jit(solution)/shard_map/ppermute | solution.py:22
  103.4 16.7 %collective-permute-start.16 = (bf16[512,2048]{1,0:T(8,128)(2,1)}, bf16[512,2048]{1,0:T(8,128)(2,1)}, u32[]{:S(2)}, u32[]{:S(2)}) collective-permute-start(bf16[512,2048]{1,0:T(8,128)(2,1)} %get-tuple-element.359), channel_id=1, source_target_pairs={{0,16},{1,17},{2,18},{3,19},{4,20},{5,21},{6,22},{7,23},{8,24},{9,... | collective-permute-start | bytes 6291464 | tf_op jit(solution)/shard_map/ppermute | solution.py:22
  103.4 16.7 %collective-permute-start.15 = (bf16[512,2048]{1,0:T(8,128)(2,1)}, bf16[512,2048]{1,0:T(8,128)(2,1)}, u32[]{:S(2)}, u32[]{:S(2)}) collective-permute-start(bf16[512,2048]{1,0:T(8,128)(2,1)} %get-tuple-element.358), channel_id=1, source_target_pairs={{0,16},{1,17},{2,18},{3,19},{4,20},{5,21},{6,22},{7,23},{8,24},{9,... | collective-permute-start | bytes 6291464 | tf_op jit(solution)/shard_map/ppermute | solution.py:22
  115.3 14.0 %collective-permute-start.14 = (bf16[512,1536]{1,0:T(8,128)(2,1)}, bf16[512,1536]{1,0:T(8,128)(2,1)}, u32[]{:S(2)}, u32[]{:S(2)}) collective-permute-start(bf16[512,1536]{1,0:T(8,128)(2,1)} %get-tuple-element.357), channel_id=1, source_target_pairs={{0,16},{1,17},{2,18},{3,19},{4,20},{5,21},{6,22},{7,23},{8,24},{9,... | collective-permute-start | bytes 4718600 | tf_op jit(solution)/shard_map/ppermute | solution.py:22
  120.0 1.0 copy-start.8
  121.0 8.2 %copy-start.3 = (bf16[512,1536]{1,0:T(8,128)(2,1)S(1)}, bf16[512,1536]{1,0:T(8,128)(2,1)}, u32[]{:S(2)}) copy-start(bf16[512,1536]{1,0:T(8,128)(2,1)} %get-tuple-element.357) | copy-start | bytes 4718596
  135.6 0.9 copy-start.1

commit v3 on v2

--- a/solution.py
+++ b/solution.py
@@ -142,22 +142,74 @@
     )()
 
 
-def outputs(is_gate, left_slot, left_up, gate, hidden, ups, up_of, first, units, begun):
+def picked(info, blocks):
+    def kernel(info_ref, *refs):
+        for source, out in zip(refs[: len(blocks)], refs[len(blocks) :]):
+            out[...] = source[...]
+
+    shapes = [(array.shape[0], wide) for array, wide, _ in blocks]
+    return pl.pallas_call(
+        kernel,
+        grid_spec=pltpu.PrefetchScalarGridSpec(
+            num_scalar_prefetch=1,
+            grid=(1,),
+            in_specs=[
+                pl.BlockSpec(shape, lambda j, info, which=which: (0, which(info)))
+                for shape, (_, _, which) in zip(shapes, blocks)
+            ],
+            out_specs=[pl.BlockSpec(shape, lambda j, info: (0, 0)) for shape in shapes],
+        ),
+        out_shape=[
+            jax.ShapeDtypeStruct(shape, array.dtype) for shape, (array, _, _) in zip(shapes, blocks)
+        ],
+    )(info, *[array for array, _, _ in blocks])
+
+
+def stacked(arrays):
+    count, wide = arrays[0].shape
+
+    def kernel(*refs):
+        for k, source in enumerate(refs[:-1]):
+            refs[-1][k * count : (k + 1) * count, :] = source[...]
+
+    return pl.pallas_call(
+        kernel,
+        out_shape=jax.ShapeDtypeStruct((len(arrays) * count, wide), arrays[0].dtype),
+    )(*arrays)
+
+
+def outputs(info, is_gate, slot_parts, up_parts, gate, hidden, up_pre, first, units, begun):
     tiles = gate.shape[1] // TILE
     count = gate.shape[0]
-    used = sorted({up_of(first + j)[0] for j in range(tiles)})
-
-    def kernel(a_slot, a_up, gate_ref, hidden_ref, *refs):
-        up_refs = refs[: len(used)]
-        slot_ref, up_ref = refs[-2:]
+    parts = slot_parts + up_parts
+    sources = []
+    for _, _, options in parts:
+        for _, array, _ in options:
+            if not any(array is known for known in sources):
+                sources.append(array)
+
+    def kernel(info_ref, gate_ref, hidden_ref, up_pre_ref, *refs):
+        held = refs[: len(sources)]
+        slot_ref, up_ref, left_slot, left_up, arrived = refs[-5:]
+
+        def copies():
+            for n, (rows, cols, options) in enumerate(parts):
+                target = (left_slot if n < len(slot_parts) else left_up).at[rows, cols]
+                for when, array, taken in options:
+                    ref = next(r for r, known in zip(held, sources) if known is array)
+                    source = ref.at[:, taken(info_ref)]
+                    yield n, when, pltpu.make_async_copy(source, target, arrived.at[n])
+
+        @pl.when(pl.program_id(0) == 0)
+        def _():
+            for _, when, copy in copies():
+                pl.when(when(info_ref))(copy.start)
+            for _, when, copy in copies():
+                pl.when(when(info_ref))(copy.wait)
+
         gate_pre = gate_ref[...].astype(jnp.float32)
         grad_hidden = hidden_ref[...].astype(jnp.float32)
-        up_pre = up_refs[0][...]
-        if len(used) == 2:
-            j = pl.program_id(0) + first
-            early = sum(up_of(first + k)[0] == used[0] for k in range(tiles)) + first
-            up_pre = jnp.where(j < early, up_pre, up_refs[1][...])
-        up_pre = up_pre.astype(jnp.float32)
+        up_pre = up_pre_ref[...].astype(jnp.float32)
         sigmoid_gate = jax.nn.sigmoid(gate_pre)
         silu = gate_pre * sigmoid_gate
         grad_up = (grad_hidden * silu).astype(jnp.bfloat16)
@@ -165,43 +217,41 @@
             right = grad_hidden * up_pre * sigmoid_gate * (1.0 + gate_pre * (1.0 - sigmoid_gate))
         else:
             right = silu * up_pre
-        slot_ref[...] = along_rows(a_slot[...], right.astype(jnp.bfloat16)).astype(jnp.bfloat16)
-        up_ref[...] = along_rows(a_up[...], grad_up).astype(jnp.bfloat16)
-
-    def up_tile(which):
-        own = [k for k in range(tiles) if up_of(first + k)[0] == which]
-        base = up_of(first + own[0])[1] - own[0]
-        return lambda j: (0, jnp.clip(j, own[0], own[-1]) + base)
-
-    whole = lambda j: (0, 0)
-    here = lambda j: (0, j)
-    there = lambda j: (0, j + first)
+        right = right.astype(jnp.bfloat16)
+
+        slot_ref[...] = along_rows(left_slot[...], right).astype(jnp.bfloat16)
+        up_ref[...] = along_rows(left_up[...], grad_up).astype(jnp.bfloat16)
+
+    here = lambda j, info: (0, j)
+    there = lambda j, info: (0, j + first)
     block = (count, TILE)
-    specs = [
-        pl.BlockSpec(left_slot.shape, whole),
-        pl.BlockSpec(left_up.shape, whole),
-        pl.BlockSpec(block, here),
-        pl.BlockSpec(block, here),
-    ] + [pl.BlockSpec(block, up_tile(k)) for k in used]
-    operands = [left_slot, left_up, gate, hidden] + [ups[k] for k in used]
-    rows = (left_slot.shape[1], left_up.shape[1])
+    specs = [pl.BlockSpec(block, here)] * 3 + [pl.BlockSpec(memory_space=pl.ANY)] * len(sources)
+    operands = [gate, hidden, up_pre] + sources
+    slot_rows = max(part[1].stop for part in slot_parts)
+    up_rows = max(part[1].stop for part in up_parts)
+    rows = (slot_rows, up_rows)
     aliases = {}
     if begun is not None:
         specs += [pl.BlockSpec(memory_space=pl.ANY)] * 2
-        aliases = {len(operands): 0, 1 + len(operands): 1}
+        aliases = {1 + len(operands): 0, 2 + len(operands): 1}
         operands += list(begun)
     return pl.pallas_call(
         kernel,
-        grid=(tiles,),
-        in_specs=specs,
-        out_specs=[pl.BlockSpec((r, TILE), there) for r in rows],
+        grid_spec=pltpu.PrefetchScalarGridSpec(
+            num_scalar_prefetch=1,
+            grid=(tiles,),
+            in_specs=specs,
+            out_specs=[pl.BlockSpec((r, TILE), there) for r in rows],
+            scratch_shapes=[pltpu.VMEM((count, r), jnp.bfloat16) for r in rows]
+            + [pltpu.SemaphoreType.DMA((len(parts),))],
+        ),
         out_shape=[jax.ShapeDtypeStruct((r, units), jnp.bfloat16) for r in rows],
         input_output_aliases=aliases,
         compiler_params=pltpu.CompilerParams(vmem_limit_bytes=48 * 1024 * 1024),
         cost_estimate=cost(
-            2 * count * sum(rows) * tiles * TILE, 2 * tiles * TILE * (4 * count + sum(rows))
-        ),
-    )(*operands)
+            2 * count * sum(rows) * tiles * TILE, 2 * tiles * TILE * (3 * count + sum(rows))
+        ),
+    )(info, *operands)
 
 
 def local_by_chip(mesh, tokens, section_weights, up_weight, cotangent):
@@ -239,34 +289,36 @@
         return (s, t ^ (2 - s), d)
 
     steps = range(1, groups)
+
+    def odd(i):
+        return (i[1] ^ (i[1] >> 1)) & 1
+
+    (own_half,) = picked(info, [(tokens, half, lambda i: i[0])])
     parity = (tensor ^ (tensor >> 1)) & 1
-    own_half = columns(tokens, section * half, half)
     own_quarter = columns(cotangent, (2 * parity + section) * quarter, quarter)
 
     mine = jnp.concatenate([own_half] + [moved(own_half, ring(k)) for k in steps], 0)
     theirs = moved(mine, other_section)
-    first_mine = jnp.concatenate([moved(own_quarter, ring(k)) for k in steps], 0)
-    both = jnp.concatenate([mine, theirs], 1)
-    beside = moved(both, near)
+    first_mine = stacked([moved(own_quarter, ring(k)) for k in steps])
+    beside = moved(mine, near)
     beside_too = moved(beside, other_section)
-    across = moved(beside[:, :half], far)
+    below = moved(mine, far)
+    below_too = moved(below, other_section)
+    across = moved(beside, far)
     across_too = moved(across, other_section)
     first_theirs = moved(first_mine, other_section)
     second_mine = moved(first_mine, near)
     second_theirs = moved(second_mine, other_section)
 
-    def odd(i):
-        return (i[1] ^ (i[1] >> 1)) & 1
-
     here = [
-        (both, 0, half, lambda i: 2 * i[1] + i[0]),
-        (both, half, half, lambda i: 2 * i[1] + 1 - i[0]),
+        (mine, 0, half, lambda i: 2 * i[1] + i[0]),
+        (theirs, 0, half, lambda i: 2 * i[1] + 1 - i[0]),
     ]
     rest = [
         (beside, 0, half, lambda i: 2 * (i[1] ^ (1 + i[0])) + i[0]),
-        (beside, half, half, lambda i: 2 * (i[1] ^ (1 + i[0])) + 1 - i[0]),
         (beside_too, 0, half, lambda i: 2 * (i[1] ^ (2 - i[0])) + 1 - i[0]),
-        (beside_too, half, half, lambda i: 2 * (i[1] ^ (2 - i[0])) + i[0]),
+        (below, 0, half, lambda i: 2 * (i[1] ^ (2 - i[0])) + i[0]),
+        (below_too, 0, half, lambda i: 2 * (i[1] ^ (1 + i[0])) + 1 - i[0]),
         (across, 0, half, lambda i: 2 * (i[1] ^ 3) + i[0]),
         (across_too, 0, half, lambda i: 2 * (i[1] ^ 3) + 1 - i[0]),
     ]
@@ -289,12 +341,12 @@
     one = lax.cond(
         is_first,
         lambda: product(info, rest, slot, 0, most, low, start=begun),
-        lambda: product(info, here + rest, up_weight, few, most, low),
+        lambda: product(info, here + rest, up_weight, most, few, low, room=most),
     )
     one_passed = moved(one, other_section)
     two = lax.cond(
         is_first,
-        lambda: product(info, here + rest, up_weight, 0, few, low, room=most),
+        lambda: product(info, here + rest, up_weight, 0, most, low),
         lambda: product(info, cots, slot, 0, most, low, head=own_rows),
     )
     two_passed = moved(two, other_section)
@@ -305,51 +357,51 @@
     )
     three_passed = moved(three, other_section)
 
-    def token_columns(at):
-        chosen = None
-        for array, begin, depth, row in here + rest:
-            piece = array[:, begin : begin + depth]
-            hit = row((section, tensor, group)) == at
-            chosen = piece if chosen is None else jnp.where(hit, piece, chosen)
-        return chosen
-
-    def cotangent_columns(at):
-        chosen = None
-        for array, _, _, row in cots:
-            hit = row((section, tensor, group)) == at
-            chosen = array if chosen is None else jnp.where(hit, array, chosen)
-        return jnp.concatenate([columns(cotangent, at * quarter, quarter), chosen], 0)
-
-    left_slot, left_up = lax.cond(
-        is_first,
-        lambda: (
-            jnp.concatenate([token_columns(2 * group), token_columns(2 * group + 1)], 1),
-            token_columns(group),
-        ),
-        lambda: (cotangent_columns(group), token_columns(groups + group)),
-    )
-
-    def up_of(j):
-        return (0, j) if j < few else (1, j - few)
+    every = slice(0, everyone)
+
+    def token_part(into, at):
+        options = [
+            (
+                lambda i, row=row: row(i) == at(i),
+                array,
+                lambda i, begin=begin: pl.ds(begin, half),
+            )
+            for array, begin, _, row in here + rest
+        ]
+        return (every, slice(into, into + half), options)
+
+    def cotangent_parts():
+        own = (lambda i: True, cotangent, lambda i: pl.ds(pl.multiple_of(i[2] * quarter, quarter), quarter))
+        others = [
+            (lambda i, row=row: row(i) == i[2], array, lambda i: pl.ds(0, quarter))
+            for array, _, _, row in cots
+        ]
+        return [
+            (slice(0, count), slice(0, quarter), [own]),
+            (slice(count, everyone), slice(0, quarter), others),
+        ]
+
+    gate_slot = [token_part(0, lambda i: 2 * i[2]), token_part(half, lambda i: 2 * i[2] + 1)]
+    gate_up = [token_part(0, lambda i: i[2])]
+    down_slot = cotangent_parts()
+    down_up = [token_part(0, lambda i: groups + i[2])]
 
     grads = lax.cond(
         is_first,
         lambda: outputs(
-            True, left_slot, left_up, one, two_passed, (two, one_passed), up_of, 0, units, None
+            info, True, gate_slot, gate_up, one, two_passed, two, 0, units, None
         ),
         lambda: outputs(
-            False, left_slot, left_up, one_passed, two, (two_passed, one), up_of, 0, units, None
+            info, False, down_slot, down_up, one_passed, two, two_passed, 0, units, None
         ),
     )
     slot_sum, up_sum = lax.cond(
         is_first,
         lambda: outputs(
-            True, left_slot, left_up, three, three_passed, (two, one_passed), up_of, most,
-            units, grads,
+            info, True, gate_slot, gate_up, three, three_passed, one_passed, most, units, grads
         ),
         lambda: outputs(
-            False, left_slot, left_up, three_passed, three, (two_passed, one), up_of, most,
-            units, grads,
+            info, False, down_slot, down_up, three_passed, three, one, most, units, grads
         ),
     )
     return (slot_sum[None], up_sum)

time: 138 us -> 143 us (1.036)
  the two profiles are of different devices: /device:TPU:13 before, /device:TPU:0 now
where the time goes in v3:
time: 143 us; the launch traced here: 142 us
  Pallas kernels  68 us (48%)
  waiting for transfers between devices  47.8 us (33%)
  starting transfers between devices  21.2 us (15%)
  local copies, waits for them, and re-layouts  3.19 us (2%)
    ppermute x19, waiting for transfers between devices, sent(): return lax.ppermute(value, AXES, pairs)  47.8 us
    pallas_call x4, Pallas kernels, product(): pl.pallas_call(kernel, grid_spec=pltpu.PrefetchScalarGridSpec(num_scalar_...  45.8 us
    ppermute x19, starting transfers between devices, sent(): return lax.ppermute(value, AXES, pairs)  21.2 us
    pallas_call x2, Pallas kernels, outputs(): pl.pallas_call(kernel, grid_spec=pltpu.PrefetchScalarGridSpec(num_scalar_...  18.1 us
  transfers between devices with their start and end apart: 19, of which 3 were waited for; matrix products, arithmetic and copies ran while one was open for 1% of the time, Pallas kernels for 31%

profile of v3, /device:TPU:0, one launch (start us, length us, event | category | flops | bytes accessed | tf_op | source)
XLA Modules:
  0.0 142.1 jit_solution(8007391856154311067)
XLA Ops:
  0.6 2.1 %shard_map.60 = bf16[128,512]{1,0:T(8,128)(2,1)} custom-call(s32[3]{0:T(128)S(1)} %compare_select_fusion.1.info_ref, bf16[128,1024]{1,0:T(8,128)(2,1)} %refs_0_.1), custom_call_target="tpu_custom_call" | custom-call | tf_op jit(solution)/shard_map/pallas_call | solution.py:151
  2.8 5.1 %collective-permute-start.8 = (bf16[128,512]{1,0:T(8,128)(2,1)}, bf16[128,512]{1,0:T(8,128)(2,1)S(1)}, u32[]{:S(2)}, u32[]{:S(2)}) collective-permute-start(bf16[128,512]{1,0:T(8,128)(2,1)} %shard_map.60), channel_id=1, source_target_pairs={{0,3},{1,0},{2,1},{3,2},{4,7},{5,4},{6,5},{7,6},{8,11},{9,8},{10,9... | collective-permute-start | bytes 393224 | tf_op jit(solution)/shard_map/ppermute | solution.py:22
  9.3 1.6 %collective-permute-start = (bf16[128,1024]{1,0:T(8,128)(2,1)S(1)}, bf16[128,1024]{1,0:T(8,128)(2,1)S(1)}, u32[]{:S(2)}, u32[]{:S(2)}) collective-permute-start(bf16[128,1024]{1,0:T(8,128)(2,1)S(1)} %constant_dynamic-slice_fusion), channel_id=1, source_target_pairs={{0,1},{1,2},{2,3},{3,0},{4,5},{5,6},{6,7},{7,4},{8,9},{9,10},{10,1... | collective-permute-start | bytes 786440 | tf_op jit(solution)/shard_map/ppermute | solution.py:22
  10.9 2.9 %collective-permute-start.7 = (bf16[128,512]{1,0:T(8,128)(2,1)}, bf16[128,512]{1,0:T(8,128)(2,1)S(1)}, u32[]{:S(2)}, u32[]{:S(2)}) collective-permute-start(bf16[128,512]{1,0:T(8,128)(2,1)} %shard_map.60), channel_id=1, source_target_pairs={{0,2},{1,3},{2,0},{3,1},{4,6},{5,7},{6,4},{7,5},{8,10},{9,11},{10,... | collective-permute-start | bytes 393224 | tf_op jit(solution)/shard_map/ppermute | solution.py:22
  13.8 27.8 %collective-permute-done.7 = bf16[128,512]{1,0:T(8,128)(2,1)S(1)} collective-permute-done((bf16[128,512]{1,0:T(8,128)(2,1)}, bf16[128,512]{1,0:T(8,128)(2,1)S(1)}, u32[]{:S(2)}, u32[]{:S(2)}) %collective-permute-start.7) | collective-permute-done | bytes 131104 | tf_op jit(solution)/shard_map/ppermute | solution.py:22
  42.5 1.6 %collective-permute-start.10 = (bf16[512,512]{1,0:T(8,128)(2,1)S(1)}, bf16[512,512]{1,0:T(8,128)(2,1)S(1)}, u32[]{:S(2)}, u32[]{:S(2)}) collective-permute-start(bf16[512,512]{1,0:T(8,128)(2,1)S(1)} %pad_maximum_fusion), channel_id=1, source_target_pairs={{0,4},{1,5},{2,6},{3,7},{4,0},{5,1},{6,2},{7,3},{8,12},{9,13},{10,... | collective-permute-start | bytes 1572872 | tf_op jit(solution)/shard_map/ppermute | solution.py:22
  45.6 2.1 %shard_map.59 = bf16[384,1024]{1,0:T(8,128)(2,1)} custom-call(bf16[128,1024]{1,0:T(8,128)(2,1)} %copy-done.4, bf16[128,1024]{1,0:T(8,128)(2,1)} %copy-done.3, bf16[128,1024]{1,0:T(8,128)(2,1)} %copy-done.2), custom_call_target="tpu_custom_call" | custom-call | tf_op jit(solution)/shard_map/pallas_call | solution.py:175
  49.8 4.6 %collective-permute-done.10 = bf16[512,512]{1,0:T(8,128)(2,1)S(1)} collective-permute-done((bf16[512,512]{1,0:T(8,128)(2,1)S(1)}, bf16[512,512]{1,0:T(8,128)(2,1)S(1)}, u32[]{:S(2)}, u32[]{:S(2)}) %collective-permute-start.10) | collective-permute-done | bytes 524320 | tf_op jit(solution)/shard_map/ppermute | solution.py:22
  54.3 1.6 %collective-permute-start.14 = (bf16[512,512]{1,0:T(8,128)(2,1)S(1)}, bf16[512,512]{1,0:T(8,128)(2,1)S(1)}, u32[]{:S(2)}, u32[]{:S(2)}) collective-permute-start(bf16[512,512]{1,0:T(8,128)(2,1)S(1)} %collective-permute-done.10), channel_id=1, source_target_pairs={{0,8},{1,9},{2,10},{3,11},{4,12},{5,13},{6,14},{7,15},{8,0},{9,1},... | collective-permute-start | bytes 1572872 | tf_op jit(solution)/shard_map/ppermute | solution.py:22
  55.9 15.4 %collective-permute-done.4 = bf16[384,1024]{1,0:T(8,128)(2,1)} collective-permute-done((bf16[384,1024]{1,0:T(8,128)(2,1)}, bf16[384,1024]{1,0:T(8,128)(2,1)}, u32[]{:S(2)}, u32[]{:S(2)}) %collective-permute-start.4) | collective-permute-done | bytes 786464 | tf_op jit(solution)/shard_map/ppermute | solution.py:22
  72.7 10.7 %conditional.6 = (f32[512,3584]{1,0:T(8,128)}, bf16[128,3584]{1,0:T(8,128)(2,1)}) conditional(s32[]{:T(128)} %convert_element_type.2, (s32[3]{0:T(128)S(1)}, bf16[128,4096]{1,0:T(8,128)(2,1)}, bf16[4096,3584]{1,0:T(8,128)(2,1)}) %tuple.76, (s32[3]{0:T(128)S(1)}, bf16[512,512]{1,0:T(8,128)(2,1)}, bf16[512,512]{1,0:T(8,128)(2,1)}, ...), branch_computations={%region_0.1_spmd, %region_1.2_spmd} | conditional | flops 3758096384 | bytes 30277648 | solution.py:333
  72.7 10.7 %branch_1_fun.7 = f32[512,3584]{1,0:T(8,128)} custom-call(s32[3]{0:T(128)S(1)} %get-tuple-element.259.info_ref, bf16[512,512]{1,0:T(8,128)(2,1)} %get-tuple-element.260.refs_0_, bf16[512,512]{1,0:T(8,128)(2,1)} %get-tuple-element.261.refs_1_, bf16[4096,3584]{1,0:T(8,128)(2,1)} %get-tuple-element.262.refs_2_.refs_3_, ...), custom_call_target="tpu_custom_call" | custom-call | flops 3758096384 | bytes 11010048 | tf_op jit(solution)/shard_map/cond/branch_1_fun/pallas_call | solution.py:123
  83.5 13.8 %conditional.9 = (bf16[512,2048]{1,0:T(8,128)(2,1)}) conditional(s32[]{:T(128)} %convert_element_type.2, (s32[3]{0:T(128)S(1)}, bf16[384,1024]{1,0:T(8,128)(2,1)}, bf16[384,1024]{1,0:T(8,128)(2,1)}, bf16[384,1024]{1,0:T(8,128)(2,1)}, bf16[384,1024]{1,0:T(8,128)(2,1)}, /*index=5*/bf16[4096,3584]{1,0:T(8,128)(2,1)}, ...), branch_computations={%region_6.7_spmd, %region_7.8_spmd} | conditional | flops 8589934592 | bytes 18874376 | solution.py:347
  83.5 13.8 %branch_1_fun.11 = bf16[512,2048]{1,0:T(8,128)(2,1)} custom-call(s32[3]{0:T(128)S(1)} %get-tuple-element.305.info_ref, bf16[512,512]{1,0:T(8,128)(2,1)} %get-tuple-element.306.refs_0_, bf16[512,512]{1,0:T(8,128)(2,1)} %get-tuple-element.307.refs_1_, bf16[512,512]{1,0:T(8,128)(2,1)S(1)} %get-tuple-element.308.refs_2_, ...), custom_call_target="tpu_custom_call" | custom-call | flops 8589934592 | bytes 18874368 | tf_op jit(solution)/shard_map/cond/branch_1_fun/pallas_call | solution.py:123
  97.3 3.1 %collective-permute-start.18 = (bf16[512,2048]{1,0:T(8,128)(2,1)}, bf16[512,2048]{1,0:T(8,128)(2,1)}, u32[]{:S(2)}, u32[]{:S(2)}) collective-permute-start(bf16[512,2048]{1,0:T(8,128)(2,1)} %get-tuple-element.442), channel_id=1, source_target_pairs={{0,16},{1,17},{2,18},{3,19},{4,20},{5,21},{6,22},{7,23},{8,24},{9,... | collective-permute-start | bytes 6291464 | tf_op jit(solution)/shard_map/ppermute | solution.py:22
  100.3 11.6 %conditional.8 = (bf16[512,2048]{1,0:T(8,128)(2,1)}) conditional(s32[]{:T(128)} %convert_element_type.2, (s32[3]{0:T(128)S(1)}, bf16[512,512]{1,0:T(8,128)(2,1)}, bf16[512,512]{1,0:T(8,128)(2,1)}, bf16[512,512]{1,0:T(8,128)(2,1)S(1)}, bf16[512,512]{1,0:T(8,128)(2,1)S(1)}, /*index=5*/bf16[512,512]{1,0:T(8,128)(2,1)S(1)}, ...), branch_computations={%region_4.5_spmd, %region_5.6_spmd} | conditional | flops 6442450944 | bytes 14680072 | solution.py:341
  100.3 11.6 %branch_1_fun.10 = bf16[512,2048]{1,0:T(8,128)(2,1)} custom-call(s32[3]{0:T(128)S(1)} %get-tuple-element.289.info_ref, bf16[512,512]{1,0:T(8,128)(2,1)S(1)} %get-tuple-element.290.refs_0_, bf16[512,512]{1,0:T(8,128)(2,1)S(1)} %get-tuple-element.291.refs_1_, bf16[512,512]{1,0:T(8,128)(2,1)S(1)} %get-tuple-element.292.refs_2_, ...), custom_call_target="tpu_custom_call" | custom-call | flops 6442450944 | bytes 14680064 | tf_op jit(solution)/shard_map/cond/branch_1_fun/pallas_call | solution.py:123
  111.9 9.7 %conditional.7 = (bf16[512,1536]{1,0:T(8,128)(2,1)}) conditional(s32[]{:T(128)} %convert_element_type.2, (s32[3]{0:T(128)S(1)}, bf16[384,1024]{1,0:T(8,128)(2,1)}, bf16[384,1024]{1,0:T(8,128)(2,1)}, bf16[384,1024]{1,0:T(8,128)(2,1)}, bf16[384,1024]{1,0:T(8,128)(2,1)}, /*index=5*/bf16[4096,3584]{1,0:T(8,128)(2,1)}, ...), branch_computations={%region_2.3_spmd, %region_3.4_spmd} | conditional | flops 4831838208 | bytes 14155784 | solution.py:353
  112.0 9.6 %branch_1_fun.9 = bf16[512,1536]{1,0:T(8,128)(2,1)} custom-call(s32[3]{0:T(128)S(1)} %get-tuple-element.270.info_ref, bf16[512,512]{1,0:T(8,128)(2,1)S(1)} %get-tuple-element.271.refs_0_, bf16[512,512]{1,0:T(8,128)(2,1)S(1)} %get-tuple-element.272.refs_1_, bf16[512,512]{1,0:T(8,128)(2,1)S(1)} %get-tuple-element.273.refs_2_, ...), custom_call_target="tpu_custom_call" | custom-call | flops 4831838208 | bytes 11010048 | tf_op jit(solution)/shard_map/cond/branch_1_fun/pallas_call | solution.py:123
  121.6 2.2 %collective-permute-start.16 = (bf16[512,1536]{1,0:T(8,128)(2,1)}, bf16[512,1536]{1,0:T(8,128)(2,1)}, u32[]{:S(2)}, u32[]{:S(2)}) collective-permute-start(bf16[512,1536]{1,0:T(8,128)(2,1)} %get-tuple-element.440), channel_id=1, source_target_pairs={{0,16},{1,17},{2,18},{3,19},{4,20},{5,21},{6,22},{7,23},{8,24},{9,... | collective-permute-start | bytes 4718600 | tf_op jit(solution)/shard_map/ppermute | solution.py:22
  123.8 9.7 %conditional.10 = ((bf16[1024,3584]{1,0:T(8,128)(2,1)}, bf16[512,3584]{1,0:T(8,128)(2,1)})) conditional(s32[]{:T(128)} %convert_element_type.2, (s32[3]{0:T(128)S(1)}, bf16[512,2048]{1,0:T(8,128)(2,1)}, bf16[512,2048]{1,0:T(8,128)(2,1)}, bf16[512,2048]{1,0:T(8,128)(2,1)}, bf16[128,4096]{1,0:T(8,128)(2,1)}, /*index=5*/bf16[384,1024]{1,0:T(8,128)(2,1)}, ...), branch_computations={%region_8.9_spmd, %region_9.10_spmd} | conditional | flops 3221225472 | bytes 12582920 | solution.py:389
  123.8 9.7 %branch_1_fun.12 = (bf16[1024,3584]{1,0:T(8,128)(2,1)}, bf16[512,3584]{1,0:T(8,128)(2,1)}) custom-call(s32[3]{0:T(128)S(1)} %get-tuple-element.332.info_ref, bf16[512,2048]{1,0:T(8,128)(2,1)} %get-tuple-element.333.gate_ref, bf16[512,2048]{1,0:T(8,128)(2,1)} %get-tuple-element.334.hidden_ref, bf16[512,2048]{1,0:T(8,128)(2,1)} %get-tuple-element.335.up_pre_ref, ...), custom_call_target="tpu_custom_call" | custom-call | flops 3221225472 | bytes 12582912 | tf_op jit(solution)/shard_map/cond/branch_1_fun/pallas_call | solution.py:238
  133.5 8.4 %conditional.11 = (bf16[512,3584]{1,0:T(8,128)(2,1)}, bf16[1,1024,3584]{2,1,0:T(8,128)(2,1)}) conditional(s32[]{:T(128)} %convert_element_type.2, (s32[3]{0:T(128)S(1)}, bf16[512,1536]{1,0:T(8,128)(2,1)}, bf16[512,1536]{1,0:T(8,128)(2,1)}, bf16[512,2048]{1,0:T(8,128)(2,1)}, bf16[128,4096]{1,0:T(8,128)(2,1)}, ...), branch_computations={%region_10.11_spmd, %region_11.12_spmd} | conditional | flops 2415919104 | bytes 9437200 | solution.py:398
  133.6 8.4 %branch_1_fun.13 = (bf16[1024,3584]{1,0:T(8,128)(2,1)}, bf16[512,3584]{1,0:T(8,128)(2,1)}) custom-call(s32[3]{0:T(128)S(1)} %get-tuple-element.365.info_ref, bf16[512,1536]{1,0:T(8,128)(2,1)} %get-tuple-element.366.gate_ref, bf16[512,1536]{1,0:T(8,128)(2,1)} %get-tuple-element.367.hidden_ref, ...), custom_call_target="tpu_custom_call", output_to_operand_aliasing={{0}: (12, {}), {1}: (13, {})} | custom-call | flops 2415919104 | bytes 9437184 | tf_op jit(solution)/shard_map/cond/branch_1_fun/pallas_call | solution.py:238
  (42 shorter events, 7.4 us)
Async XLA Ops:
  2.8 11.1 %collective-permute-start.8 = (bf16[128,512]{1,0:T(8,128)(2,1)}, bf16[128,512]{1,0:T(8,128)(2,1)S(1)}, u32[]{:S(2)}, u32[]{:S(2)}) collective-permute-start(bf16[128,512]{1,0:T(8,128)(2,1)} %shard_map.60), channel_id=1, source_target_pairs={{0,3},{1,0},{2,1},{3,2},{4,7},{5,4},{6,5},{7,6},{8,11},{9,8},{10,9... | collective-permute-start | bytes 393224 | tf_op jit(solution)/shard_map/ppermute | solution.py:22
  8.8 35.3 %collective-permute-start.2 = (bf16[128,1024]{1,0:T(8,128)(2,1)S(1)}, bf16[128,1024]{1,0:T(8,128)(2,1)S(1)}, u32[]{:S(2)}, u32[]{:S(2)}) collective-permute-start(bf16[128,1024]{1,0:T(8,128)(2,1)S(1)} %constant_dynamic-slice_fusion), channel_id=1, source_target_pairs={{0,3},{1,0},{2,1},{3,2},{4,7},{5,4},{6,5},{7,6},{8,11},{9,8},{10,9... | collective-permute-start | bytes 786440 | tf_op jit(solution)/shard_map/ppermute | solution.py:22
  9.3 34.8 %collective-permute-start.1 = (bf16[128,1024]{1,0:T(8,128)(2,1)S(1)}, bf16[128,1024]{1,0:T(8,128)(2,1)S(1)}, u32[]{:S(2)}, u32[]{:S(2)}) collective-permute-start(bf16[128,1024]{1,0:T(8,128)(2,1)S(1)} %constant_dynamic-slice_fusion), channel_id=1, source_target_pairs={{0,2},{1,3},{2,0},{3,1},{4,6},{5,7},{6,4},{7,5},{8,10},{9,11},{10,... | collective-permute-start | bytes 786440 | tf_op jit(solution)/shard_map/ppermute | solution.py:22
  9.3 34.8 %collective-permute-start = (bf16[128,1024]{1,0:T(8,128)(2,1)S(1)}, bf16[128,1024]{1,0:T(8,128)(2,1)S(1)}, u32[]{:S(2)}, u32[]{:S(2)}) collective-permute-start(bf16[128,1024]{1,0:T(8,128)(2,1)S(1)} %constant_dynamic-slice_fusion), channel_id=1, source_target_pairs={{0,1},{1,2},{2,3},{3,0},{4,5},{5,6},{6,7},{7,4},{8,9},{9,10},{10,1... | collective-permute-start | bytes 786440 | tf_op jit(solution)/shard_map/ppermute | solution.py:22
  10.9 30.7 %collective-permute-start.7 = (bf16[128,512]{1,0:T(8,128)(2,1)}, bf16[128,512]{1,0:T(8,128)(2,1)S(1)}, u32[]{:S(2)}, u32[]{:S(2)}) collective-permute-start(bf16[128,512]{1,0:T(8,128)(2,1)} %shard_map.60), channel_id=1, source_target_pairs={{0,2},{1,3},{2,0},{3,1},{4,6},{5,7},{6,4},{7,5},{8,10},{9,11},{10,... | collective-permute-start | bytes 393224 | tf_op jit(solution)/shard_map/ppermute | solution.py:22
  13.8 27.8 %collective-permute-start.6 = (bf16[128,512]{1,0:T(8,128)(2,1)}, bf16[128,512]{1,0:T(8,128)(2,1)S(1)}, u32[]{:S(2)}, u32[]{:S(2)}) collective-permute-start(bf16[128,512]{1,0:T(8,128)(2,1)} %shard_map.60), channel_id=1, source_target_pairs={{0,1},{1,2},{2,3},{3,0},{4,5},{5,6},{6,7},{7,4},{8,9},{9,10},{10,1... | collective-permute-start | bytes 393224 | tf_op jit(solution)/shard_map/ppermute | solution.py:22
  42.5 29.3 %copy-start = (bf16[512,512]{1,0:T(8,128)(2,1)}, bf16[512,512]{1,0:T(8,128)(2,1)S(1)}, u32[]{:S(2)}) copy-start(bf16[512,512]{1,0:T(8,128)(2,1)S(1)} %pad_maximum_fusion) | copy-start | bytes 1572868
  42.5 11.8 %collective-permute-start.10 = (bf16[512,512]{1,0:T(8,128)(2,1)S(1)}, bf16[512,512]{1,0:T(8,128)(2,1)S(1)}, u32[]{:S(2)}, u32[]{:S(2)}) collective-permute-start(bf16[512,512]{1,0:T(8,128)(2,1)S(1)} %pad_maximum_fusion), channel_id=1, source_target_pairs={{0,4},{1,5},{2,6},{3,7},{4,0},{5,1},{6,2},{7,3},{8,12},{9,13},{10,... | collective-permute-start | bytes 1572872 | tf_op jit(solution)/shard_map/ppermute | solution.py:22
  44.1 0.7 copy-start.2
  44.1 0.8 copy-start.3
  44.9 0.7 copy-start.4
  47.7 23.7 %collective-permute-start.4 = (bf16[384,1024]{1,0:T(8,128)(2,1)}, bf16[384,1024]{1,0:T(8,128)(2,1)}, u32[]{:S(2)}, u32[]{:S(2)}) collective-permute-start(bf16[384,1024]{1,0:T(8,128)(2,1)} %shard_map.59), channel_id=1, source_target_pairs={{0,4},{1,5},{2,6},{3,7},{4,0},{5,1},{6,2},{7,3},{8,12},{9,13},{10,... | collective-permute-start | bytes 2359304 | tf_op jit(solution)/shard_map/ppermute | solution.py:22
  48.2 23.1 %collective-permute-start.12 = (bf16[512,512]{1,0:T(8,128)(2,1)S(1)}, bf16[512,512]{1,0:T(8,128)(2,1)S(1)}, u32[]{:S(2)}, u32[]{:S(2)}) collective-permute-start(bf16[512,512]{1,0:T(8,128)(2,1)S(1)} %pad_maximum_fusion), channel_id=1, source_target_pairs={{0,8},{1,9},{2,10},{3,11},{4,12},{5,13},{6,14},{7,15},{8,0},{9,1},... | collective-permute-start | bytes 1572872 | tf_op jit(solution)/shard_map/ppermute | solution.py:22
  49.8 22.1 %collective-permute-start.9 = (bf16[512,512]{1,0:T(8,128)(2,1)S(1)}, bf16[512,512]{1,0:T(8,128)(2,1)S(1)}, u32[]{:S(2)}, u32[]{:S(2)}) collective-permute-start(bf16[512,512]{1,0:T(8,128)(2,1)S(1)} %pad_maximum_fusion), channel_id=1, source_target_pairs={{0,16},{1,17},{2,18},{3,19},{4,20},{5,21},{6,22},{7,23},{8,24},{9,... | collective-permute-start | bytes 1572872 | tf_op jit(solution)/shard_map/ppermute | solution.py:22
  54.3 17.6 %collective-permute-start.14 = (bf16[512,512]{1,0:T(8,128)(2,1)S(1)}, bf16[512,512]{1,0:T(8,128)(2,1)S(1)}, u32[]{:S(2)}, u32[]{:S(2)}) collective-permute-start(bf16[512,512]{1,0:T(8,128)(2,1)S(1)} %collective-permute-done.10), channel_id=1, source_target_pairs={{0,8},{1,9},{2,10},{3,11},{4,12},{5,13},{6,14},{7,15},{8,0},{9,1},... | collective-permute-start | bytes 1572872 | tf_op jit(solution)/shard_map/ppermute | solution.py:22
  55.9 27.5 %collective-permute-start.3 = (bf16[384,1024]{1,0:T(8,128)(2,1)}, bf16[384,1024]{1,0:T(8,128)(2,1)}, u32[]{:S(2)}, u32[]{:S(2)}) collective-permute-start(bf16[384,1024]{1,0:T(8,128)(2,1)} %shard_map.59), channel_id=1, source_target_pairs={{0,16},{1,17},{2,18},{3,19},{4,20},{5,21},{6,22},{7,23},{8,24},{9,... | collective-permute-start | bytes 2359304 | tf_op jit(solution)/shard_map/ppermute | solution.py:22
  71.3 12.1 %collective-permute-start.5 = (bf16[384,1024]{1,0:T(8,128)(2,1)}, bf16[384,1024]{1,0:T(8,128)(2,1)}, u32[]{:S(2)}, u32[]{:S(2)}) collective-permute-start(bf16[384,1024]{1,0:T(8,128)(2,1)} %collective-permute-done.4), channel_id=1, source_target_pairs={{0,16},{1,17},{2,18},{3,19},{4,20},{5,21},{6,22},{7,23},{8,24},{9,... | collective-permute-start | bytes 2359304 | tf_op jit(solution)/shard_map/ppermute | solution.py:22
  71.3 12.1 %collective-permute-start.11 = (bf16[512,512]{1,0:T(8,128)(2,1)S(1)}, bf16[512,512]{1,0:T(8,128)(2,1)S(1)}, u32[]{:S(2)}, u32[]{:S(2)}) collective-permute-start(bf16[512,512]{1,0:T(8,128)(2,1)S(1)} %collective-permute-done.10), channel_id=1, source_target_pairs={{0,16},{1,17},{2,18},{3,19},{4,20},{5,21},{6,22},{7,23},{8,24},{9,... | collective-permute-start | bytes 1572872 | tf_op jit(solution)/shard_map/ppermute | solution.py:22
  71.8 0.8 copy-start.1
  71.8 11.6 %collective-permute-start.13 = (bf16[512,512]{1,0:T(8,128)(2,1)S(1)}, bf16[512,512]{1,0:T(8,128)(2,1)S(1)}, u32[]{:S(2)}, u32[]{:S(2)}) collective-permute-start(bf16[512,512]{1,0:T(8,128)(2,1)S(1)} %collective-permute-done.12), channel_id=1, source_target_pairs={{0,16},{1,17},{2,18},{3,19},{4,20},{5,21},{6,22},{7,23},{8,24},{9,... | collective-permute-start | bytes 1572872 | tf_op jit(solution)/shard_map/ppermute | solution.py:22
  72.7 10.8 %collective-permute-start.15 = (bf16[512,512]{1,0:T(8,128)(2,1)S(1)}, bf16[512,512]{1,0:T(8,128)(2,1)S(1)}, u32[]{:S(2)}, u32[]{:S(2)}) collective-permute-start(bf16[512,512]{1,0:T(8,128)(2,1)S(1)} %collective-permute-done.14), channel_id=1, source_target_pairs={{0,16},{1,17},{2,18},{3,19},{4,20},{5,21},{6,22},{7,23},{8,24},{9,... | collective-permute-start | bytes 1572872 | tf_op jit(solution)/shard_map/ppermute | solution.py:22
  97.3 26.5 %collective-permute-start.18 = (bf16[512,2048]{1,0:T(8,128)(2,1)}, bf16[512,2048]{1,0:T(8,128)(2,1)}, u32[]{:S(2)}, u32[]{:S(2)}) collective-permute-start(bf16[512,2048]{1,0:T(8,128)(2,1)} %get-tuple-element.442), channel_id=1, source_target_pairs={{0,16},{1,17},{2,18},{3,19},{4,20},{5,21},{6,22},{7,23},{8,24},{9,... | collective-permute-start | bytes 6291464 | tf_op jit(solution)/shard_map/ppermute | solution.py:22
  111.9 11.9 %collective-permute-start.17 = (bf16[512,2048]{1,0:T(8,128)(2,1)}, bf16[512,2048]{1,0:T(8,128)(2,1)}, u32[]{:S(2)}, u32[]{:S(2)}) collective-permute-start(bf16[512,2048]{1,0:T(8,128)(2,1)} %get-tuple-element.441), channel_id=1, source_target_pairs={{0,16},{1,17},{2,18},{3,19},{4,20},{5,21},{6,22},{7,23},{8,24},{9,... | collective-permute-start | bytes 6291464 | tf_op jit(solution)/shard_map/ppermute | solution.py:22
  121.6 11.9 %collective-permute-start.16 = (bf16[512,1536]{1,0:T(8,128)(2,1)}, bf16[512,1536]{1,0:T(8,128)(2,1)}, u32[]{:S(2)}, u32[]{:S(2)}) collective-permute-start(bf16[512,1536]{1,0:T(8,128)(2,1)} %get-tuple-element.440), channel_id=1, source_target_pairs={{0,16},{1,17},{2,18},{3,19},{4,20},{5,21},{6,22},{7,23},{8,24},{9,... | collective-permute-start | bytes 4718600 | tf_op jit(solution)/shard_map/ppermute | solution.py:22

commit v4 on v3

--- a/solution.py
+++ b/solution.py
@@ -84,7 +84,14 @@
     return pl.CostEstimate(flops=int(flops), bytes_accessed=int(moved), transcendentals=0)
 
 
-def product(info, pieces, weight, first_tile, tiles, dtype, start=None, head=None, room=None):
+def product(info, pieces, weight, first_tile, tiles, dtype, start=None, head=None, room=None, parts=None):
+    joined = parts or ([], [])
+    flat = [(n, part) for n in (0, 1) for part in joined[n]]
+    sources = []
+    for _, (_, _, options) in flat:
+        for _, array, _ in options:
+            if not any(array is known for known in sources):
+                sources.append(array)
     arrays = []
     for array, _, _, _ in pieces:
         if not any(array is a for a in arrays):
@@ -92,12 +99,32 @@
     which = [next(i for i, a in enumerate(arrays) if a is array) for array, _, _, _ in pieces]
     count = arrays[0].shape[0]
     above = 0 if head is None else head.shape[0]
+    extras = [x for x in (start, head) if x is not None]
 
     def kernel(info_ref, *refs):
         lefts = refs[: len(arrays)]
         rights = refs[len(arrays) : len(arrays) + len(pieces)]
         rest = list(refs[len(arrays) + len(pieces) :])
-        out = rest.pop()
+        arrived = rest.pop() if parts else None
+        targets = rest[-2:] if parts else []
+        out = rest[-3] if parts else rest[-1]
+        held = rest[len(extras) : len(extras) + len(sources)]
+
+        def copies():
+            for k, (n, (rows, cols, options)) in enumerate(flat):
+                for when, array, taken in options:
+                    ref = next(r for r, known in zip(held, sources) if known is array)
+                    source = ref.at[:, taken(info_ref)]
+                    target = targets[n].at[rows, cols]
+                    yield when, pltpu.make_async_copy(source, target, arrived.at[k])
+
+        if parts:
+
+            @pl.when(pl.program_id(0) == 0)
+            def _():
+                for when, copy in copies():
+                    pl.when(when(info_ref))(copy.start)
+
         total = None
         for (_, begin, depth, _), i, right in zip(pieces, which, rights):
             term = matmul(lefts[i][:, begin : begin + depth], right[...])
@@ -107,6 +134,12 @@
         if head is not None:
             out[:above, :] = rest.pop(0)[...]
         out[above:, :] = total.astype(dtype)
+        if parts:
+
+            @pl.when(pl.program_id(0) == tiles - 1)
+            def _():
+                for when, copy in copies():
+                    pl.when(when(info_ref))(copy.wait)
 
     specs = [pl.BlockSpec(a.shape, lambda j, info: (0, 0)) for a in arrays]
     for _, _, depth, row in pieces:
@@ -116,9 +149,20 @@
     operands = list(arrays) + [weight] * len(pieces)
     for extra in (start, head):
         if extra is not None:
-            specs.append(pl.BlockSpec((extra.shape[0], TILE), lambda j, info: (0, first_tile + j)))
+            specs.append(pl.BlockSpec((extra.shape[0], TILE), lambda j, info: (0, j)))
             operands.append(extra)
+    specs += [pl.BlockSpec(memory_space=pl.ANY)] * len(sources)
+    operands += sources
     out = jax.ShapeDtypeStruct((above + count, (room or tiles) * TILE), dtype)
+    out_spec = pl.BlockSpec((above + count, TILE), lambda j, info: (0, j))
+    outs, out_specs, scratch = out, out_spec, []
+    if parts:
+        shapes = [
+            (max(q[0].stop for q in side), max(q[1].stop for q in side)) for side in joined
+        ]
+        outs = [out] + [jax.ShapeDtypeStruct(shape, jnp.bfloat16) for shape in shapes]
+        out_specs = [out_spec] + [pl.BlockSpec(shape, lambda j, info: (0, 0)) for shape in shapes]
+        scratch = [pltpu.SemaphoreType.DMA((len(flat),))]
     deep = sum(p[2] for p in pieces)
     return pl.pallas_call(
         kernel,
@@ -126,9 +170,10 @@
             num_scalar_prefetch=1,
             grid=(tiles,),
             in_specs=specs,
-            out_specs=pl.BlockSpec((above + count, TILE), lambda j, info: (0, j)),
-        ),
-        out_shape=out,
+            out_specs=out_specs,
+            scratch_shapes=scratch,
+        ),
+        out_shape=outs,
         compiler_params=pltpu.CompilerParams(vmem_limit_bytes=48 * 1024 * 1024),
         cost_estimate=cost(2 * count * deep * tiles * TILE, 2 * deep * tiles * TILE + out.size * 2),
     )(info, *operands)
@@ -178,35 +223,12 @@
     )(*arrays)
 
 
-def outputs(info, is_gate, slot_parts, up_parts, gate, hidden, up_pre, first, units, begun):
+def outputs(info, is_gate, left_slot, left_up, gate, hidden, up_pre, first, units, begun):
     tiles = gate.shape[1] // TILE
     count = gate.shape[0]
-    parts = slot_parts + up_parts
-    sources = []
-    for _, _, options in parts:
-        for _, array, _ in options:
-            if not any(array is known for known in sources):
-                sources.append(array)
-
-    def kernel(info_ref, gate_ref, hidden_ref, up_pre_ref, *refs):
-        held = refs[: len(sources)]
-        slot_ref, up_ref, left_slot, left_up, arrived = refs[-5:]
-
-        def copies():
-            for n, (rows, cols, options) in enumerate(parts):
-                target = (left_slot if n < len(slot_parts) else left_up).at[rows, cols]
-                for when, array, taken in options:
-                    ref = next(r for r, known in zip(held, sources) if known is array)
-                    source = ref.at[:, taken(info_ref)]
-                    yield n, when, pltpu.make_async_copy(source, target, arrived.at[n])
-
-        @pl.when(pl.program_id(0) == 0)
-        def _():
-            for _, when, copy in copies():
-                pl.when(when(info_ref))(copy.start)
-            for _, when, copy in copies():
-                pl.when(when(info_ref))(copy.wait)
-
+
+    def kernel(info_ref, gate_ref, hidden_ref, up_pre_ref, slot_left, up_left, *refs):
+        slot_ref, up_ref = refs[-2:]
         gate_pre = gate_ref[...].astype(jnp.float32)
         grad_hidden = hidden_ref[...].astype(jnp.float32)
         up_pre = up_pre_ref[...].astype(jnp.float32)
@@ -217,19 +239,16 @@
             right = grad_hidden * up_pre * sigmoid_gate * (1.0 + gate_pre * (1.0 - sigmoid_gate))
         else:
             right = silu * up_pre
-        right = right.astype(jnp.bfloat16)
-
-        slot_ref[...] = along_rows(left_slot[...], right).astype(jnp.bfloat16)
-        up_ref[...] = along_rows(left_up[...], grad_up).astype(jnp.bfloat16)
+        slot_ref[...] = along_rows(slot_left[...], right.astype(jnp.bfloat16)).astype(jnp.bfloat16)
+        up_ref[...] = along_rows(up_left[...], grad_up).astype(jnp.bfloat16)
 
     here = lambda j, info: (0, j)
     there = lambda j, info: (0, j + first)
     block = (count, TILE)
-    specs = [pl.BlockSpec(block, here)] * 3 + [pl.BlockSpec(memory_space=pl.ANY)] * len(sources)
-    operands = [gate, hidden, up_pre] + sources
-    slot_rows = max(part[1].stop for part in slot_parts)
-    up_rows = max(part[1].stop for part in up_parts)
-    rows = (slot_rows, up_rows)
+    specs = [pl.BlockSpec(block, here)] * 3
+    specs += [pl.BlockSpec(left.shape, lambda j, info: (0, 0)) for left in (left_slot, left_up)]
+    operands = [gate, hidden, up_pre, left_slot, left_up]
+    rows = (left_slot.shape[1], left_up.shape[1])
     aliases = {}
     if begun is not None:
         specs += [pl.BlockSpec(memory_space=pl.ANY)] * 2
@@ -242,8 +261,6 @@
             grid=(tiles,),
             in_specs=specs,
             out_specs=[pl.BlockSpec((r, TILE), there) for r in rows],
-            scratch_shapes=[pltpu.VMEM((count, r), jnp.bfloat16) for r in rows]
-            + [pltpu.SemaphoreType.DMA((len(parts),))],
         ),
         out_shape=[jax.ShapeDtypeStruct((r, units), jnp.bfloat16) for r in rows],
         input_output_aliases=aliases,
@@ -293,9 +310,10 @@
     def odd(i):
         return (i[1] ^ (i[1] >> 1)) & 1
 
-    (own_half,) = picked(info, [(tokens, half, lambda i: i[0])])
-    parity = (tensor ^ (tensor >> 1)) & 1
-    own_quarter = columns(cotangent, (2 * parity + section) * quarter, quarter)
+    own_half, own_quarter = picked(
+        info,
+        [(tokens, half, lambda i: i[0]), (cotangent, quarter, lambda i: 2 * odd(i) + i[0])],
+    )
 
     mine = jnp.concatenate([own_half] + [moved(own_half, ring(k)) for k in steps], 0)
     theirs = moved(mine, other_section)
@@ -330,13 +348,18 @@
     ]
     whole = [(cotangent, 0, width, lambda i: 0)]
 
-    begun, own_rows = lax.cond(
-        is_first,
-        lambda: (
-            product(info, here, slot, 0, tiles, jnp.float32),
-            unset((count, units), low),
-        ),
-        lambda: (unset((everyone, units), jnp.float32), product(info, whole, slot, 0, tiles, low)),
+    def own_rows(begin, many):
+        return product(info, whole, slot, begin, many, low)
+
+    own_high = lax.cond(
+        is_first,
+        lambda: unset((count, few * TILE), low),
+        lambda: own_rows(most, few),
+    )
+    begun, own_low = lax.cond(
+        is_first,
+        lambda: (product(info, here, slot, 0, most, jnp.float32), unset((count, most * TILE), low)),
+        lambda: (unset((everyone, most * TILE), jnp.float32), own_rows(0, most)),
     )
     one = lax.cond(
         is_first,
@@ -347,16 +370,9 @@
     two = lax.cond(
         is_first,
         lambda: product(info, here + rest, up_weight, 0, most, low),
-        lambda: product(info, cots, slot, 0, most, low, head=own_rows),
+        lambda: product(info, cots, slot, 0, most, low, head=own_low),
     )
     two_passed = moved(two, other_section)
-    three = lax.cond(
-        is_first,
-        lambda: product(info, rest, slot, most, few, low, start=begun),
-        lambda: product(info, cots, slot, most, few, low, head=own_rows),
-    )
-    three_passed = moved(three, other_section)
-
     every = slice(0, everyone)
 
     def token_part(into, at):
@@ -386,22 +402,37 @@
     down_slot = cotangent_parts()
     down_up = [token_part(0, lambda i: groups + i[2])]
 
+    three, left_slot, left_up = lax.cond(
+        is_first,
+        lambda: tuple(
+            product(
+                info, here + rest, slot, most, few, low, parts=(gate_slot, gate_up)
+            )
+        ),
+        lambda: tuple(
+            product(
+                info, cots, slot, most, few, low, head=own_high, parts=(down_slot, down_up)
+            )
+        ),
+    )
+    three_passed = moved(three, other_section)
+
     grads = lax.cond(
         is_first,
         lambda: outputs(
-            info, True, gate_slot, gate_up, one, two_passed, two, 0, units, None
+            info, True, left_slot, left_up, one, two_passed, two, 0, units, None
         ),
         lambda: outputs(
-            info, False, down_slot, down_up, one_passed, two, two_passed, 0, units, None
+            info, False, left_slot, left_up, one_passed, two, two_passed, 0, units, None
         ),
     )
     slot_sum, up_sum = lax.cond(
         is_first,
         lambda: outputs(
-            info, True, gate_slot, gate_up, three, three_passed, one_passed, most, units, grads
+            info, True, left_slot, left_up, three, three_passed, one_passed, most, units, grads
         ),
         lambda: outputs(
-            info, False, down_slot, down_up, three_passed, three, one, most, units, grads
+            info, False, left_slot, left_up, three_passed, three, one, most, units, grads
         ),
     )
     return (slot_sum[None], up_sum)

time: 143 us -> 136 us (0.951)
  the two profiles are of different devices: /device:TPU:0 before, /device:TPU:13 now
where the time goes in v4:
time: 136 us
  Pallas kernels  71.4 us (53%)
  waiting for transfers between devices  45.1 us (33%)
  starting transfers between devices  16.3 us (12%)
  local copies, waits for them, and re-layouts  1.68 us (1%)
    pallas_call x5, Pallas kernels, product(): pl.pallas_call(kernel, grid_spec=pltpu.PrefetchScalarGridSpec(num_scalar_...  51.9 us
    ppermute x19, waiting for transfers between devices, sent(): return lax.ppermute(value, AXES, pairs)  45.1 us
    ppermute x19, starting transfers between devices, sent(): return lax.ppermute(value, AXES, pairs)  16.3 us
    pallas_call x2, Pallas kernels, outputs(): pl.pallas_call(kernel, grid_spec=pltpu.PrefetchScalarGridSpec(num_scalar_...  15.2 us
  transfers between devices with their start and end apart: 19, of which 7 were waited for; matrix products, arithmetic and copies ran while one was open for 1% of the time, Pallas kernels for 36%

profile of v4, /device:TPU:13, one launch (start us, length us, event | category | flops | bytes accessed | tf_op | source)
XLA Modules:
  0.0 135.6 jit_solution(11047281644404515531)
XLA Ops:
  0.6 2.3 %shard_map.59 = (bf16[128,512]{1,0:T(8,128)(2,1)}, bf16[128,1024]{1,0:T(8,128)(2,1)}) custom-call(s32[3]{0:T(128)S(1)} %compare_select_fusion.1.info_ref, bf16[128,1024]{1,0:T(8,128)(2,1)} %refs_0_.1, bf16[128,4096]{1,0:T(8,128)(2,1)} %refs_1_.1), custom_call_target="tpu_custom_call" | custom-call | tf_op jit(solution)/shard_map/pallas_call | solution.py:196
  6.7 3.1 %collective-permute-start.1 = (bf16[128,1024]{1,0:T(8,128)(2,1)}, bf16[128,1024]{1,0:T(8,128)(2,1)S(1)}, u32[]{:S(2)}, u32[]{:S(2)}) collective-permute-start(bf16[128,1024]{1,0:T(8,128)(2,1)} %get-tuple-element.331), channel_id=1, source_target_pairs={{0,2},{1,3},{2,0},{3,1},{4,6},{5,7},{6,4},{7,5},{8,10},{9,11},{10,... | collective-permute-start | bytes 786440 | tf_op jit(solution)/shard_map/ppermute | solution.py:22
  10.9 4.3 %collective-permute-done.7 = bf16[128,512]{1,0:T(8,128)(2,1)S(1)} collective-permute-done((bf16[128,512]{1,0:T(8,128)(2,1)}, bf16[128,512]{1,0:T(8,128)(2,1)S(1)}, u32[]{:S(2)}, u32[]{:S(2)}) %collective-permute-start.7) | collective-permute-done | bytes 131104 | tf_op jit(solution)/shard_map/ppermute | solution.py:22
  15.2 13.9 %collective-permute-done.8 = bf16[128,512]{1,0:T(8,128)(2,1)S(1)} collective-permute-done((bf16[128,512]{1,0:T(8,128)(2,1)}, bf16[128,512]{1,0:T(8,128)(2,1)S(1)}, u32[]{:S(2)}, u32[]{:S(2)}) %collective-permute-start.8) | collective-permute-done | bytes 131104 | tf_op jit(solution)/shard_map/ppermute | solution.py:22
  29.5 2.6 %collective-permute-done.refs_0_ = bf16[128,1024]{1,0:T(8,128)(2,1)S(1)} collective-permute-done((bf16[128,1024]{1,0:T(8,128)(2,1)}, bf16[128,1024]{1,0:T(8,128)(2,1)S(1)}, u32[]{:S(2)}, u32[]{:S(2)}) %collective-permute-start) | collective-permute-done | bytes 262176 | tf_op jit(solution)/shard_map/ppermute | solution.py:22
  32.1 5.6 %collective-permute-done.1.refs_1_ = bf16[128,1024]{1,0:T(8,128)(2,1)S(1)} collective-permute-done((bf16[128,1024]{1,0:T(8,128)(2,1)}, bf16[128,1024]{1,0:T(8,128)(2,1)S(1)}, u32[]{:S(2)}, u32[]{:S(2)}) %collective-permute-start.1) | collective-permute-done | bytes 262176 | tf_op jit(solution)/shard_map/ppermute | solution.py:22
  37.7 2.7 %collective-permute-done.2.refs_2_ = bf16[128,1024]{1,0:T(8,128)(2,1)S(1)} collective-permute-done((bf16[128,1024]{1,0:T(8,128)(2,1)}, bf16[128,1024]{1,0:T(8,128)(2,1)S(1)}, u32[]{:S(2)}, u32[]{:S(2)}) %collective-permute-start.2) | collective-permute-done | bytes 262176 | tf_op jit(solution)/shard_map/ppermute | solution.py:22
  47.2 13.6 %collective-permute-done.4 = bf16[384,1024]{1,0:T(8,128)(2,1)} collective-permute-done((bf16[384,1024]{1,0:T(8,128)(2,1)}, bf16[384,1024]{1,0:T(8,128)(2,1)}, u32[]{:S(2)}, u32[]{:S(2)}) %collective-permute-start.4) | collective-permute-done | bytes 786464 | tf_op jit(solution)/shard_map/ppermute | solution.py:22
  60.8 2.8 %collective-permute-start.5 = (bf16[384,1024]{1,0:T(8,128)(2,1)}, bf16[384,1024]{1,0:T(8,128)(2,1)}, u32[]{:S(2)}, u32[]{:S(2)}) collective-permute-start(bf16[384,1024]{1,0:T(8,128)(2,1)} %collective-permute-done.4), channel_id=1, source_target_pairs={{0,16},{1,17},{2,18},{3,19},{4,20},{5,21},{6,22},{7,23},{8,24},{9,... | collective-permute-start | bytes 2359304 | tf_op jit(solution)/shard_map/ppermute | solution.py:22
  64.1 2.3 %collective-permute-done.14 = bf16[512,512]{1,0:T(8,128)(2,1)S(1)} collective-permute-done((bf16[512,512]{1,0:T(8,128)(2,1)S(1)}, bf16[512,512]{1,0:T(8,128)(2,1)S(1)}, u32[]{:S(2)}, u32[]{:S(2)}) %collective-permute-start.14) | collective-permute-done | bytes 524320 | tf_op jit(solution)/shard_map/ppermute | solution.py:22
  66.4 8.9 %conditional.9 = (f32[512,2048]{1,0:T(8,128)}, bf16[128,2048]{1,0:T(8,128)(2,1)}) conditional(s32[]{:T(128)} %convert_element_type.2, (s32[3]{0:T(128)S(1)}, bf16[128,4096]{1,0:T(8,128)(2,1)}, bf16[4096,3584]{1,0:T(8,128)(2,1)}) %tuple.89, (s32[3]{0:T(128)S(1)}, bf16[512,512]{1,0:T(8,128)(2,1)S(1)}, bf16[512,512]{1,0:T(8,128)(2,1)S(1)}, ...), branch_computations={%region_4.5_spmd, %region_5.6_spmd} | conditional | flops 2147483648 | bytes 17301520 | solution.py:359
  66.4 8.9 %branch_0_fun.11 = bf16[128,2048]{1,0:T(8,128)(2,1)} custom-call(s32[3]{0:T(128)S(1)} %get-tuple-element.243.info_ref, bf16[128,4096]{1,0:T(8,128)(2,1)} %get-tuple-element.244.refs_0_, bf16[4096,3584]{1,0:T(8,128)(2,1)} %get-tuple-element.245.refs_1_), custom_call_target="tpu_custom_call" | custom-call | flops 2147483648 | bytes 17301504 | tf_op jit(solution)/shard_map/cond/branch_0_fun/pallas_call | solution.py:167
  75.4 13.3 %conditional.11 = (bf16[512,2048]{1,0:T(8,128)(2,1)}) conditional(s32[]{:T(128)} %convert_element_type.2, (s32[3]{0:T(128)S(1)}, bf16[384,1024]{1,0:T(8,128)(2,1)}, bf16[384,1024]{1,0:T(8,128)(2,1)}, bf16[384,1024]{1,0:T(8,128)(2,1)}, bf16[384,1024]{1,0:T(8,128)(2,1)}, /*index=5*/bf16[4096,3584]{1,0:T(8,128)(2,1)}, ...), branch_computations={%region_8.9_spmd, %region_9.10_spmd} | conditional | flops 8589934592 | bytes 18874376 | solution.py:370
  75.4 13.3 %branch_0_fun.13 = bf16[512,2048]{1,0:T(8,128)(2,1)} custom-call(s32[3]{0:T(128)S(1)} %get-tuple-element.269.info_ref, bf16[384,1024]{1,0:T(8,128)(2,1)} %get-tuple-element.270.refs_0_, bf16[384,1024]{1,0:T(8,128)(2,1)} %get-tuple-element.271.refs_1_, bf16[384,1024]{1,0:T(8,128)(2,1)} %get-tuple-element.272.refs_2_, ...), custom_call_target="tpu_custom_call" | custom-call | flops 6442450944 | bytes 18874368 | tf_op jit(solution)/shard_map/cond/branch_0_fun/pallas_call | solution.py:167
  88.7 11.3 %conditional.10 = (bf16[512,2048]{1,0:T(8,128)(2,1)}) conditional(s32[]{:T(128)} %convert_element_type.2, (s32[3]{0:T(128)S(1)}, bf16[512,512]{1,0:T(8,128)(2,1)S(1)}, bf16[512,512]{1,0:T(8,128)(2,1)S(1)}, bf16[512,512]{1,0:T(8,128)(2,1)S(1)}, bf16[512,512]{1,0:T(8,128)(2,1)S(1)}, /*index=5*/bf16[512,512]{1,0:T(8,128)(2,1)S(1)}, ...), branch_computations={%region_6.7_spmd, %region_7.8_spmd} | conditional | flops 6442450944 | bytes 14680072 | solution.py:364
  88.7 11.2 %branch_0_fun.12 = bf16[512,2048]{1,0:T(8,128)(2,1)} custom-call(s32[3]{0:T(128)S(1)} %get-tuple-element.250.info_ref, bf16[512,512]{1,0:T(8,128)(2,1)S(1)} %get-tuple-element.251.refs_0_, bf16[512,512]{1,0:T(8,128)(2,1)S(1)} %get-tuple-element.252.refs_1_, bf16[512,512]{1,0:T(8,128)(2,1)S(1)} %get-tuple-element.253.refs_2_, ...), custom_call_target="tpu_custom_call" | custom-call | flops 6442450944 | bytes 14680064 | tf_op jit(solution)/shard_map/cond/branch_0_fun/pallas_call | solution.py:167
  101.6 6.9 %conditional.7 = (bf16[128,1536]{1,0:T(8,128)(2,1)S(1)}) conditional(s32[]{:T(128)} %convert_element_type.2, (s32[3]{0:T(128)S(1)}, bf16[128,4096]{1,0:T(8,128)(2,1)}, bf16[4096,3584]{1,0:T(8,128)(2,1)}) %tuple.93, () %tuple.57), branch_computations={%region_0.1_spmd, %region_1.2_spmd} | conditional | flops 1610612736 | bytes 12976136 | solution.py:354
  101.6 6.9 %branch_0_fun.8 = bf16[128,1536]{1,0:T(8,128)(2,1)S(1)} custom-call(s32[3]{0:T(128)S(1)} %get-tuple-element.214.info_ref, bf16[128,4096]{1,0:T(8,128)(2,1)} %get-tuple-element.215.refs_0_, bf16[4096,3584]{1,0:T(8,128)(2,1)} %get-tuple-element.216.refs_1_), custom_call_target="tpu_custom_call" | custom-call | flops 1610612736 | bytes 12976128 | tf_op jit(solution)/shard_map/cond/branch_0_fun/pallas_call | solution.py:167
  108.5 11.5 %conditional.8 = ((bf16[512,1536]{1,0:T(8,128)(2,1)}, bf16[512,1024]{1,0:T(8,128)(2,1)}, bf16[512,512]{1,0:T(8,128)(2,1)})) conditional(s32[]{:T(128)} %convert_element_type.2, (s32[3]{0:T(128)S(1)}, bf16[384,1024]{1,0:T(8,128)(2,1)}, bf16[384,1024]{1,0:T(8,128)(2,1)}, bf16[384,1024]{1,0:T(8,128)(2,1)}, bf16[384,1024]{1,0:T(8,128)(2,1)}, ...), branch_computations={%region_2.3_spmd, %region_3.4_spmd} | conditional | flops 6442450944 | bytes 14155784 | solution.py:405
  108.5 11.5 %branch_0_fun.9 = (bf16[512,1536]{1,0:T(8,128)(2,1)}, bf16[512,1024]{1,0:T(8,128)(2,1)}, bf16[512,512]{1,0:T(8,128)(2,1)}) custom-call(s32[3]{0:T(128)S(1)} %get-tuple-element.217.info_ref, bf16[384,1024]{1,0:T(8,128)(2,1)} %get-tuple-element.218.refs_0_.refs_10_, bf16[384,1024]{1,0:T(8,128)(2,1)} %get-tuple-element.219.refs_1_.refs_11_, ...), custom_call_target="tpu_custom_call" | custom-call | flops 4831838208 | bytes 14155776 | tf_op jit(solution)/shard_map/cond/branch_0_fun/pallas_call | solution.py:167
  120.1 8.8 %conditional.12 = ((bf16[1024,3584]{1,0:T(8,128)(2,1)}, bf16[512,3584]{1,0:T(8,128)(2,1)})) conditional(s32[]{:T(128)} %convert_element_type.2, (s32[3]{0:T(128)S(1)}, bf16[512,2048]{1,0:T(8,128)(2,1)}, bf16[512,2048]{1,0:T(8,128)(2,1)}, bf16[512,2048]{1,0:T(8,128)(2,1)}, bf16[512,1024]{1,0:T(8,128)(2,1)}, ...), branch_computations={%region_10.11_spmd, %region_11.12_spmd} | conditional | flops 3221225472 | bytes 12582920 | solution.py:420
  120.3 8.6 %branch_0_fun.14 = (bf16[1024,3584]{1,0:T(8,128)(2,1)}, bf16[512,3584]{1,0:T(8,128)(2,1)}) custom-call(s32[3]{0:T(128)S(1)} %get-tuple-element.286.info_ref, bf16[512,2048]{1,0:T(8,128)(2,1)} %get-tuple-element.287.gate_ref, bf16[512,2048]{1,0:T(8,128)(2,1)} %get-tuple-element.288.hidden_ref, bf16[512,2048]{1,0:T(8,128)(2,1)} %get-tuple-element.289.up_pre_ref, ...), custom_call_target="tpu_custom_call" | custom-call | flops 3221225472 | bytes 12582912 | tf_op jit(solution)/shard_map/cond/branch_0_fun/pallas_call | solution.py:257
  129.0 6.6 %conditional.13 = (bf16[512,3584]{1,0:T(8,128)(2,1)}, bf16[1,1024,3584]{2,1,0:T(8,128)(2,1)}) conditional(s32[]{:T(128)} %convert_element_type.2, (s32[3]{0:T(128)S(1)}, bf16[512,1536]{1,0:T(8,128)(2,1)S(1)}, bf16[512,1536]{1,0:T(8,128)(2,1)S(1)}, bf16[512,2048]{1,0:T(8,128)(2,1)}, bf16[512,1024]{1,0:T(8,128)(2,1)}, ...), branch_computations={%region_12.13_spmd, %region_13.14_spmd} | conditional | flops 2415919104 | bytes 9437200 | solution.py:429
  129.0 6.6 %branch_0_fun.15 = (bf16[1024,3584]{1,0:T(8,128)(2,1)}, bf16[512,3584]{1,0:T(8,128)(2,1)}) custom-call(s32[3]{0:T(128)S(1)} %get-tuple-element.298.info_ref, bf16[512,1536]{1,0:T(8,128)(2,1)S(1)} %get-tuple-element.299.gate_ref, bf16[512,1536]{1,0:T(8,128)(2,1)S(1)} %get-tuple-element.300.hidden_ref, ...), custom_call_target="tpu_custom_call", output_to_operand_aliasing={{0}: (6, {}), {1}: (7, {})} | custom-call | flops 2415919104 | bytes 9437184 | tf_op jit(solution)/shard_map/cond/branch_0_fun/pallas_call | solution.py:257
  (44 shorter events, 14.1 us)
Async XLA Ops:
  3.0 7.8 %collective-permute-start.6 = (bf16[128,512]{1,0:T(8,128)(2,1)}, bf16[128,512]{1,0:T(8,128)(2,1)S(1)}, u32[]{:S(2)}, u32[]{:S(2)}) collective-permute-start(bf16[128,512]{1,0:T(8,128)(2,1)} %get-tuple-element.332), channel_id=1, source_target_pairs={{0,1},{1,2},{2,3},{3,0},{4,5},{5,6},{6,7},{7,4},{8,9},{9,10},{10,1... | collective-permute-start | bytes 393224 | tf_op jit(solution)/shard_map/ppermute | solution.py:22
  4.3 11.0 %collective-permute-start.7 = (bf16[128,512]{1,0:T(8,128)(2,1)}, bf16[128,512]{1,0:T(8,128)(2,1)S(1)}, u32[]{:S(2)}, u32[]{:S(2)}) collective-permute-start(bf16[128,512]{1,0:T(8,128)(2,1)} %get-tuple-element.332), channel_id=1, source_target_pairs={{0,2},{1,3},{2,0},{3,1},{4,6},{5,7},{6,4},{7,5},{8,10},{9,11},{10,... | collective-permute-start | bytes 393224 | tf_op jit(solution)/shard_map/ppermute | solution.py:22
  5.3 23.9 %collective-permute-start.8 = (bf16[128,512]{1,0:T(8,128)(2,1)}, bf16[128,512]{1,0:T(8,128)(2,1)S(1)}, u32[]{:S(2)}, u32[]{:S(2)}) collective-permute-start(bf16[128,512]{1,0:T(8,128)(2,1)} %get-tuple-element.332), channel_id=1, source_target_pairs={{0,3},{1,0},{2,1},{3,2},{4,7},{5,4},{6,5},{7,6},{8,11},{9,8},{10,9... | collective-permute-start | bytes 393224 | tf_op jit(solution)/shard_map/ppermute | solution.py:22
  6.7 25.3 %collective-permute-start = (bf16[128,1024]{1,0:T(8,128)(2,1)}, bf16[128,1024]{1,0:T(8,128)(2,1)S(1)}, u32[]{:S(2)}, u32[]{:S(2)}) collective-permute-start(bf16[128,1024]{1,0:T(8,128)(2,1)} %get-tuple-element.331), channel_id=1, source_target_pairs={{0,1},{1,2},{2,3},{3,0},{4,5},{5,6},{6,7},{7,4},{8,9},{9,10},{10,1... | collective-permute-start | bytes 786440 | tf_op jit(solution)/shard_map/ppermute | solution.py:22
  6.7 31.0 %collective-permute-start.1 = (bf16[128,1024]{1,0:T(8,128)(2,1)}, bf16[128,1024]{1,0:T(8,128)(2,1)S(1)}, u32[]{:S(2)}, u32[]{:S(2)}) collective-permute-start(bf16[128,1024]{1,0:T(8,128)(2,1)} %get-tuple-element.331), channel_id=1, source_target_pairs={{0,2},{1,3},{2,0},{3,1},{4,6},{5,7},{6,4},{7,5},{8,10},{9,11},{10,... | collective-permute-start | bytes 786440 | tf_op jit(solution)/shard_map/ppermute | solution.py:22
  10.8 29.6 %collective-permute-start.2 = (bf16[128,1024]{1,0:T(8,128)(2,1)}, bf16[128,1024]{1,0:T(8,128)(2,1)S(1)}, u32[]{:S(2)}, u32[]{:S(2)}) collective-permute-start(bf16[128,1024]{1,0:T(8,128)(2,1)} %get-tuple-element.331), channel_id=1, source_target_pairs={{0,3},{1,0},{2,1},{3,2},{4,7},{5,4},{6,5},{7,6},{8,11},{9,8},{10,9... | collective-permute-start | bytes 786440 | tf_op jit(solution)/shard_map/ppermute | solution.py:22
  29.2 16.2 %collective-permute-start.10 = (bf16[512,512]{1,0:T(8,128)(2,1)S(1)}, bf16[512,512]{1,0:T(8,128)(2,1)S(1)}, u32[]{:S(2)}, u32[]{:S(2)}) collective-permute-start(bf16[512,512]{1,0:T(8,128)(2,1)S(1)} %constant_dynamic-update-slice_fusion), channel_id=1, source_target_pairs={{0,4},{1,5},{2,6},{3,7},{4,0},{5,1},{6,2},{7,3},{8,12},{9,13},{10,... | collective-permute-start | bytes 1572872 | tf_op jit(solution)/shard_map/ppermute | solution.py:22
  32.1 8.3 %copy-start.1 = (bf16[128,1024]{1,0:T(8,128)(2,1)}, bf16[128,1024]{1,0:T(8,128)(2,1)S(1)}, u32[]{:S(2)}) copy-start(bf16[128,1024]{1,0:T(8,128)(2,1)S(1)} %collective-permute-done.refs_0_) | copy-start | bytes 786436
  37.7 2.7 %copy-start.2 = (bf16[128,1024]{1,0:T(8,128)(2,1)}, bf16[128,1024]{1,0:T(8,128)(2,1)S(1)}, u32[]{:S(2)}) copy-start(bf16[128,1024]{1,0:T(8,128)(2,1)S(1)} %collective-permute-done.1.refs_1_) | copy-start | bytes 786436
  40.4 0.7 copy-start.3
  43.1 17.6 %collective-permute-start.4 = (bf16[384,1024]{1,0:T(8,128)(2,1)}, bf16[384,1024]{1,0:T(8,128)(2,1)}, u32[]{:S(2)}, u32[]{:S(2)}) collective-permute-start(bf16[384,1024]{1,0:T(8,128)(2,1)} %shard_map.60), channel_id=1, source_target_pairs={{0,4},{1,5},{2,6},{3,7},{4,0},{5,1},{6,2},{7,3},{8,12},{9,13},{10,... | collective-permute-start | bytes 2359304 | tf_op jit(solution)/shard_map/ppermute | solution.py:22
  43.4 20.2 %collective-permute-start.9 = (bf16[512,512]{1,0:T(8,128)(2,1)S(1)}, bf16[512,512]{1,0:T(8,128)(2,1)S(1)}, u32[]{:S(2)}, u32[]{:S(2)}) collective-permute-start(bf16[512,512]{1,0:T(8,128)(2,1)S(1)} %constant_dynamic-update-slice_fusion), channel_id=1, source_target_pairs={{0,16},{1,17},{2,18},{3,19},{4,20},{5,21},{6,22},{7,23},{8,24},{9,... | collective-permute-start | bytes 1572872 | tf_op jit(solution)/shard_map/ppermute | solution.py:22
  45.1 18.4 %collective-permute-start.12 = (bf16[512,512]{1,0:T(8,128)(2,1)S(1)}, bf16[512,512]{1,0:T(8,128)(2,1)S(1)}, u32[]{:S(2)}, u32[]{:S(2)}) collective-permute-start(bf16[512,512]{1,0:T(8,128)(2,1)S(1)} %constant_dynamic-update-slice_fusion), channel_id=1, source_target_pairs={{0,8},{1,9},{2,10},{3,11},{4,12},{5,13},{6,14},{7,15},{8,0},{9,1},... | collective-permute-start | bytes 1572872 | tf_op jit(solution)/shard_map/ppermute | solution.py:22
  45.4 21.0 %collective-permute-start.14 = (bf16[512,512]{1,0:T(8,128)(2,1)S(1)}, bf16[512,512]{1,0:T(8,128)(2,1)S(1)}, u32[]{:S(2)}, u32[]{:S(2)}) collective-permute-start(bf16[512,512]{1,0:T(8,128)(2,1)S(1)} %collective-permute-done.10), channel_id=1, source_target_pairs={{0,8},{1,9},{2,10},{3,11},{4,12},{5,13},{6,14},{7,15},{8,0},{9,1},... | collective-permute-start | bytes 1572872 | tf_op jit(solution)/shard_map/ppermute | solution.py:22
  46.6 28.8 %collective-permute-start.3 = (bf16[384,1024]{1,0:T(8,128)(2,1)}, bf16[384,1024]{1,0:T(8,128)(2,1)}, u32[]{:S(2)}, u32[]{:S(2)}) collective-permute-start(bf16[384,1024]{1,0:T(8,128)(2,1)} %shard_map.60), channel_id=1, source_target_pairs={{0,16},{1,17},{2,18},{3,19},{4,20},{5,21},{6,22},{7,23},{8,24},{9,... | collective-permute-start | bytes 2359304 | tf_op jit(solution)/shard_map/ppermute | solution.py:22
  60.8 14.6 %collective-permute-start.5 = (bf16[384,1024]{1,0:T(8,128)(2,1)}, bf16[384,1024]{1,0:T(8,128)(2,1)}, u32[]{:S(2)}, u32[]{:S(2)}) collective-permute-start(bf16[384,1024]{1,0:T(8,128)(2,1)} %collective-permute-done.4), channel_id=1, source_target_pairs={{0,16},{1,17},{2,18},{3,19},{4,20},{5,21},{6,22},{7,23},{8,24},{9,... | collective-permute-start | bytes 2359304 | tf_op jit(solution)/shard_map/ppermute | solution.py:22
  63.6 11.8 %collective-permute-start.11 = (bf16[512,512]{1,0:T(8,128)(2,1)S(1)}, bf16[512,512]{1,0:T(8,128)(2,1)S(1)}, u32[]{:S(2)}, u32[]{:S(2)}) collective-permute-start(bf16[512,512]{1,0:T(8,128)(2,1)S(1)} %collective-permute-done.10), channel_id=1, source_target_pairs={{0,16},{1,17},{2,18},{3,19},{4,20},{5,21},{6,22},{7,23},{8,24},{9,... | collective-permute-start | bytes 1572872 | tf_op jit(solution)/shard_map/ppermute | solution.py:22
  63.6 11.8 %collective-permute-start.13 = (bf16[512,512]{1,0:T(8,128)(2,1)S(1)}, bf16[512,512]{1,0:T(8,128)(2,1)}, u32[]{:S(2)}, u32[]{:S(2)}) collective-permute-start(bf16[512,512]{1,0:T(8,128)(2,1)S(1)} %collective-permute-done.12), channel_id=1, source_target_pairs={{0,16},{1,17},{2,18},{3,19},{4,20},{5,21},{6,22},{7,23},{8,24},{9,... | collective-permute-start | bytes 1572872 | tf_op jit(solution)/shard_map/ppermute | solution.py:22
  66.4 9.0 %collective-permute-start.15 = (bf16[512,512]{1,0:T(8,128)(2,1)S(1)}, bf16[512,512]{1,0:T(8,128)(2,1)}, u32[]{:S(2)}, u32[]{:S(2)}) collective-permute-start(bf16[512,512]{1,0:T(8,128)(2,1)S(1)} %collective-permute-done.14), channel_id=1, source_target_pairs={{0,16},{1,17},{2,18},{3,19},{4,20},{5,21},{6,22},{7,23},{8,24},{9,... | collective-permute-start | bytes 1572872 | tf_op jit(solution)/shard_map/ppermute | solution.py:22
  88.7 31.4 %collective-permute-start.18 = (bf16[512,2048]{1,0:T(8,128)(2,1)}, bf16[512,2048]{1,0:T(8,128)(2,1)}, u32[]{:S(2)}, u32[]{:S(2)}) collective-permute-start(bf16[512,2048]{1,0:T(8,128)(2,1)} %get-tuple-element.379), channel_id=1, source_target_pairs={{0,16},{1,17},{2,18},{3,19},{4,20},{5,21},{6,22},{7,23},{8,24},{9,... | collective-permute-start | bytes 6291464 | tf_op jit(solution)/shard_map/ppermute | solution.py:22
  99.9 20.2 %collective-permute-start.17 = (bf16[512,2048]{1,0:T(8,128)(2,1)}, bf16[512,2048]{1,0:T(8,128)(2,1)}, u32[]{:S(2)}, u32[]{:S(2)}) collective-permute-start(bf16[512,2048]{1,0:T(8,128)(2,1)} %get-tuple-element.378), channel_id=1, source_target_pairs={{0,16},{1,17},{2,18},{3,19},{4,20},{5,21},{6,22},{7,23},{8,24},{9,... | collective-permute-start | bytes 6291464 | tf_op jit(solution)/shard_map/ppermute | solution.py:22
  120.0 8.9 %collective-permute-start.16 = (bf16[512,1536]{1,0:T(8,128)(2,1)}, bf16[512,1536]{1,0:T(8,128)(2,1)S(1)}, u32[]{:S(2)}, u32[]{:S(2)}) collective-permute-start(bf16[512,1536]{1,0:T(8,128)(2,1)} %get-tuple-element.369), channel_id=1, source_target_pairs={{0,16},{1,17},{2,18},{3,19},{4,20},{5,21},{6,22},{7,23},{8,24},{9,... | collective-permute-start | bytes 4718600 | tf_op jit(solution)/shard_map/ppermute | solution.py:22
  120.1 8.8 %copy-start = (bf16[512,1536]{1,0:T(8,128)(2,1)S(1)}, bf16[512,1536]{1,0:T(8,128)(2,1)}, u32[]{:S(2)}) copy-start(bf16[512,1536]{1,0:T(8,128)(2,1)} %get-tuple-element.369) | copy-start | bytes 4718596

commit v5 on v4

--- a/solution.py
+++ b/solution.py
@@ -358,8 +358,11 @@
     )
     begun, own_low = lax.cond(
         is_first,
-        lambda: (product(info, here, slot, 0, most, jnp.float32), unset((count, most * TILE), low)),
-        lambda: (unset((everyone, most * TILE), jnp.float32), own_rows(0, most)),
+        lambda: (
+            product(info, here, slot, 0, most, low),
+            unset((count, most * TILE), low),
+        ),
+        lambda: (unset((everyone, most * TILE), low), own_rows(0, most)),
     )
     one = lax.cond(
         is_first,

time: 136 us -> 136 us (level)
  no operation moved by 1% of the time
where the time goes in v5:
time: 136 us; the launch traced here: 135 us
  Pallas kernels  71.4 us (53%)
  waiting for transfers between devices  45.1 us (33%)
  starting transfers between devices  15.9 us (12%)
  local copies, waits for them, and re-layouts  1.66 us (1%)
    pallas_call x5, Pallas kernels, product(): pl.pallas_call(kernel, grid_spec=pltpu.PrefetchScalarGridSpec(num_scalar_...  51.8 us
    ppermute x19, waiting for transfers between devices, sent(): return lax.ppermute(value, AXES, pairs)  45.1 us
    ppermute x19, starting transfers between devices, sent(): return lax.ppermute(value, AXES, pairs)  15.9 us
    pallas_call x2, Pallas kernels, outputs(): pl.pallas_call(kernel, grid_spec=pltpu.PrefetchScalarGridSpec(num_scalar_...  15.2 us
  transfers between devices with their start and end apart: 19, of which 7 were waited for; matrix products, arithmetic and copies ran while one was open for 1% of the time, Pallas kernels for 36%

profile of v5, /device:TPU:13, one launch (start us, length us, event | category | flops | bytes accessed | tf_op | source)
XLA Modules:
  0.0 135.1 jit_solution(15096289145414827450)
XLA Ops:
  0.6 2.3 %shard_map.59 = (bf16[128,512]{1,0:T(8,128)(2,1)}, bf16[128,1024]{1,0:T(8,128)(2,1)}) custom-call(s32[3]{0:T(128)S(1)} %compare_select_fusion.1.info_ref, bf16[128,1024]{1,0:T(8,128)(2,1)} %refs_0_.1, bf16[128,4096]{1,0:T(8,128)(2,1)} %refs_1_.1), custom_call_target="tpu_custom_call" | custom-call | tf_op jit(solution)/shard_map/pallas_call | solution.py:196
  6.7 3.1 %collective-permute-start.1 = (bf16[128,1024]{1,0:T(8,128)(2,1)}, bf16[128,1024]{1,0:T(8,128)(2,1)S(1)}, u32[]{:S(2)}, u32[]{:S(2)}) collective-permute-start(bf16[128,1024]{1,0:T(8,128)(2,1)} %get-tuple-element.331), channel_id=1, source_target_pairs={{0,2},{1,3},{2,0},{3,1},{4,6},{5,7},{6,4},{7,5},{8,10},{9,11},{10,... | collective-permute-start | bytes 786440 | tf_op jit(solution)/shard_map/ppermute | solution.py:22
  10.9 4.3 %collective-permute-done.7 = bf16[128,512]{1,0:T(8,128)(2,1)S(1)} collective-permute-done((bf16[128,512]{1,0:T(8,128)(2,1)}, bf16[128,512]{1,0:T(8,128)(2,1)S(1)}, u32[]{:S(2)}, u32[]{:S(2)}) %collective-permute-start.7) | collective-permute-done | bytes 131104 | tf_op jit(solution)/shard_map/ppermute | solution.py:22
  15.2 13.9 %collective-permute-done.8 = bf16[128,512]{1,0:T(8,128)(2,1)S(1)} collective-permute-done((bf16[128,512]{1,0:T(8,128)(2,1)}, bf16[128,512]{1,0:T(8,128)(2,1)S(1)}, u32[]{:S(2)}, u32[]{:S(2)}) %collective-permute-start.8) | collective-permute-done | bytes 131104 | tf_op jit(solution)/shard_map/ppermute | solution.py:22
  29.5 2.6 %collective-permute-done.refs_0_ = bf16[128,1024]{1,0:T(8,128)(2,1)S(1)} collective-permute-done((bf16[128,1024]{1,0:T(8,128)(2,1)}, bf16[128,1024]{1,0:T(8,128)(2,1)S(1)}, u32[]{:S(2)}, u32[]{:S(2)}) %collective-permute-start) | collective-permute-done | bytes 262176 | tf_op jit(solution)/shard_map/ppermute | solution.py:22
  32.1 5.6 %collective-permute-done.1.refs_1_ = bf16[128,1024]{1,0:T(8,128)(2,1)S(1)} collective-permute-done((bf16[128,1024]{1,0:T(8,128)(2,1)}, bf16[128,1024]{1,0:T(8,128)(2,1)S(1)}, u32[]{:S(2)}, u32[]{:S(2)}) %collective-permute-start.1) | collective-permute-done | bytes 262176 | tf_op jit(solution)/shard_map/ppermute | solution.py:22
  37.7 2.7 %collective-permute-done.2.refs_2_ = bf16[128,1024]{1,0:T(8,128)(2,1)S(1)} collective-permute-done((bf16[128,1024]{1,0:T(8,128)(2,1)}, bf16[128,1024]{1,0:T(8,128)(2,1)S(1)}, u32[]{:S(2)}, u32[]{:S(2)}) %collective-permute-start.2) | collective-permute-done | bytes 262176 | tf_op jit(solution)/shard_map/ppermute | solution.py:22
  47.2 13.6 %collective-permute-done.4 = bf16[384,1024]{1,0:T(8,128)(2,1)} collective-permute-done((bf16[384,1024]{1,0:T(8,128)(2,1)}, bf16[384,1024]{1,0:T(8,128)(2,1)}, u32[]{:S(2)}, u32[]{:S(2)}) %collective-permute-start.4) | collective-permute-done | bytes 786464 | tf_op jit(solution)/shard_map/ppermute | solution.py:22
  60.8 2.8 %collective-permute-start.5 = (bf16[384,1024]{1,0:T(8,128)(2,1)}, bf16[384,1024]{1,0:T(8,128)(2,1)}, u32[]{:S(2)}, u32[]{:S(2)}) collective-permute-start(bf16[384,1024]{1,0:T(8,128)(2,1)} %collective-permute-done.4), channel_id=1, source_target_pairs={{0,16},{1,17},{2,18},{3,19},{4,20},{5,21},{6,22},{7,23},{8,24},{9,... | collective-permute-start | bytes 2359304 | tf_op jit(solution)/shard_map/ppermute | solution.py:22
  64.1 2.3 %collective-permute-done.14 = bf16[512,512]{1,0:T(8,128)(2,1)S(1)} collective-permute-done((bf16[512,512]{1,0:T(8,128)(2,1)S(1)}, bf16[512,512]{1,0:T(8,128)(2,1)S(1)}, u32[]{:S(2)}, u32[]{:S(2)}) %collective-permute-start.14) | collective-permute-done | bytes 524320 | tf_op jit(solution)/shard_map/ppermute | solution.py:22
  66.4 8.9 %conditional.9 = (bf16[512,2048]{1,0:T(8,128)(2,1)}, bf16[128,2048]{1,0:T(8,128)(2,1)}) conditional(s32[]{:T(128)} %convert_element_type.2, (s32[3]{0:T(128)S(1)}, bf16[128,4096]{1,0:T(8,128)(2,1)}, bf16[4096,3584]{1,0:T(8,128)(2,1)}) %tuple.89, (s32[3]{0:T(128)S(1)}, bf16[512,512]{1,0:T(8,128)(2,1)S(1)}, bf16[512,512]{1,0:T(8,128)(2,1)S(1)}, ...), branch_computations={%region_4.5_spmd, %region_5.6_spmd} | conditional | flops 2147483648 | bytes 17301520 | solution.py:359
  66.4 8.9 %branch_0_fun.11 = bf16[128,2048]{1,0:T(8,128)(2,1)} custom-call(s32[3]{0:T(128)S(1)} %get-tuple-element.243.info_ref, bf16[128,4096]{1,0:T(8,128)(2,1)} %get-tuple-element.244.refs_0_, bf16[4096,3584]{1,0:T(8,128)(2,1)} %get-tuple-element.245.refs_1_), custom_call_target="tpu_custom_call" | custom-call | flops 2147483648 | bytes 17301504 | tf_op jit(solution)/shard_map/cond/branch_0_fun/pallas_call | solution.py:167
  75.4 13.3 %conditional.11 = (bf16[512,2048]{1,0:T(8,128)(2,1)}) conditional(s32[]{:T(128)} %convert_element_type.2, (s32[3]{0:T(128)S(1)}, bf16[384,1024]{1,0:T(8,128)(2,1)}, bf16[384,1024]{1,0:T(8,128)(2,1)}, bf16[384,1024]{1,0:T(8,128)(2,1)}, bf16[384,1024]{1,0:T(8,128)(2,1)}, /*index=5*/bf16[4096,3584]{1,0:T(8,128)(2,1)}, ...), branch_computations={%region_8.9_spmd, %region_9.10_spmd} | conditional | flops 8589934592 | bytes 18874376 | solution.py:373
  75.4 13.3 %branch_0_fun.13 = bf16[512,2048]{1,0:T(8,128)(2,1)} custom-call(s32[3]{0:T(128)S(1)} %get-tuple-element.269.info_ref, bf16[384,1024]{1,0:T(8,128)(2,1)} %get-tuple-element.270.refs_0_, bf16[384,1024]{1,0:T(8,128)(2,1)} %get-tuple-element.271.refs_1_, bf16[384,1024]{1,0:T(8,128)(2,1)} %get-tuple-element.272.refs_2_, ...), custom_call_target="tpu_custom_call" | custom-call | flops 6442450944 | bytes 18874368 | tf_op jit(solution)/shard_map/cond/branch_0_fun/pallas_call | solution.py:167
  88.6 11.3 %conditional.10 = (bf16[512,2048]{1,0:T(8,128)(2,1)}) conditional(s32[]{:T(128)} %convert_element_type.2, (s32[3]{0:T(128)S(1)}, bf16[512,512]{1,0:T(8,128)(2,1)S(1)}, bf16[512,512]{1,0:T(8,128)(2,1)S(1)}, bf16[512,512]{1,0:T(8,128)(2,1)S(1)}, bf16[512,512]{1,0:T(8,128)(2,1)S(1)}, /*index=5*/bf16[512,512]{1,0:T(8,128)(2,1)S(1)}, ...), branch_computations={%region_6.7_spmd, %region_7.8_spmd} | conditional | flops 6442450944 | bytes 14680072 | solution.py:367
  88.7 11.2 %branch_0_fun.12 = bf16[512,2048]{1,0:T(8,128)(2,1)} custom-call(s32[3]{0:T(128)S(1)} %get-tuple-element.250.info_ref, bf16[512,512]{1,0:T(8,128)(2,1)S(1)} %get-tuple-element.251.refs_0_, bf16[512,512]{1,0:T(8,128)(2,1)S(1)} %get-tuple-element.252.refs_1_, bf16[512,512]{1,0:T(8,128)(2,1)S(1)} %get-tuple-element.253.refs_2_, ...), custom_call_target="tpu_custom_call" | custom-call | flops 6442450944 | bytes 14680064 | tf_op jit(solution)/shard_map/cond/branch_0_fun/pallas_call | solution.py:167
  101.2 6.9 %conditional.7 = (bf16[128,1536]{1,0:T(8,128)(2,1)S(1)}) conditional(s32[]{:T(128)} %convert_element_type.2, (s32[3]{0:T(128)S(1)}, bf16[128,4096]{1,0:T(8,128)(2,1)}, bf16[4096,3584]{1,0:T(8,128)(2,1)}) %tuple.93, () %tuple.57), branch_computations={%region_0.1_spmd, %region_1.2_spmd} | conditional | flops 1610612736 | bytes 12976136 | solution.py:354
  101.2 6.9 %branch_0_fun.8 = bf16[128,1536]{1,0:T(8,128)(2,1)S(1)} custom-call(s32[3]{0:T(128)S(1)} %get-tuple-element.214.info_ref, bf16[128,4096]{1,0:T(8,128)(2,1)} %get-tuple-element.215.refs_0_, bf16[4096,3584]{1,0:T(8,128)(2,1)} %get-tuple-element.216.refs_1_), custom_call_target="tpu_custom_call" | custom-call | flops 1610612736 | bytes 12976128 | tf_op jit(solution)/shard_map/cond/branch_0_fun/pallas_call | solution.py:167
  108.1 11.5 %conditional.8 = ((bf16[512,1536]{1,0:T(8,128)(2,1)}, bf16[512,1024]{1,0:T(8,128)(2,1)}, bf16[512,512]{1,0:T(8,128)(2,1)})) conditional(s32[]{:T(128)} %convert_element_type.2, (s32[3]{0:T(128)S(1)}, bf16[384,1024]{1,0:T(8,128)(2,1)}, bf16[384,1024]{1,0:T(8,128)(2,1)}, bf16[384,1024]{1,0:T(8,128)(2,1)}, bf16[384,1024]{1,0:T(8,128)(2,1)}, ...), branch_computations={%region_2.3_spmd, %region_3.4_spmd} | conditional | flops 6442450944 | bytes 14155784 | solution.py:408
  108.1 11.4 %branch_0_fun.9 = (bf16[512,1536]{1,0:T(8,128)(2,1)}, bf16[512,1024]{1,0:T(8,128)(2,1)}, bf16[512,512]{1,0:T(8,128)(2,1)}) custom-call(s32[3]{0:T(128)S(1)} %get-tuple-element.217.info_ref, bf16[384,1024]{1,0:T(8,128)(2,1)} %get-tuple-element.218.refs_0_.refs_10_, bf16[384,1024]{1,0:T(8,128)(2,1)} %get-tuple-element.219.refs_1_.refs_11_, ...), custom_call_target="tpu_custom_call" | custom-call | flops 4831838208 | bytes 14155776 | tf_op jit(solution)/shard_map/cond/branch_0_fun/pallas_call | solution.py:167
  119.7 8.8 %conditional.12 = ((bf16[1024,3584]{1,0:T(8,128)(2,1)}, bf16[512,3584]{1,0:T(8,128)(2,1)})) conditional(s32[]{:T(128)} %convert_element_type.2, (s32[3]{0:T(128)S(1)}, bf16[512,2048]{1,0:T(8,128)(2,1)}, bf16[512,2048]{1,0:T(8,128)(2,1)}, bf16[512,2048]{1,0:T(8,128)(2,1)}, bf16[512,1024]{1,0:T(8,128)(2,1)}, ...), branch_computations={%region_10.11_spmd, %region_11.12_spmd} | conditional | flops 3221225472 | bytes 12582920 | solution.py:423
  119.9 8.6 %branch_0_fun.14 = (bf16[1024,3584]{1,0:T(8,128)(2,1)}, bf16[512,3584]{1,0:T(8,128)(2,1)}) custom-call(s32[3]{0:T(128)S(1)} %get-tuple-element.286.info_ref, bf16[512,2048]{1,0:T(8,128)(2,1)} %get-tuple-element.287.gate_ref, bf16[512,2048]{1,0:T(8,128)(2,1)} %get-tuple-element.288.hidden_ref, bf16[512,2048]{1,0:T(8,128)(2,1)} %get-tuple-element.289.up_pre_ref, ...), custom_call_target="tpu_custom_call" | custom-call | flops 3221225472 | bytes 12582912 | tf_op jit(solution)/shard_map/cond/branch_0_fun/pallas_call | solution.py:257
  128.5 6.6 %conditional.13 = (bf16[512,3584]{1,0:T(8,128)(2,1)}, bf16[1,1024,3584]{2,1,0:T(8,128)(2,1)}) conditional(s32[]{:T(128)} %convert_element_type.2, (s32[3]{0:T(128)S(1)}, bf16[512,1536]{1,0:T(8,128)(2,1)S(1)}, bf16[512,1536]{1,0:T(8,128)(2,1)S(1)}, bf16[512,2048]{1,0:T(8,128)(2,1)}, bf16[512,1024]{1,0:T(8,128)(2,1)}, ...), branch_computations={%region_12.13_spmd, %region_13.14_spmd} | conditional | flops 2415919104 | bytes 9437200 | solution.py:432
  128.5 6.6 %branch_0_fun.15 = (bf16[1024,3584]{1,0:T(8,128)(2,1)}, bf16[512,3584]{1,0:T(8,128)(2,1)}) custom-call(s32[3]{0:T(128)S(1)} %get-tuple-element.298.info_ref, bf16[512,1536]{1,0:T(8,128)(2,1)S(1)} %get-tuple-element.299.gate_ref, bf16[512,1536]{1,0:T(8,128)(2,1)S(1)} %get-tuple-element.300.hidden_ref, ...), custom_call_target="tpu_custom_call", output_to_operand_aliasing={{0}: (6, {}), {1}: (7, {})} | custom-call | flops 2415919104 | bytes 9437184 | tf_op jit(solution)/shard_map/cond/branch_0_fun/pallas_call | solution.py:257
  (44 shorter events, 13.8 us)
Async XLA Ops:
  3.0 7.8 %collective-permute-start.6 = (bf16[128,512]{1,0:T(8,128)(2,1)}, bf16[128,512]{1,0:T(8,128)(2,1)S(1)}, u32[]{:S(2)}, u32[]{:S(2)}) collective-permute-start(bf16[128,512]{1,0:T(8,128)(2,1)} %get-tuple-element.332), channel_id=1, source_target_pairs={{0,1},{1,2},{2,3},{3,0},{4,5},{5,6},{6,7},{7,4},{8,9},{9,10},{10,1... | collective-permute-start | bytes 393224 | tf_op jit(solution)/shard_map/ppermute | solution.py:22
  4.3 11.0 %collective-permute-start.7 = (bf16[128,512]{1,0:T(8,128)(2,1)}, bf16[128,512]{1,0:T(8,128)(2,1)S(1)}, u32[]{:S(2)}, u32[]{:S(2)}) collective-permute-start(bf16[128,512]{1,0:T(8,128)(2,1)} %get-tuple-element.332), channel_id=1, source_target_pairs={{0,2},{1,3},{2,0},{3,1},{4,6},{5,7},{6,4},{7,5},{8,10},{9,11},{10,... | collective-permute-start | bytes 393224 | tf_op jit(solution)/shard_map/ppermute | solution.py:22
  5.3 23.9 %collective-permute-start.8 = (bf16[128,512]{1,0:T(8,128)(2,1)}, bf16[128,512]{1,0:T(8,128)(2,1)S(1)}, u32[]{:S(2)}, u32[]{:S(2)}) collective-permute-start(bf16[128,512]{1,0:T(8,128)(2,1)} %get-tuple-element.332), channel_id=1, source_target_pairs={{0,3},{1,0},{2,1},{3,2},{4,7},{5,4},{6,5},{7,6},{8,11},{9,8},{10,9... | collective-permute-start | bytes 393224 | tf_op jit(solution)/shard_map/ppermute | solution.py:22
  6.7 25.3 %collective-permute-start = (bf16[128,1024]{1,0:T(8,128)(2,1)}, bf16[128,1024]{1,0:T(8,128)(2,1)S(1)}, u32[]{:S(2)}, u32[]{:S(2)}) collective-permute-start(bf16[128,1024]{1,0:T(8,128)(2,1)} %get-tuple-element.331), channel_id=1, source_target_pairs={{0,1},{1,2},{2,3},{3,0},{4,5},{5,6},{6,7},{7,4},{8,9},{9,10},{10,1... | collective-permute-start | bytes 786440 | tf_op jit(solution)/shard_map/ppermute | solution.py:22
  6.7 31.0 %collective-permute-start.1 = (bf16[128,1024]{1,0:T(8,128)(2,1)}, bf16[128,1024]{1,0:T(8,128)(2,1)S(1)}, u32[]{:S(2)}, u32[]{:S(2)}) collective-permute-start(bf16[128,1024]{1,0:T(8,128)(2,1)} %get-tuple-element.331), channel_id=1, source_target_pairs={{0,2},{1,3},{2,0},{3,1},{4,6},{5,7},{6,4},{7,5},{8,10},{9,11},{10,... | collective-permute-start | bytes 786440 | tf_op jit(solution)/shard_map/ppermute | solution.py:22
  10.8 29.6 %collective-permute-start.2 = (bf16[128,1024]{1,0:T(8,128)(2,1)}, bf16[128,1024]{1,0:T(8,128)(2,1)S(1)}, u32[]{:S(2)}, u32[]{:S(2)}) collective-permute-start(bf16[128,1024]{1,0:T(8,128)(2,1)} %get-tuple-element.331), channel_id=1, source_target_pairs={{0,3},{1,0},{2,1},{3,2},{4,7},{5,4},{6,5},{7,6},{8,11},{9,8},{10,9... | collective-permute-start | bytes 786440 | tf_op jit(solution)/shard_map/ppermute | solution.py:22
  29.2 16.2 %collective-permute-start.10 = (bf16[512,512]{1,0:T(8,128)(2,1)S(1)}, bf16[512,512]{1,0:T(8,128)(2,1)S(1)}, u32[]{:S(2)}, u32[]{:S(2)}) collective-permute-start(bf16[512,512]{1,0:T(8,128)(2,1)S(1)} %constant_dynamic-update-slice_fusion), channel_id=1, source_target_pairs={{0,4},{1,5},{2,6},{3,7},{4,0},{5,1},{6,2},{7,3},{8,12},{9,13},{10,... | collective-permute-start | bytes 1572872 | tf_op jit(solution)/shard_map/ppermute | solution.py:22
  32.1 8.3 %copy-start.1 = (bf16[128,1024]{1,0:T(8,128)(2,1)}, bf16[128,1024]{1,0:T(8,128)(2,1)S(1)}, u32[]{:S(2)}) copy-start(bf16[128,1024]{1,0:T(8,128)(2,1)S(1)} %collective-permute-done.refs_0_) | copy-start | bytes 786436
  37.7 2.7 %copy-start.2 = (bf16[128,1024]{1,0:T(8,128)(2,1)}, bf16[128,1024]{1,0:T(8,128)(2,1)S(1)}, u32[]{:S(2)}) copy-start(bf16[128,1024]{1,0:T(8,128)(2,1)S(1)} %collective-permute-done.1.refs_1_) | copy-start | bytes 786436
  40.4 0.7 copy-start.3
  43.1 17.6 %collective-permute-start.4 = (bf16[384,1024]{1,0:T(8,128)(2,1)}, bf16[384,1024]{1,0:T(8,128)(2,1)}, u32[]{:S(2)}, u32[]{:S(2)}) collective-permute-start(bf16[384,1024]{1,0:T(8,128)(2,1)} %shard_map.60), channel_id=1, source_target_pairs={{0,4},{1,5},{2,6},{3,7},{4,0},{5,1},{6,2},{7,3},{8,12},{9,13},{10,... | collective-permute-start | bytes 2359304 | tf_op jit(solution)/shard_map/ppermute | solution.py:22
  43.4 20.2 %collective-permute-start.9 = (bf16[512,512]{1,0:T(8,128)(2,1)S(1)}, bf16[512,512]{1,0:T(8,128)(2,1)S(1)}, u32[]{:S(2)}, u32[]{:S(2)}) collective-permute-start(bf16[512,512]{1,0:T(8,128)(2,1)S(1)} %constant_dynamic-update-slice_fusion), channel_id=1, source_target_pairs={{0,16},{1,17},{2,18},{3,19},{4,20},{5,21},{6,22},{7,23},{8,24},{9,... | collective-permute-start | bytes 1572872 | tf_op jit(solution)/shard_map/ppermute | solution.py:22
  45.1 18.4 %collective-permute-start.12 = (bf16[512,512]{1,0:T(8,128)(2,1)S(1)}, bf16[512,512]{1,0:T(8,128)(2,1)S(1)}, u32[]{:S(2)}, u32[]{:S(2)}) collective-permute-start(bf16[512,512]{1,0:T(8,128)(2,1)S(1)} %constant_dynamic-update-slice_fusion), channel_id=1, source_target_pairs={{0,8},{1,9},{2,10},{3,11},{4,12},{5,13},{6,14},{7,15},{8,0},{9,1},... | collective-permute-start | bytes 1572872 | tf_op jit(solution)/shard_map/ppermute | solution.py:22
  45.4 21.0 %collective-permute-start.14 = (bf16[512,512]{1,0:T(8,128)(2,1)S(1)}, bf16[512,512]{1,0:T(8,128)(2,1)S(1)}, u32[]{:S(2)}, u32[]{:S(2)}) collective-permute-start(bf16[512,512]{1,0:T(8,128)(2,1)S(1)} %collective-permute-done.10), channel_id=1, source_target_pairs={{0,8},{1,9},{2,10},{3,11},{4,12},{5,13},{6,14},{7,15},{8,0},{9,1},... | collective-permute-start | bytes 1572872 | tf_op jit(solution)/shard_map/ppermute | solution.py:22
  46.6 28.8 %collective-permute-start.3 = (bf16[384,1024]{1,0:T(8,128)(2,1)}, bf16[384,1024]{1,0:T(8,128)(2,1)}, u32[]{:S(2)}, u32[]{:S(2)}) collective-permute-start(bf16[384,1024]{1,0:T(8,128)(2,1)} %shard_map.60), channel_id=1, source_target_pairs={{0,16},{1,17},{2,18},{3,19},{4,20},{5,21},{6,22},{7,23},{8,24},{9,... | collective-permute-start | bytes 2359304 | tf_op jit(solution)/shard_map/ppermute | solution.py:22
  60.8 14.6 %collective-permute-start.5 = (bf16[384,1024]{1,0:T(8,128)(2,1)}, bf16[384,1024]{1,0:T(8,128)(2,1)}, u32[]{:S(2)}, u32[]{:S(2)}) collective-permute-start(bf16[384,1024]{1,0:T(8,128)(2,1)} %collective-permute-done.4), channel_id=1, source_target_pairs={{0,16},{1,17},{2,18},{3,19},{4,20},{5,21},{6,22},{7,23},{8,24},{9,... | collective-permute-start | bytes 2359304 | tf_op jit(solution)/shard_map/ppermute | solution.py:22
  63.5 11.8 %collective-permute-start.11 = (bf16[512,512]{1,0:T(8,128)(2,1)S(1)}, bf16[512,512]{1,0:T(8,128)(2,1)S(1)}, u32[]{:S(2)}, u32[]{:S(2)}) collective-permute-start(bf16[512,512]{1,0:T(8,128)(2,1)S(1)} %collective-permute-done.10), channel_id=1, source_target_pairs={{0,16},{1,17},{2,18},{3,19},{4,20},{5,21},{6,22},{7,23},{8,24},{9,... | collective-permute-start | bytes 1572872 | tf_op jit(solution)/shard_map/ppermute | solution.py:22
  63.5 11.8 %collective-permute-start.13 = (bf16[512,512]{1,0:T(8,128)(2,1)S(1)}, bf16[512,512]{1,0:T(8,128)(2,1)}, u32[]{:S(2)}, u32[]{:S(2)}) collective-permute-start(bf16[512,512]{1,0:T(8,128)(2,1)S(1)} %collective-permute-done.12), channel_id=1, source_target_pairs={{0,16},{1,17},{2,18},{3,19},{4,20},{5,21},{6,22},{7,23},{8,24},{9,... | collective-permute-start | bytes 1572872 | tf_op jit(solution)/shard_map/ppermute | solution.py:22
  66.4 9.0 %collective-permute-start.15 = (bf16[512,512]{1,0:T(8,128)(2,1)S(1)}, bf16[512,512]{1,0:T(8,128)(2,1)}, u32[]{:S(2)}, u32[]{:S(2)}) collective-permute-start(bf16[512,512]{1,0:T(8,128)(2,1)S(1)} %collective-permute-done.14), channel_id=1, source_target_pairs={{0,16},{1,17},{2,18},{3,19},{4,20},{5,21},{6,22},{7,23},{8,24},{9,... | collective-permute-start | bytes 1572872 | tf_op jit(solution)/shard_map/ppermute | solution.py:22
  88.6 31.0 %collective-permute-start.18 = (bf16[512,2048]{1,0:T(8,128)(2,1)}, bf16[512,2048]{1,0:T(8,128)(2,1)}, u32[]{:S(2)}, u32[]{:S(2)}) collective-permute-start(bf16[512,2048]{1,0:T(8,128)(2,1)} %get-tuple-element.379), channel_id=1, source_target_pairs={{0,16},{1,17},{2,18},{3,19},{4,20},{5,21},{6,22},{7,23},{8,24},{9,... | collective-permute-start | bytes 6291464 | tf_op jit(solution)/shard_map/ppermute | solution.py:22
  99.9 19.8 %collective-permute-start.17 = (bf16[512,2048]{1,0:T(8,128)(2,1)}, bf16[512,2048]{1,0:T(8,128)(2,1)}, u32[]{:S(2)}, u32[]{:S(2)}) collective-permute-start(bf16[512,2048]{1,0:T(8,128)(2,1)} %get-tuple-element.378), channel_id=1, source_target_pairs={{0,16},{1,17},{2,18},{3,19},{4,20},{5,21},{6,22},{7,23},{8,24},{9,... | collective-permute-start | bytes 6291464 | tf_op jit(solution)/shard_map/ppermute | solution.py:22
  119.6 8.9 %collective-permute-start.16 = (bf16[512,1536]{1,0:T(8,128)(2,1)}, bf16[512,1536]{1,0:T(8,128)(2,1)S(1)}, u32[]{:S(2)}, u32[]{:S(2)}) collective-permute-start(bf16[512,1536]{1,0:T(8,128)(2,1)} %get-tuple-element.369), channel_id=1, source_target_pairs={{0,16},{1,17},{2,18},{3,19},{4,20},{5,21},{6,22},{7,23},{8,24},{9,... | collective-permute-start | bytes 4718600 | tf_op jit(solution)/shard_map/ppermute | solution.py:22
  119.7 8.8 %copy-start = (bf16[512,1536]{1,0:T(8,128)(2,1)S(1)}, bf16[512,1536]{1,0:T(8,128)(2,1)}, u32[]{:S(2)}) copy-start(bf16[512,1536]{1,0:T(8,128)(2,1)} %get-tuple-element.369) | copy-start | bytes 4718596
